TPU v7x, 512 devices: a whole 4x4x16 slice. The times are simulated.
512 devices in a mesh: section: 4 (over x), row: 8 (over y, core), col: 16 (over z).
Axes of the slice: x: 4, y: 4, z: 16, core: 2. Of those that a mesh axis runs over, the one named last changes fastest.
Arguments:
- latent: bfloat16 [2, 128, 256, 128], P(None, 'row', 'col'), may hold values from -6 to 6
- hidden_old: bfloat16 [4, 2, 128, 256, 128], P('section', None, 'row', 'col'), may hold values from -1 to 1
- cell_old: float32 [4, 2, 128, 256, 128], P('section', None, 'row', 'col'), may hold values from -6 to 6
- weights: bfloat16 [4, 9, 256, 512], P('section'), may hold values from -0.125 to 0.125
- bias: float32 [4, 512], P('section'), may hold values from -3 to 3
Outputs:
- hidden_new: bfloat16 [4, 2, 128, 256, 128], P('section', None, 'row', 'col')
- cell_new: float32 [4, 2, 128, 256, 128], P('section', None, 'row', 'col')
All inputs are finite; a program needn't handle non-finite values.
Results may differ from a plain program's by a relative error of at most 0.0016.
Values may be sent and summed in bfloat16 or wider, within the bound.
No kernel may reach another device: no remote copies, remote signals or barrier semaphores. Data moves between devices by JAX's collectives and lax.ppermute only.
A program may use at most 64 MiB of HBM per device.

v0:
```python
import jax
import jax.numpy as jnp
from jax import lax
from jax.sharding import PartitionSpec as P


def shifted(x, axis, by):
    length = lax.axis_size(axis)
    pairs = [(i, i + by) for i in range(length) if 0 <= i + by < length]
    return lax.ppermute(x, axis, pairs)


def padded_2(cells, sides, width):
    for axis, dim in sides:
        count = lax.axis_size(axis)
        ends = count - 1
        head = lax.slice_in_dim(cells, 0, width, axis=dim)
        tail = lax.slice_in_dim(cells, cells.shape[dim] - width, cells.shape[dim], axis=dim)
        cells = jnp.concatenate(
            [
                lax.ppermute(tail, axis, [(i, (i + 1) % count) for i in range(ends)]),
                cells,
                lax.ppermute(head, axis, [((i + 1) % count, i) for i in range(ends)]),
            ],
            axis=dim,
        )
    return cells


def gate_update(padded, cell_prev, kernel, offset):
    batch = padded.shape[0]
    height = padded.shape[1] - 2
    width = padded.shape[2] - 2
    chans = padded.shape[3]
    gates = jnp.zeros((batch * height * width, kernel.shape[-1]), jnp.float32)
    for tap in range(9):
        dy = tap // 3
        dx = tap % 3
        window = padded[:, dy : dy + height, dx : dx + width, :].reshape(-1, chans)
        gates = gates + jnp.dot(window, kernel[tap], preferred_element_type=jnp.float32)
    gates = (gates + offset[None, :]).reshape(batch, height, width, -1)
    quarter = gates.shape[-1] // 4
    gate_i = jax.nn.sigmoid(gates[..., :quarter])
    gate_f = jax.nn.sigmoid(gates[..., quarter : 2 * quarter])
    gate_g = jnp.tanh(gates[..., 2 * quarter : 3 * quarter])
    gate_o = jax.nn.sigmoid(gates[..., 3 * quarter :])
    cell = gate_f * cell_prev + gate_i * gate_g
    hidden = (gate_o * jnp.tanh(cell)).astype(jnp.bfloat16)
    return (hidden, cell)


def on_device(latent, hidden_old, cell_old, weights, bias):
    kernel = weights[0]
    offset = bias[0]
    hidden_prev = hidden_old[0]
    cell_prev = cell_old[0]
    section_idx = lax.axis_index("section")
    sections = lax.axis_size("section")
    count = 1
    hidden_acc = jnp.zeros_like(hidden_prev)
    cell_acc = jnp.zeros_like(cell_prev)
    outgoing = None
    for tick in range(count + sections - 1):
        micro = tick - section_idx
        if tick == 0:
            layer_in = latent
        else:
            received = shifted(outgoing, "section", 1)
            layer_in = jnp.where(section_idx == 0, latent, received)
        stacked = jnp.concatenate([layer_in, hidden_prev], axis=-1)
        padded = padded_2(stacked, (("row", 1), ("col", 2)), 1)
        hidden_step, cell_step = gate_update(padded, cell_prev, kernel, offset)
        active = (micro >= 0) & (micro < count)
        hidden_acc = jnp.where(active, hidden_step, hidden_acc)
        cell_acc = jnp.where(active, cell_step, cell_acc)
        outgoing = hidden_step
    return (hidden_acc[None], cell_acc[None])


def solution(mesh):
    in_specs = (
        P(None, "row", "col", None),
        P("section", None, "row", "col", None),
        P("section", None, "row", "col", None),
        P("section", None, None, None),
        P("section", None),
    )
    out_specs = (P("section", None, "row", "col", None), P("section", None, "row", "col", None))
    return jax.shard_map(
        on_device, mesh=mesh, in_specs=in_specs, out_specs=out_specs, check_vma=False
    )
```

profile of v0, /device:TPU:103, one launch (start us, length us, event | category | flops | bytes accessed | tf_op | source)
XLA Modules:
  0.0 114.3 jit_solution(7798067351845072292)
XLA Ops:
  0.7 0.8 fusion.191
  1.5 3.8 %collective-permute-start = (bf16[2,1,16,256]{3,2,1,0:T(8,128)(2,1)S(1)}, bf16[2,1,16,256]{3,2,1,0:T(8,128)(2,1)S(1)}, u32[]{:S(2)}, u32[]{:S(2)}) collective-permute-start(bf16[2,1,16,256]{3,2,1,0:T(8,128)(2,1)S(1)} %get-tuple-element.10), channel_id=1, source_target_pairs={{0,16},{16,32},{32,48},{48,64},{64,80},{80,96},{96,112},{1,17},{17... | collective-permute-start | bytes 49160 | tf_op jit(solution)/shard_map/ppermute | solution.py:21
  5.2 1.9 %collective-permute-start.1 = (bf16[2,1,16,256]{3,2,1,0:T(8,128)(2,1)S(1)}, bf16[2,1,16,256]{3,2,1,0:T(8,128)(2,1)S(1)}, u32[]{:S(2)}, u32[]{:S(2)}) collective-permute-start(bf16[2,1,16,256]{3,2,1,0:T(8,128)(2,1)S(1)} %get-tuple-element.68), channel_id=1, source_target_pairs={{16,0},{32,16},{48,32},{64,48},{80,64},{96,80},{112,96},{17,1},{33... | collective-permute-start | bytes 49160 | tf_op jit(solution)/shard_map/ppermute | solution.py:23
  7.2 3.1 %collective-permute-done.1 = bf16[2,1,16,256]{3,2,1,0:T(8,128)(2,1)S(1)} collective-permute-done((bf16[2,1,16,256]{3,2,1,0:T(8,128)(2,1)S(1)}, bf16[2,1,16,256]{3,2,1,0:T(8,128)(2,1)S(1)}, u32[]{:S(2)}, u32[]{:S(2)}) %collective-permute-start.1) | collective-permute-done | bytes 16416 | tf_op jit(solution)/shard_map/ppermute | solution.py:23
  10.3 1.0 fusion.33
  11.4 4.8 %collective-permute-start.2 = (bf16[2,18,1,256]{3,2,1,0:T(2,128)(2,1)S(1)}, bf16[2,18,1,256]{3,2,1,0:T(2,128)(2,1)S(1)}, u32[]{:S(2)}, u32[]{:S(2)}) collective-permute-start(bf16[2,18,1,256]{3,2,1,0:T(2,128)(2,1)S(1)} %get-tuple-element.52), channel_id=1, source_target_pairs={{0,1},{1,2},{2,3},{3,4},{4,5},{5,6},{6,7},{7,8},{8,9},{9,10},{10,1... | collective-permute-start | bytes 55304 | tf_op jit(solution)/shard_map/ppermute | solution.py:21
  16.1 1.9 %collective-permute-start.3 = (bf16[2,18,1,256]{3,2,1,0:T(2,128)(2,1)S(1)}, bf16[2,18,1,256]{3,2,1,0:T(2,128)(2,1)S(1)}, u32[]{:S(2)}, u32[]{:S(2)}) collective-permute-start(bf16[2,18,1,256]{3,2,1,0:T(2,128)(2,1)S(1)} %get-tuple-element.53), channel_id=1, source_target_pairs={{1,0},{2,1},{3,2},{4,3},{5,4},{6,5},{7,6},{8,7},{9,8},{10,9},{11,1... | collective-permute-start | bytes 55304 | tf_op jit(solution)/shard_map/ppermute | solution.py:23
  18.1 1.2 %fusion.44 = (bf16[2,16,16,256]{3,2,1,0:T(8,128)(2,1)S(1)}, bf16[2,16,16,256]{3,2,1,0:T(8,128)(2,1)S(1)}) fusion(bf16[2,16,16,128]{3,2,1,0:T(8,128)(2,1)} %bitcast.171, bf16[2,1,16,256]{3,2,1,0:T(8,128)(2,1)S(1)} %collective-permute-done.1, bf16[2,16,16,128]{3,2,1,0:T(8,128)(2,1)} %param.5, bf16[2,1,16,256]{3,2,1,0:T(8,128)(2,1)S(1)} %collective-permute-done), kind=kLoop, calls=%fused_computation.96 | loop fusion | flops 1572864 | bytes 819200 | tf_op jit(solution)/shard_map/concatenate | solution.py:19
  19.2 1.2 %fusion.142 = f32[512,512]{1,0:T(8,128)S(1)} fusion(bf16[512,256]{1,0:T(8,128)(2,1)S(1)} %bitcast.220, bf16[1,9,256,512]{3,2,1,0:T(8,128)(2,1)} %param.8), kind=kOutput, calls=%fused_computation.210 | convolution fusion | flops 134217728 | bytes 1572864 | tf_op jit(solution)/shard_map/dot_general | solution.py:40
  20.5 1.6 %collective-permute-done.3 = bf16[2,18,1,256]{3,2,1,0:T(2,128)(2,1)S(1)} collective-permute-done((bf16[2,18,1,256]{3,2,1,0:T(2,128)(2,1)S(1)}, bf16[2,18,1,256]{3,2,1,0:T(2,128)(2,1)S(1)}, u32[]{:S(2)}, u32[]{:S(2)}) %collective-permute-start.3) | collective-permute-done | bytes 18464 | tf_op jit(solution)/shard_map/ppermute | solution.py:23
  24.0 0.3 convolution_add_fusion.23
  24.9 0.6 copy-done.3
  25.8 1.3 %collective-permute-start.4 = (bf16[2,16,16,128]{3,2,1,0:T(8,128)(2,1)S(1)}, bf16[2,16,16,128]{3,2,1,0:T(8,128)(2,1)S(1)}, u32[]{:S(2)}, u32[]{:S(2)}) collective-permute-start(bf16[2,16,16,128]{3,2,1,0:T(8,128)(2,1)S(1)} %get-tuple-element.8), channel_id=1, source_target_pairs={{0,128},{128,256},{256,384},{1,129},{129,257},{257,385},{2,130},{1... | collective-permute-start | bytes 393224 | tf_op jit(solution)/shard_map/ppermute | solution.py:10
  27.1 5.9 %collective-permute-done.4 = bf16[2,16,16,128]{3,2,1,0:T(8,128)(2,1)S(1)} collective-permute-done((bf16[2,16,16,128]{3,2,1,0:T(8,128)(2,1)S(1)}, bf16[2,16,16,128]{3,2,1,0:T(8,128)(2,1)S(1)}, u32[]{:S(2)}, u32[]{:S(2)}) %collective-permute-start.4) | collective-permute-done | bytes 131104 | tf_op jit(solution)/shard_map/ppermute | solution.py:10
  33.1 3.7 %collective-permute-start.5 = (bf16[2,1,16,256]{3,2,1,0:T(8,128)(2,1)S(1)}, bf16[2,1,16,256]{3,2,1,0:T(8,128)(2,1)S(1)}, u32[]{:S(2)}, u32[]{:S(2)}) collective-permute-start(bf16[2,1,16,256]{3,2,1,0:T(8,128)(2,1)S(1)} %get-tuple-element.66), channel_id=1, source_target_pairs={{0,16},{16,32},{32,48},{48,64},{64,80},{80,96},{96,112},{1,17},{17... | collective-permute-start | bytes 49160 | tf_op jit(solution)/shard_map/ppermute | solution.py:21
  36.8 1.9 %collective-permute-start.6 = (bf16[2,1,16,256]{3,2,1,0:T(8,128)(2,1)S(1)}, bf16[2,1,16,256]{3,2,1,0:T(8,128)(2,1)S(1)}, u32[]{:S(2)}, u32[]{:S(2)}) collective-permute-start(bf16[2,1,16,256]{3,2,1,0:T(8,128)(2,1)S(1)} %get-tuple-element.67), channel_id=1, source_target_pairs={{16,0},{32,16},{48,32},{64,48},{80,64},{96,80},{112,96},{17,1},{33... | collective-permute-start | bytes 49160 | tf_op jit(solution)/shard_map/ppermute | solution.py:23
  38.7 3.1 %collective-permute-done.6 = bf16[2,1,16,256]{3,2,1,0:T(8,128)(2,1)S(1)} collective-permute-done((bf16[2,1,16,256]{3,2,1,0:T(8,128)(2,1)S(1)}, bf16[2,1,16,256]{3,2,1,0:T(8,128)(2,1)S(1)}, u32[]{:S(2)}, u32[]{:S(2)}) %collective-permute-start.6) | collective-permute-done | bytes 16416 | tf_op jit(solution)/shard_map/ppermute | solution.py:23
  42.0 4.0 %collective-permute-start.7 = (bf16[2,18,1,256]{3,2,1,0:T(2,128)(2,1)S(1)}, bf16[2,18,1,256]{3,2,1,0:T(2,128)(2,1)S(1)}, u32[]{:S(2)}, u32[]{:S(2)}) collective-permute-start(bf16[2,18,1,256]{3,2,1,0:T(2,128)(2,1)S(1)} %get-tuple-element.48), channel_id=1, source_target_pairs={{0,1},{1,2},{2,3},{3,4},{4,5},{5,6},{6,7},{7,8},{8,9},{9,10},{10,1... | collective-permute-start | bytes 55304 | tf_op jit(solution)/shard_map/ppermute | solution.py:21
  45.9 1.9 %collective-permute-start.8 = (bf16[2,18,1,256]{3,2,1,0:T(2,128)(2,1)S(1)}, bf16[2,18,1,256]{3,2,1,0:T(2,128)(2,1)S(1)}, u32[]{:S(2)}, u32[]{:S(2)}) collective-permute-start(bf16[2,18,1,256]{3,2,1,0:T(2,128)(2,1)S(1)} %get-tuple-element.49), channel_id=1, source_target_pairs={{1,0},{2,1},{3,2},{4,3},{5,4},{6,5},{7,6},{8,7},{9,8},{10,9},{11,1... | collective-permute-start | bytes 55304 | tf_op jit(solution)/shard_map/ppermute | solution.py:23
  47.9 0.3 fusion.140
  48.2 3.6 %collective-permute-done.8 = bf16[2,18,1,256]{3,2,1,0:T(2,128)(2,1)S(1)} collective-permute-done((bf16[2,18,1,256]{3,2,1,0:T(2,128)(2,1)S(1)}, bf16[2,18,1,256]{3,2,1,0:T(2,128)(2,1)S(1)}, u32[]{:S(2)}, u32[]{:S(2)}) %collective-permute-start.8) | collective-permute-done | bytes 18464 | tf_op jit(solution)/shard_map/ppermute | solution.py:23
  52.3 0.3 fusion.108
  53.2 0.3 convolution_add_fusion.18
  54.4 0.3 fusion.5
  55.0 1.3 %collective-permute-start.9 = (bf16[2,16,16,128]{3,2,1,0:T(8,128)(2,1)S(1)}, bf16[2,16,16,128]{3,2,1,0:T(8,128)(2,1)S(1)}, u32[]{:S(2)}, u32[]{:S(2)}) collective-permute-start(bf16[2,16,16,128]{3,2,1,0:T(8,128)(2,1)S(1)} %get-tuple-element.6), channel_id=1, source_target_pairs={{0,128},{128,256},{256,384},{1,129},{129,257},{257,385},{2,130},{1... | collective-permute-start | bytes 393224 | tf_op jit(solution)/shard_map/ppermute | solution.py:10
  56.3 6.0 %collective-permute-done.9 = bf16[2,16,16,128]{3,2,1,0:T(8,128)(2,1)S(1)} collective-permute-done((bf16[2,16,16,128]{3,2,1,0:T(8,128)(2,1)S(1)}, bf16[2,16,16,128]{3,2,1,0:T(8,128)(2,1)S(1)}, u32[]{:S(2)}, u32[]{:S(2)}) %collective-permute-start.9) | collective-permute-done | bytes 131104 | tf_op jit(solution)/shard_map/ppermute | solution.py:10
  62.3 3.6 %collective-permute-start.10 = (bf16[2,1,16,256]{3,2,1,0:T(8,128)(2,1)S(1)}, bf16[2,1,16,256]{3,2,1,0:T(8,128)(2,1)S(1)}, u32[]{:S(2)}, u32[]{:S(2)}) collective-permute-start(bf16[2,1,16,256]{3,2,1,0:T(8,128)(2,1)S(1)} %get-tuple-element.64), channel_id=1, source_target_pairs={{0,16},{16,32},{32,48},{48,64},{64,80},{80,96},{96,112},{1,17},{17... | collective-permute-start | bytes 49160 | tf_op jit(solution)/shard_map/ppermute | solution.py:21
  65.9 1.9 %collective-permute-start.11 = (bf16[2,1,16,256]{3,2,1,0:T(8,128)(2,1)S(1)}, bf16[2,1,16,256]{3,2,1,0:T(8,128)(2,1)S(1)}, u32[]{:S(2)}, u32[]{:S(2)}) collective-permute-start(bf16[2,1,16,256]{3,2,1,0:T(8,128)(2,1)S(1)} %get-tuple-element.65), channel_id=1, source_target_pairs={{16,0},{32,16},{48,32},{64,48},{80,64},{96,80},{112,96},{17,1},{33... | collective-permute-start | bytes 49160 | tf_op jit(solution)/shard_map/ppermute | solution.py:23
  67.8 3.1 %collective-permute-done.11 = bf16[2,1,16,256]{3,2,1,0:T(8,128)(2,1)S(1)} collective-permute-done((bf16[2,1,16,256]{3,2,1,0:T(8,128)(2,1)S(1)}, bf16[2,1,16,256]{3,2,1,0:T(8,128)(2,1)S(1)}, u32[]{:S(2)}, u32[]{:S(2)}) %collective-permute-start.11) | collective-permute-done | bytes 16416 | tf_op jit(solution)/shard_map/ppermute | solution.py:23
  71.1 2.0 %collective-permute-start.12 = (bf16[2,18,1,256]{3,2,1,0:T(2,128)(2,1)S(1)}, bf16[2,18,1,256]{3,2,1,0:T(2,128)(2,1)S(1)}, u32[]{:S(2)}, u32[]{:S(2)}) collective-permute-start(bf16[2,18,1,256]{3,2,1,0:T(2,128)(2,1)S(1)} %get-tuple-element.44), channel_id=1, source_target_pairs={{0,1},{1,2},{2,3},{3,4},{4,5},{5,6},{6,7},{7,8},{8,9},{9,10},{10,1... | collective-permute-start | bytes 55304 | tf_op jit(solution)/shard_map/ppermute | solution.py:21
  73.1 3.3 %collective-permute-start.13 = (bf16[2,18,1,256]{3,2,1,0:T(2,128)(2,1)S(1)}, bf16[2,18,1,256]{3,2,1,0:T(2,128)(2,1)S(1)}, u32[]{:S(2)}, u32[]{:S(2)}) collective-permute-start(bf16[2,18,1,256]{3,2,1,0:T(2,128)(2,1)S(1)} %get-tuple-element.45), channel_id=1, source_target_pairs={{1,0},{2,1},{3,2},{4,3},{5,4},{6,5},{7,6},{8,7},{9,8},{10,9},{11,1... | collective-permute-start | bytes 55304 | tf_op jit(solution)/shard_map/ppermute | solution.py:23
  76.4 0.3 fusion.138
  76.7 2.7 %collective-permute-done.13 = bf16[2,18,1,256]{3,2,1,0:T(2,128)(2,1)S(1)} collective-permute-done((bf16[2,18,1,256]{3,2,1,0:T(2,128)(2,1)S(1)}, bf16[2,18,1,256]{3,2,1,0:T(2,128)(2,1)S(1)}, u32[]{:S(2)}, u32[]{:S(2)}) %collective-permute-start.13) | collective-permute-done | bytes 18464 | tf_op jit(solution)/shard_map/ppermute | solution.py:23
  80.2 0.3 convolution_add_fusion.13
  81.4 0.3 convolution_add_fusion.9
  82.4 1.0 fusion.150
  83.4 1.3 %collective-permute-start.14 = (bf16[2,16,16,128]{3,2,1,0:T(8,128)(2,1)S(1)}, bf16[2,16,16,128]{3,2,1,0:T(8,128)(2,1)S(1)}, u32[]{:S(2)}, u32[]{:S(2)}) collective-permute-start(bf16[2,16,16,128]{3,2,1,0:T(8,128)(2,1)S(1)} %get-tuple-element.4), channel_id=1, source_target_pairs={{0,128},{128,256},{256,384},{1,129},{129,257},{257,385},{2,130},{1... | collective-permute-start | bytes 393224 | tf_op jit(solution)/shard_map/ppermute | solution.py:10
  84.7 5.5 %collective-permute-done.14 = bf16[2,16,16,128]{3,2,1,0:T(8,128)(2,1)S(1)} collective-permute-done((bf16[2,16,16,128]{3,2,1,0:T(8,128)(2,1)S(1)}, bf16[2,16,16,128]{3,2,1,0:T(8,128)(2,1)S(1)}, u32[]{:S(2)}, u32[]{:S(2)}) %collective-permute-start.14) | collective-permute-done | bytes 131104 | tf_op jit(solution)/shard_map/ppermute | solution.py:10
  90.2 3.6 %collective-permute-start.15 = (bf16[2,1,16,256]{3,2,1,0:T(8,128)(2,1)S(1)}, bf16[2,1,16,256]{3,2,1,0:T(8,128)(2,1)S(1)}, u32[]{:S(2)}, u32[]{:S(2)}) collective-permute-start(bf16[2,1,16,256]{3,2,1,0:T(8,128)(2,1)S(1)} %get-tuple-element.62), channel_id=1, source_target_pairs={{0,16},{16,32},{32,48},{48,64},{64,80},{80,96},{96,112},{1,17},{17... | collective-permute-start | bytes 49160 | tf_op jit(solution)/shard_map/ppermute | solution.py:21
  93.8 1.9 %collective-permute-start.16 = (bf16[2,1,16,256]{3,2,1,0:T(8,128)(2,1)S(1)}, bf16[2,1,16,256]{3,2,1,0:T(8,128)(2,1)S(1)}, u32[]{:S(2)}, u32[]{:S(2)}) collective-permute-start(bf16[2,1,16,256]{3,2,1,0:T(8,128)(2,1)S(1)} %get-tuple-element.63), channel_id=1, source_target_pairs={{16,0},{32,16},{48,32},{64,48},{80,64},{96,80},{112,96},{17,1},{33... | collective-permute-start | bytes 49160 | tf_op jit(solution)/shard_map/ppermute | solution.py:23
  95.8 3.1 %collective-permute-done.16 = bf16[2,1,16,256]{3,2,1,0:T(8,128)(2,1)S(1)} collective-permute-done((bf16[2,1,16,256]{3,2,1,0:T(8,128)(2,1)S(1)}, bf16[2,1,16,256]{3,2,1,0:T(8,128)(2,1)S(1)}, u32[]{:S(2)}, u32[]{:S(2)}) %collective-permute-start.16) | collective-permute-done | bytes 16416 | tf_op jit(solution)/shard_map/ppermute | solution.py:23
  99.0 3.8 %collective-permute-start.17 = (bf16[2,18,1,256]{3,2,1,0:T(2,128)(2,1)S(1)}, bf16[2,18,1,256]{3,2,1,0:T(2,128)(2,1)S(1)}, u32[]{:S(2)}, u32[]{:S(2)}) collective-permute-start(bf16[2,18,1,256]{3,2,1,0:T(2,128)(2,1)S(1)} %get-tuple-element.40), channel_id=1, source_target_pairs={{0,1},{1,2},{2,3},{3,4},{4,5},{5,6},{6,7},{7,8},{8,9},{9,10},{10,1... | collective-permute-start | bytes 55304 | tf_op jit(solution)/shard_map/ppermute | solution.py:21
  102.7 1.9 %collective-permute-start.18 = (bf16[2,18,1,256]{3,2,1,0:T(2,128)(2,1)S(1)}, bf16[2,18,1,256]{3,2,1,0:T(2,128)(2,1)S(1)}, u32[]{:S(2)}, u32[]{:S(2)}) collective-permute-start(bf16[2,18,1,256]{3,2,1,0:T(2,128)(2,1)S(1)} %get-tuple-element.41), channel_id=1, source_target_pairs={{1,0},{2,1},{3,2},{4,3},{5,4},{6,5},{7,6},{8,7},{9,8},{10,9},{11,1... | collective-permute-start | bytes 55304 | tf_op jit(solution)/shard_map/ppermute | solution.py:23
  105.0 4.1 %collective-permute-done.18 = bf16[2,18,1,256]{3,2,1,0:T(2,128)(2,1)S(1)} collective-permute-done((bf16[2,18,1,256]{3,2,1,0:T(2,128)(2,1)S(1)}, bf16[2,18,1,256]{3,2,1,0:T(2,128)(2,1)S(1)}, u32[]{:S(2)}, u32[]{:S(2)}) %collective-permute-start.18) | collective-permute-done | bytes 18464 | tf_op jit(solution)/shard_map/ppermute | solution.py:23
  111.1 0.3 convolution_add_fusion.2
  112.0 0.6 copy-done.4
  112.6 0.9 select_bitcast_fusion
  113.5 0.8 select_bitcast_fusion.1
  (93 shorter events, 10.6 us)
Async XLA Ops:
  0.6 21.4 %copy-start = (bf16[1,2,16,16,128]{4,3,2,1,0:T(8,128)(2,1)S(1)}, bf16[1,2,16,16,128]{4,3,2,1,0:T(8,128)(2,1)}, u32[]{:S(2)}) copy-start(bf16[1,2,16,16,128]{4,3,2,1,0:T(8,128)(2,1)} %param.6) | copy-start | bytes 393220
  0.6 21.4 %copy-start.2 = (bf16[2,16,16,128]{3,2,1,0:T(8,128)(2,1)S(1)}, bf16[2,16,16,128]{3,2,1,0:T(8,128)(2,1)}, u32[]{:S(2)}) copy-start(bf16[2,16,16,128]{3,2,1,0:T(8,128)(2,1)} %param.5) | copy-start | bytes 393220
  1.5 31.6 %copy-start.11 = (bf16[2,1,16,256]{3,2,1,0:T(8,128)(2,1)}, bf16[2,1,16,256]{3,2,1,0:T(8,128)(2,1)S(1)}, u32[]{:S(2)}) copy-start(bf16[2,1,16,256]{3,2,1,0:T(8,128)(2,1)S(1)} %get-tuple-element.69) | copy-start | bytes 49156
  1.5 5.7 %collective-permute-start = (bf16[2,1,16,256]{3,2,1,0:T(8,128)(2,1)S(1)}, bf16[2,1,16,256]{3,2,1,0:T(8,128)(2,1)S(1)}, u32[]{:S(2)}, u32[]{:S(2)}) collective-permute-start(bf16[2,1,16,256]{3,2,1,0:T(8,128)(2,1)S(1)} %get-tuple-element.10), channel_id=1, source_target_pairs={{0,16},{16,32},{32,48},{48,64},{64,80},{80,96},{96,112},{1,17},{17... | collective-permute-start | bytes 49160 | tf_op jit(solution)/shard_map/ppermute | solution.py:21
  5.2 5.1 %collective-permute-start.1 = (bf16[2,1,16,256]{3,2,1,0:T(8,128)(2,1)S(1)}, bf16[2,1,16,256]{3,2,1,0:T(8,128)(2,1)S(1)}, u32[]{:S(2)}, u32[]{:S(2)}) collective-permute-start(bf16[2,1,16,256]{3,2,1,0:T(8,128)(2,1)S(1)} %get-tuple-element.68), channel_id=1, source_target_pairs={{16,0},{32,16},{48,32},{64,48},{80,64},{96,80},{112,96},{17,1},{33... | collective-permute-start | bytes 49160 | tf_op jit(solution)/shard_map/ppermute | solution.py:23
  11.4 9.1 %collective-permute-start.2 = (bf16[2,18,1,256]{3,2,1,0:T(2,128)(2,1)S(1)}, bf16[2,18,1,256]{3,2,1,0:T(2,128)(2,1)S(1)}, u32[]{:S(2)}, u32[]{:S(2)}) collective-permute-start(bf16[2,18,1,256]{3,2,1,0:T(2,128)(2,1)S(1)} %get-tuple-element.52), channel_id=1, source_target_pairs={{0,1},{1,2},{2,3},{3,4},{4,5},{5,6},{6,7},{7,8},{8,9},{9,10},{10,1... | collective-permute-start | bytes 55304 | tf_op jit(solution)/shard_map/ppermute | solution.py:21
  16.1 5.9 %collective-permute-start.3 = (bf16[2,18,1,256]{3,2,1,0:T(2,128)(2,1)S(1)}, bf16[2,18,1,256]{3,2,1,0:T(2,128)(2,1)S(1)}, u32[]{:S(2)}, u32[]{:S(2)}) collective-permute-start(bf16[2,18,1,256]{3,2,1,0:T(2,128)(2,1)S(1)} %get-tuple-element.53), channel_id=1, source_target_pairs={{1,0},{2,1},{3,2},{4,3},{5,4},{6,5},{7,6},{8,7},{9,8},{10,9},{11,1... | collective-permute-start | bytes 55304 | tf_op jit(solution)/shard_map/ppermute | solution.py:23
  20.5 2.0 %copy-start.1 = (bf16[1,9,256,512]{3,2,1,0:T(8,128)(2,1)S(1)}, bf16[1,9,256,512]{3,2,1,0:T(8,128)(2,1)}, u32[]{:S(2)}) copy-start(bf16[1,9,256,512]{3,2,1,0:T(8,128)(2,1)} %param.8) | copy-start | bytes 7077892
  24.0 0.7 copy-start.13
  24.6 1.0 copy-start.3
  25.8 26.3 %copy-start.5 = (bf16[2,16,16,128]{3,2,1,0:T(8,128)(2,1)}, bf16[2,16,16,128]{3,2,1,0:T(8,128)(2,1)S(1)}, u32[]{:S(2)}) copy-start(bf16[2,16,16,128]{3,2,1,0:T(8,128)(2,1)S(1)} %get-tuple-element.8) | copy-start | bytes 393220
  25.8 7.3 %collective-permute-start.4 = (bf16[2,16,16,128]{3,2,1,0:T(8,128)(2,1)S(1)}, bf16[2,16,16,128]{3,2,1,0:T(8,128)(2,1)S(1)}, u32[]{:S(2)}, u32[]{:S(2)}) collective-permute-start(bf16[2,16,16,128]{3,2,1,0:T(8,128)(2,1)S(1)} %get-tuple-element.8), channel_id=1, source_target_pairs={{0,128},{128,256},{256,384},{1,129},{129,257},{257,385},{2,130},{1... | collective-permute-start | bytes 393224 | tf_op jit(solution)/shard_map/ppermute | solution.py:10
  33.1 5.6 %collective-permute-start.5 = (bf16[2,1,16,256]{3,2,1,0:T(8,128)(2,1)S(1)}, bf16[2,1,16,256]{3,2,1,0:T(8,128)(2,1)S(1)}, u32[]{:S(2)}, u32[]{:S(2)}) collective-permute-start(bf16[2,1,16,256]{3,2,1,0:T(8,128)(2,1)S(1)} %get-tuple-element.66), channel_id=1, source_target_pairs={{0,16},{16,32},{32,48},{48,64},{64,80},{80,96},{96,112},{1,17},{17... | collective-permute-start | bytes 49160 | tf_op jit(solution)/shard_map/ppermute | solution.py:21
  36.8 5.1 %collective-permute-start.6 = (bf16[2,1,16,256]{3,2,1,0:T(8,128)(2,1)S(1)}, bf16[2,1,16,256]{3,2,1,0:T(8,128)(2,1)S(1)}, u32[]{:S(2)}, u32[]{:S(2)}) collective-permute-start(bf16[2,1,16,256]{3,2,1,0:T(8,128)(2,1)S(1)} %get-tuple-element.67), channel_id=1, source_target_pairs={{16,0},{32,16},{48,32},{64,48},{80,64},{96,80},{112,96},{17,1},{33... | collective-permute-start | bytes 49160 | tf_op jit(solution)/shard_map/ppermute | solution.py:23
  42.0 6.2 %collective-permute-start.7 = (bf16[2,18,1,256]{3,2,1,0:T(2,128)(2,1)S(1)}, bf16[2,18,1,256]{3,2,1,0:T(2,128)(2,1)S(1)}, u32[]{:S(2)}, u32[]{:S(2)}) collective-permute-start(bf16[2,18,1,256]{3,2,1,0:T(2,128)(2,1)S(1)} %get-tuple-element.48), channel_id=1, source_target_pairs={{0,1},{1,2},{2,3},{3,4},{4,5},{5,6},{6,7},{7,8},{8,9},{9,10},{10,1... | collective-permute-start | bytes 55304 | tf_op jit(solution)/shard_map/ppermute | solution.py:21
  45.9 5.9 %collective-permute-start.8 = (bf16[2,18,1,256]{3,2,1,0:T(2,128)(2,1)S(1)}, bf16[2,18,1,256]{3,2,1,0:T(2,128)(2,1)S(1)}, u32[]{:S(2)}, u32[]{:S(2)}) collective-permute-start(bf16[2,18,1,256]{3,2,1,0:T(2,128)(2,1)S(1)} %get-tuple-element.49), channel_id=1, source_target_pairs={{1,0},{2,1},{3,2},{4,3},{5,4},{6,5},{7,6},{8,7},{9,8},{10,9},{11,1... | collective-permute-start | bytes 55304 | tf_op jit(solution)/shard_map/ppermute | solution.py:23
  54.4 7.9 %copy-start.12 = (bf16[2,1,16,256]{3,2,1,0:T(8,128)(2,1)S(1)}, bf16[2,1,16,256]{3,2,1,0:T(8,128)(2,1)}, u32[]{:S(2)}) copy-start(bf16[2,1,16,256]{3,2,1,0:T(8,128)(2,1)} %copy-done.11) | copy-start | bytes 49156
  55.0 24.8 %copy-start.7 = (bf16[2,16,16,128]{3,2,1,0:T(8,128)(2,1)}, bf16[2,16,16,128]{3,2,1,0:T(8,128)(2,1)S(1)}, u32[]{:S(2)}) copy-start(bf16[2,16,16,128]{3,2,1,0:T(8,128)(2,1)S(1)} %get-tuple-element.6) | copy-start | bytes 393220
  55.0 7.2 %collective-permute-start.9 = (bf16[2,16,16,128]{3,2,1,0:T(8,128)(2,1)S(1)}, bf16[2,16,16,128]{3,2,1,0:T(8,128)(2,1)S(1)}, u32[]{:S(2)}, u32[]{:S(2)}) collective-permute-start(bf16[2,16,16,128]{3,2,1,0:T(8,128)(2,1)S(1)} %get-tuple-element.6), channel_id=1, source_target_pairs={{0,128},{128,256},{256,384},{1,129},{129,257},{257,385},{2,130},{1... | collective-permute-start | bytes 393224 | tf_op jit(solution)/shard_map/ppermute | solution.py:10
  62.3 5.6 %collective-permute-start.10 = (bf16[2,1,16,256]{3,2,1,0:T(8,128)(2,1)S(1)}, bf16[2,1,16,256]{3,2,1,0:T(8,128)(2,1)S(1)}, u32[]{:S(2)}, u32[]{:S(2)}) collective-permute-start(bf16[2,1,16,256]{3,2,1,0:T(8,128)(2,1)S(1)} %get-tuple-element.64), channel_id=1, source_target_pairs={{0,16},{16,32},{32,48},{48,64},{64,80},{80,96},{96,112},{1,17},{17... | collective-permute-start | bytes 49160 | tf_op jit(solution)/shard_map/ppermute | solution.py:21
  65.9 5.1 %collective-permute-start.11 = (bf16[2,1,16,256]{3,2,1,0:T(8,128)(2,1)S(1)}, bf16[2,1,16,256]{3,2,1,0:T(8,128)(2,1)S(1)}, u32[]{:S(2)}, u32[]{:S(2)}) collective-permute-start(bf16[2,1,16,256]{3,2,1,0:T(8,128)(2,1)S(1)} %get-tuple-element.65), channel_id=1, source_target_pairs={{16,0},{32,16},{48,32},{64,48},{80,64},{96,80},{112,96},{17,1},{33... | collective-permute-start | bytes 49160 | tf_op jit(solution)/shard_map/ppermute | solution.py:23
  71.1 5.6 %collective-permute-start.12 = (bf16[2,18,1,256]{3,2,1,0:T(2,128)(2,1)S(1)}, bf16[2,18,1,256]{3,2,1,0:T(2,128)(2,1)S(1)}, u32[]{:S(2)}, u32[]{:S(2)}) collective-permute-start(bf16[2,18,1,256]{3,2,1,0:T(2,128)(2,1)S(1)} %get-tuple-element.44), channel_id=1, source_target_pairs={{0,1},{1,2},{2,3},{3,4},{4,5},{5,6},{6,7},{7,8},{8,9},{9,10},{10,1... | collective-permute-start | bytes 55304 | tf_op jit(solution)/shard_map/ppermute | solution.py:21
  73.1 6.4 %collective-permute-start.13 = (bf16[2,18,1,256]{3,2,1,0:T(2,128)(2,1)S(1)}, bf16[2,18,1,256]{3,2,1,0:T(2,128)(2,1)S(1)}, u32[]{:S(2)}, u32[]{:S(2)}) collective-permute-start(bf16[2,18,1,256]{3,2,1,0:T(2,128)(2,1)S(1)} %get-tuple-element.45), channel_id=1, source_target_pairs={{1,0},{2,1},{3,2},{4,3},{5,4},{6,5},{7,6},{8,7},{9,8},{10,9},{11,1... | collective-permute-start | bytes 55304 | tf_op jit(solution)/shard_map/ppermute | solution.py:23
  81.4 0.7 copy-start.14
  83.4 1.3 %copy-start.9 = (bf16[2,16,16,128]{3,2,1,0:T(8,128)(2,1)}, bf16[2,16,16,128]{3,2,1,0:T(8,128)(2,1)S(1)}, u32[]{:S(2)}) copy-start(bf16[2,16,16,128]{3,2,1,0:T(8,128)(2,1)S(1)} %get-tuple-element.4) | copy-start | bytes 393220
  83.4 6.8 %collective-permute-start.14 = (bf16[2,16,16,128]{3,2,1,0:T(8,128)(2,1)S(1)}, bf16[2,16,16,128]{3,2,1,0:T(8,128)(2,1)S(1)}, u32[]{:S(2)}, u32[]{:S(2)}) collective-permute-start(bf16[2,16,16,128]{3,2,1,0:T(8,128)(2,1)S(1)} %get-tuple-element.4), channel_id=1, source_target_pairs={{0,128},{128,256},{256,384},{1,129},{129,257},{257,385},{2,130},{1... | collective-permute-start | bytes 393224 | tf_op jit(solution)/shard_map/ppermute | solution.py:10
  90.2 5.6 %collective-permute-start.15 = (bf16[2,1,16,256]{3,2,1,0:T(8,128)(2,1)S(1)}, bf16[2,1,16,256]{3,2,1,0:T(8,128)(2,1)S(1)}, u32[]{:S(2)}, u32[]{:S(2)}) collective-permute-start(bf16[2,1,16,256]{3,2,1,0:T(8,128)(2,1)S(1)} %get-tuple-element.62), channel_id=1, source_target_pairs={{0,16},{16,32},{32,48},{48,64},{64,80},{80,96},{96,112},{1,17},{17... | collective-permute-start | bytes 49160 | tf_op jit(solution)/shard_map/ppermute | solution.py:21
  93.8 5.1 %collective-permute-start.16 = (bf16[2,1,16,256]{3,2,1,0:T(8,128)(2,1)S(1)}, bf16[2,1,16,256]{3,2,1,0:T(8,128)(2,1)S(1)}, u32[]{:S(2)}, u32[]{:S(2)}) collective-permute-start(bf16[2,1,16,256]{3,2,1,0:T(8,128)(2,1)S(1)} %get-tuple-element.63), channel_id=1, source_target_pairs={{16,0},{32,16},{48,32},{64,48},{80,64},{96,80},{112,96},{17,1},{33... | collective-permute-start | bytes 49160 | tf_op jit(solution)/shard_map/ppermute | solution.py:23
  99.0 6.1 %collective-permute-start.17 = (bf16[2,18,1,256]{3,2,1,0:T(2,128)(2,1)S(1)}, bf16[2,18,1,256]{3,2,1,0:T(2,128)(2,1)S(1)}, u32[]{:S(2)}, u32[]{:S(2)}) collective-permute-start(bf16[2,18,1,256]{3,2,1,0:T(2,128)(2,1)S(1)} %get-tuple-element.40), channel_id=1, source_target_pairs={{0,1},{1,2},{2,3},{3,4},{4,5},{5,6},{6,7},{7,8},{8,9},{9,10},{10,1... | collective-permute-start | bytes 55304 | tf_op jit(solution)/shard_map/ppermute | solution.py:21
  102.7 6.4 %collective-permute-start.18 = (bf16[2,18,1,256]{3,2,1,0:T(2,128)(2,1)S(1)}, bf16[2,18,1,256]{3,2,1,0:T(2,128)(2,1)S(1)}, u32[]{:S(2)}, u32[]{:S(2)}) collective-permute-start(bf16[2,18,1,256]{3,2,1,0:T(2,128)(2,1)S(1)} %get-tuple-element.41), channel_id=1, source_target_pairs={{1,0},{2,1},{3,2},{4,3},{5,4},{6,5},{7,6},{8,7},{9,8},{10,9},{11,1... | collective-permute-start | bytes 55304 | tf_op jit(solution)/shard_map/ppermute | solution.py:23
  111.1 0.7 copy-start.15
  111.7 1.0 copy-start.4
  111.7 1.8 %copy-start.6 = (bf16[2,16,16,128]{3,2,1,0:T(8,128)(2,1)S(1)}, bf16[2,16,16,128]{3,2,1,0:T(8,128)(2,1)}, u32[]{:S(2)}) copy-start(bf16[2,16,16,128]{3,2,1,0:T(8,128)(2,1)} %copy-done.5) | copy-start | bytes 393220
  111.7 1.8 %copy-start.8 = (bf16[2,16,16,128]{3,2,1,0:T(8,128)(2,1)S(1)}, bf16[2,16,16,128]{3,2,1,0:T(8,128)(2,1)}, u32[]{:S(2)}) copy-start(bf16[2,16,16,128]{3,2,1,0:T(8,128)(2,1)} %copy-done.7) | copy-start | bytes 393220
  111.7 1.8 %copy-start.10 = (bf16[2,16,16,128]{3,2,1,0:T(8,128)(2,1)S(1)}, bf16[2,16,16,128]{3,2,1,0:T(8,128)(2,1)}, u32[]{:S(2)}) copy-start(bf16[2,16,16,128]{3,2,1,0:T(8,128)(2,1)} %copy-done.9) | copy-start | bytes 393220
where the time goes:
time: 115 us; the launch traced here: 114 us
  starting transfers between devices  49.7 us (43%)
  waiting for transfers between devices  41.9 us (36%)
  matrix products  11.5 us (10%)
  other arithmetic  7.56 us (7%)
  local copies, waits for them, and re-layouts  2.28 us (2%)
  between operations  1.4 us (1%)
    ppermute x8, starting transfers between devices, padded_2(): lax.ppermute(tail, axis, [(i, (i + 1) % count) for i in range(ends)])  29.2 us
    ppermute x8, waiting for transfers between devices, padded_2(): lax.ppermute(head, axis, [((i + 1) % count, i) for i in range(ends)])  24.5 us
    ppermute x3, waiting for transfers between devices, shifted(): return lax.ppermute(x, axis, pairs)  17.4 us
    ppermute x8, starting transfers between devices, padded_2(): lax.ppermute(head, axis, [((i + 1) % count, i) for i in range(ends)])  16.7 us
    dot_general x36, matrix products, gate_update(): jnp.dot(window, kernel[tap], preferred_element_type=jnp.float32)  11.5 us
    ppermute x3, starting transfers between devices, shifted(): return lax.ppermute(x, axis, pairs)  3.86 us
    concatenate x12, other arithmetic, padded_2(): jnp.concatenate([lax.ppermute(tail, axis, [(i, (i + 1) % count) for i in...  3.42 us
  transfers between devices with their start and end apart: 19, of which 11 were waited for; matrix products, arithmetic and copies ran while one was open for 3% of the time, Pallas kernels for 0%

commit v1 on v0

v1 whole, which is shorter than its diff:
```python
import functools

import jax
import jax.numpy as jnp
from jax import lax
from jax.experimental import pallas as pl
from jax.experimental.pallas import tpu as pltpu
from jax.sharding import PartitionSpec as P

F32 = jnp.float32
BF16 = jnp.bfloat16


def sigmoid(x):
    return 0.5 * jnp.tanh(0.5 * x) + 0.5


def rolled(x, by):
    rows = x.shape[0]
    by = by % rows
    return x if by == 0 else pltpu.roll(x, rows - by, 0)


def layer_kernel(tick, batch, stride, tile, blocks, first, sec_ref, x_ref, hid_ref, cell_ref, w_ref, b_ref, m_ref, *rest):
    if first:
        hout_ref, cout_ref, send_ref, cols, htile, ctile, sems = rest
    else:
        _, _, hout_ref, cout_ref, send_ref, cols, htile, ctile, sems = rest
    edge = 3 - tick
    count = tile + 2 * edge
    rows = count * stride
    chans = 128

    @pl.when(sec_ref[0] == tick)
    def _():
        layer_in = (x_ref[batch] if tick == 0 else x_ref[...]).astype(F32)
        hidden = hid_ref[batch].astype(F32)
        for dx in range(3):
            xs = rolled(layer_in, dx)
            hs = rolled(hidden, tick + dx)
            for dy in range(3):
                at = (3 * dy + dx) * 2 * chans
                cols[:, at : at + chans] = xs[dy * stride : dy * stride + rows].astype(BF16)
                cols[:, at + chans : at + 2 * chans] = hs[
                    (tick + dy) * stride : (tick + dy) * stride + rows
                ].astype(BF16)
        cell_prev = rolled(cell_ref[batch], tick + 1)[(tick + 1) * stride : (tick + 1) * stride + rows]
        size = rows // blocks
        hs, cs = [], []
        for k in range(blocks):
            part = slice(k * size, (k + 1) * size)
            gates = jnp.dot(cols[part], w_ref[...], preferred_element_type=F32) + b_ref[...]
            cell = sigmoid(gates[:, chans : 2 * chans]) * cell_prev[part] + sigmoid(gates[:, :chans]) * jnp.tanh(
                gates[:, 2 * chans : 3 * chans]
            )
            hid = sigmoid(gates[:, 3 * chans :]) * jnp.tanh(cell)
            hs.append(hid * m_ref[part, :])
            cs.append(cell)
        hid = jnp.concatenate(hs, axis=0)
        cell = jnp.concatenate(cs, axis=0)
        send_ref[...] = hid.astype(BF16)
        mid = lambda v: rolled(v, edge)[edge * stride : (edge + tile) * stride].reshape(tile, stride, chans)[:, :tile]
        htile[...] = mid(hid).astype(BF16)
        ctile[...] = mid(cell)
        store_h = pltpu.make_async_copy(htile, hout_ref.at[0, batch], sems.at[0])
        store_c = pltpu.make_async_copy(ctile, cout_ref.at[0, batch], sems.at[1])
        store_h.start()
        store_c.start()
        store_h.wait()
        store_c.wait()


def layer(tick, batch, tile, sec, x, hid, cell, w, b, mask, outs):
    stride = tile + 8
    rows = (tile + 2 * (3 - tick)) * stride
    first = outs is None
    vmem = pl.BlockSpec(memory_space=pltpu.VMEM)
    any_ = pl.BlockSpec(memory_space=pl.ANY)
    args = [sec, x, hid, cell, w, b, mask] + ([] if first else list(outs))
    shape_h = jax.ShapeDtypeStruct((1, 2, tile, tile, 128), BF16)
    shape_c = jax.ShapeDtypeStruct((1, 2, tile, tile, 128), F32)
    hout, cout, send = pl.pallas_call(
        functools.partial(layer_kernel, tick, batch, stride, tile, 3, first),
        out_shape=(shape_h, shape_c, jax.ShapeDtypeStruct((rows, 128), BF16)),
        in_specs=[pl.BlockSpec(memory_space=pltpu.SMEM)] + [vmem] * 6 + [any_] * (len(args) - 7),
        out_specs=(any_, any_, vmem),
        scratch_shapes=[
            pltpu.VMEM((rows, 18 * 128), BF16),
            pltpu.VMEM((tile, tile, 128), BF16),
            pltpu.VMEM((tile, tile, 128), F32),
            pltpu.SemaphoreType.DMA((2,)),
        ],
        input_output_aliases={} if first else {7: 0, 8: 1},
        compiler_params=pltpu.CompilerParams(vmem_limit_bytes=24 << 20),
        cost_estimate=pl.CostEstimate(
            flops=2 * rows * 2304 * 512, bytes_accessed=4 << 20, transcendentals=rows * 640
        ),
        name=f"layer_{tick}_{batch}",
    )(*args)
    return (hout, cout), send


def exchanged(x, axis, up):
    count = lax.axis_size(axis)
    pairs = [(i, i + 1) for i in range(count - 1)]
    return lax.ppermute(x, axis, pairs if up else [(j, i) for i, j in pairs])


def on_device(latent, hidden_old, cell_old, weights, bias):
    tile = latent.shape[1]
    wide = 4
    sec = lax.axis_index("section")
    row = lax.axis_index("row")
    col = lax.axis_index("col")
    hid = hidden_old[0]
    cell = cell_old[0]

    def stacked(rows, cols):
        return jnp.concatenate(
            [latent[:, rows, cols], hid[:, rows, cols], cell[:, rows, cols].astype(BF16)], axis=-1
        )

    everything, low, high = slice(None), slice(0, wide), slice(tile - wide, tile)
    left = exchanged(stacked(everything, high), "col", True)
    right = exchanged(stacked(everything, low), "col", False)
    ends = lambda part: jnp.concatenate([left[:, part], stacked(part, everything), right[:, part]], axis=2)
    above = exchanged(ends(high), "row", True)
    below = exchanged(ends(low), "row", False)

    def whole(k, own):
        part = slice(128 * k, 128 * (k + 1))
        grab = lambda v: v[..., part].astype(own.dtype)
        mid = jnp.concatenate([grab(left), own, grab(right)], axis=2)
        full = jnp.concatenate([grab(above), mid, grab(below)], axis=1)
        return full.reshape(2, -1, 128)

    full_in, full_hid, full_cell = whole(0, latent), whole(1, hid), whole(2, cell)
    stride = tile + 2 * wide
    w = weights.reshape(-1, weights.shape[-1])
    sec_arr = sec.reshape(1).astype(jnp.int32)
    total_r = tile * lax.axis_size("row")
    total_c = tile * lax.axis_size("col")

    def mask(tick):
        edge = 3 - tick
        count = tile + 2 * edge
        r = row * tile - edge + lax.broadcasted_iota(jnp.int32, (count, stride, 128), 0)
        c = col * tile - edge + lax.broadcasted_iota(jnp.int32, (count, stride, 128), 1)
        inside = (r >= 0) & (r < total_r) & (c >= 0) & (c < total_c)
        return inside.astype(F32).reshape(-1, 128)

    outs = None
    xs = [full_in, full_in]
    for tick in range(4):
        m = mask(tick)
        nxt = []
        for batch in range(2):
            outs, send = layer(tick, batch, tile, sec_arr, xs[batch], full_hid, full_cell, w, bias, m, outs)
            if tick < 3:
                nxt.append(lax.ppermute(send, "section", [(tick, tick + 1)]))
        xs = nxt
    return outs


def solution(mesh):
    in_specs = (
        P(None, "row", "col", None),
        P("section", None, "row", "col", None),
        P("section", None, "row", "col", None),
        P("section", None, None, None),
        P("section", None),
    )
    out_specs = (P("section", None, "row", "col", None), P("section", None, "row", "col", None))
    return jax.shard_map(
        on_device, mesh=mesh, in_specs=in_specs, out_specs=out_specs, check_vma=False
    )
```

time: 115 us -> 58.5 us (0.51)
  the two profiles are of different devices: /device:TPU:103 before, /device:TPU:246 now
where the time goes in v1:
time: 58.5 us; the launch traced here: 58.1 us
  waiting for transfers between devices  23.9 us (41%)
  starting transfers between devices  18.4 us (31%)
  Pallas kernels  9.91 us (17%)
  local copies, waits for them, and re-layouts  2.73 us (5%)
  other arithmetic  2.02 us (3%)
  between operations  1.09 us (2%)
    ppermute x6, waiting for transfers between devices, on_device(): nxt.append(lax.ppermute(send, 'section', [(tick, tick + 1)]))  16.9 us
    ppermute x4, starting transfers between devices, exchanged(): return lax.ppermute(x, axis, pairs if up else [(j, i) for i, j in pairs])  12.5 us
    pallas_call x8, Pallas kernels, layer(): pl.pallas_call(functools.partial(layer_kernel, tick, batch, stride, tile,...  9.91 us
    ppermute x4, waiting for transfers between devices, exchanged(): return lax.ppermute(x, axis, pairs if up else [(j, i) for i, j in pairs])  6.98 us
    ppermute x6, starting transfers between devices, on_device(): nxt.append(lax.ppermute(send, 'section', [(tick, tick + 1)]))  5.91 us
    slice x2, local copies, waits for them, and re-layouts, stacked(): latent[:, rows, cols]  1.83 us
  transfers between devices with their start and end apart: 10, of which 5 were waited for; matrix products, arithmetic and copies ran while one was open for 4% of the time, Pallas kernels for 12%

profile of v1, /device:TPU:246, one launch (start us, length us, event | category | flops | bytes accessed | tf_op | source)
XLA Modules:
  0.0 58.1 jit_solution(7671867112950416078)
XLA Ops:
  0.6 0.0 copy-start.3
  0.6 0.0 copy-start.4
  0.7 1.0 %bitcast_convert_fusion = bf16[2,16,16,128]{3,2,1,0:T(8,128)(2,1)S(1)} fusion(f32[1,2,16,16,128]{4,3,2,1,0:T(8,128)} %param.7), kind=kLoop, calls=%fused_computation.31 | loop fusion | flops 65536 | bytes 393216 | tf_op jit(solution)/shard_map/convert.7
  1.7 1.0 %fusion.11 = (bf16[2,16,4,128]{3,2,1,0:T(4,128)(2,1)S(1)}, bf16[2,16,4,128]{3,2,1,0:T(4,128)(2,1)S(1)}, bf16[2,16,4,128]{3,2,1,0:T(4,128)(2,1)S(1)}, bf16[2,16,4,128]{3,2,1,0:T(4,128)(2,1)S(1)}) fusion(bf16[2,16,16,128]{3,2,1,0:T(8,128)(2,1)} %param.5, bf16[2,16,16,128]{3,2,1,0:T(8,128)(2,1)} %bitcast.35), kind=kLoop, calls=%fused_computation.35 | loop fusion | bytes 262144 | tf_op jit(solution)/shard_map/slice | solution.py:120
  2.8 5.0 %collective-permute-start = (bf16[2,16,4,384]{3,2,1,0:T(4,128)(2,1)S(1)}, bf16[2,16,4,384]{3,2,1,0:T(4,128)(2,1)S(1)}, u32[]{:S(2)}, u32[]{:S(2)}) collective-permute-start(bf16[2,16,4,384]{3,2,1,0:T(4,128)(2,1)S(1)} %pad_maximum_fusion.5), channel_id=1, source_target_pairs={{0,1},{1,2},{2,3},{3,4},{4,5},{5,6},{6,7},{7,8},{8,9},{9,10},{10,1... | collective-permute-start | bytes 294920 | tf_op jit(solution)/shard_map/ppermute | solution.py:106
  7.9 1.9 %collective-permute-start.1 = (bf16[2,16,4,384]{3,2,1,0:T(4,128)(2,1)S(1)}, bf16[2,16,4,384]{3,2,1,0:T(4,128)(2,1)S(1)}, u32[]{:S(2)}, u32[]{:S(2)}) collective-permute-start(bf16[2,16,4,384]{3,2,1,0:T(4,128)(2,1)S(1)} %pad_maximum_fusion.6), channel_id=1, source_target_pairs={{1,0},{2,1},{3,2},{4,3},{5,4},{6,5},{7,6},{8,7},{9,8},{10,9},{11,1... | collective-permute-start | bytes 294920 | tf_op jit(solution)/shard_map/ppermute | solution.py:106
  9.8 0.8 %fusion.8 = (bf16[2,4,16,128]{3,2,1,0:T(8,128)(2,1)S(1)}, bf16[2,4,16,128]{3,2,1,0:T(8,128)(2,1)S(1)}, bf16[2,4,16,128]{3,2,1,0:T(8,128)(2,1)S(1)}, bf16[2,4,16,128]{3,2,1,0:T(8,128)(2,1)S(1)}) fusion(bf16[2,16,16,128]{3,2,1,0:T(8,128)(2,1)} %param.5, bf16[2,16,16,128]{3,2,1,0:T(8,128)(2,1)} %bitcast.36), kind=kLoop, calls=%fused_computation.32 | loop fusion | bytes 262144 | tf_op jit(solution)/shard_map/slice | solution.py:120
  10.7 0.0 copy-start
  10.7 0.0 copy-start.1
  10.8 0.1 and_convert_fusion.2
  10.9 0.1 and_convert_fusion.1
  10.9 0.1 and_convert_fusion
  11.0 0.1 reshape.64
  11.1 0.0 copy-start.2
  11.1 4.4 %collective-permute-done.1 = bf16[2,16,4,384]{3,2,1,0:T(4,128)(2,1)S(1)} collective-permute-done((bf16[2,16,4,384]{3,2,1,0:T(4,128)(2,1)S(1)}, bf16[2,16,4,384]{3,2,1,0:T(4,128)(2,1)S(1)}, u32[]{:S(2)}, u32[]{:S(2)}) %collective-permute-start.1) | collective-permute-done | bytes 98336 | tf_op jit(solution)/shard_map/ppermute | solution.py:106
  15.6 0.1 pad_maximum_fusion.3
  15.7 1.9 %collective-permute-start.2 = (bf16[2,4,24,384]{3,2,1,0:T(8,128)(2,1)S(1)}, bf16[2,4,24,384]{3,2,1,0:T(8,128)(2,1)S(1)}, u32[]{:S(2)}, u32[]{:S(2)}) collective-permute-start(bf16[2,4,24,384]{3,2,1,0:T(8,128)(2,1)S(1)} %pad_maximum_fusion.3), channel_id=1, source_target_pairs={{0,16},{16,32},{32,48},{48,64},{64,80},{80,96},{96,112},{1,17},{17... | collective-permute-start | bytes 442376 | tf_op jit(solution)/shard_map/ppermute | solution.py:106
  17.6 0.1 pad_maximum_fusion.4
  17.7 3.6 %collective-permute-start.3 = (bf16[2,4,24,384]{3,2,1,0:T(8,128)(2,1)S(1)}, bf16[2,4,24,384]{3,2,1,0:T(8,128)(2,1)S(1)}, u32[]{:S(2)}, u32[]{:S(2)}) collective-permute-start(bf16[2,4,24,384]{3,2,1,0:T(8,128)(2,1)S(1)} %pad_maximum_fusion.4), channel_id=1, source_target_pairs={{16,0},{32,16},{48,32},{64,48},{80,64},{96,80},{112,96},{17,1},{33... | collective-permute-start | bytes 442376 | tf_op jit(solution)/shard_map/ppermute | solution.py:106
  21.4 0.7 %collective-permute-done.2 = bf16[2,4,24,384]{3,2,1,0:T(8,128)(2,1)S(1)} collective-permute-done((bf16[2,4,24,384]{3,2,1,0:T(8,128)(2,1)S(1)}, bf16[2,4,24,384]{3,2,1,0:T(8,128)(2,1)S(1)}, u32[]{:S(2)}, u32[]{:S(2)}) %collective-permute-start.2) | collective-permute-done | bytes 147488 | tf_op jit(solution)/shard_map/ppermute | solution.py:106
  22.2 1.8 %collective-permute-done.3 = bf16[2,4,24,384]{3,2,1,0:T(8,128)(2,1)S(1)} collective-permute-done((bf16[2,4,24,384]{3,2,1,0:T(8,128)(2,1)S(1)}, bf16[2,4,24,384]{3,2,1,0:T(8,128)(2,1)S(1)}, u32[]{:S(2)}, u32[]{:S(2)}) %collective-permute-start.3) | collective-permute-done | bytes 147488 | tf_op jit(solution)/shard_map/ppermute | solution.py:106
  24.0 0.1 pad_maximum_fusion.2
  24.1 0.1 pad_maximum_fusion.1
  24.3 0.1 pad_maximum_fusion
  24.4 0.1 iota.69.m_ref
  24.5 0.7 %layer_0_0.1 = (bf16[1,2,16,16,128]{4,3,2,1,0:T(8,128)(2,1)}, f32[1,2,16,16,128]{4,3,2,1,0:T(8,128)}, bf16[528,128]{1,0:T(8,128)(2,1)}) custom-call(s32[1]{0:T(128)} %bitcast.sec_ref, bf16[2,576,128]{2,1,0:T(8,128)(2,1)S(1)} %bitcast.32, bf16[2,576,128]{2,1,0:T(8,128)(2,1)S(1)} %bitcast.24, f32[2,576,128]{2,1,0:T(8,128)S(1)} %bitcast.16, ...), custom_call_target="tpu_custom_call" | custom-call | flops 1245708288 | bytes 4194304 | tf_op jit(solution)/shard_map/layer_0_0/pallas_call | solution.py:82
  25.2 0.7 %collective-permute-start.5 = (bf16[528,128]{1,0:T(8,128)(2,1)}, bf16[528,128]{1,0:T(8,128)(2,1)S(1)}, u32[]{:S(2)}, u32[]{:S(2)}) collective-permute-start(bf16[528,128]{1,0:T(8,128)(2,1)} %get-tuple-element.27), channel_id=1, source_target_pairs={{0,128},{1,129},{2,130},{3,131},{4,132},{5,133},{6,134},{7,135},{8... | collective-permute-start | bytes 405512 | tf_op jit(solution)/shard_map/ppermute | solution.py:160
  25.9 0.7 %layer_0_1.1 = (bf16[1,2,16,16,128]{4,3,2,1,0:T(8,128)(2,1)}, f32[1,2,16,16,128]{4,3,2,1,0:T(8,128)}, bf16[528,128]{1,0:T(8,128)(2,1)}) custom-call(s32[1]{0:T(128)} %bitcast.sec_ref, bf16[2,576,128]{2,1,0:T(8,128)(2,1)S(1)} %bitcast.33, bf16[2,576,128]{2,1,0:T(8,128)(2,1)S(1)} %bitcast.25, ...), custom_call_target="tpu_custom_call", output_to_operand_aliasing={{0}: (7, {}), {1}: (8, {})} | custom-call | flops 1245708288 | bytes 4194304 | tf_op jit(solution)/shard_map/layer_0_1/pallas_call | solution.py:82
  26.6 1.3 %collective-permute-start.4 = (bf16[528,128]{1,0:T(8,128)(2,1)}, bf16[528,128]{1,0:T(8,128)(2,1)}, u32[]{:S(2)}, u32[]{:S(2)}) collective-permute-start(bf16[528,128]{1,0:T(8,128)(2,1)} %get-tuple-element.26), channel_id=1, source_target_pairs={{0,128},{1,129},{2,130},{3,131},{4,132},{5,133},{6,134},{7,135},{8... | collective-permute-start | bytes 405512 | tf_op jit(solution)/shard_map/ppermute | solution.py:160
  27.9 0.1 reshape.65
  28.0 0.1 iota.75.m_ref
  28.1 0.7 %layer_1_0.1 = (bf16[1,2,16,16,128]{4,3,2,1,0:T(8,128)(2,1)}, f32[1,2,16,16,128]{4,3,2,1,0:T(8,128)}, bf16[480,128]{1,0:T(8,128)(2,1)}) custom-call(s32[1]{0:T(128)} %bitcast.sec_ref, bf16[528,128]{1,0:T(8,128)(2,1)S(1)} %collective-permute-done.5.x_ref, bf16[2,576,128]{2,1,0:T(8,128)(2,1)S(1)} %bitcast.26, ...), custom_call_target="tpu_custom_call", output_to_operand_aliasing={{0}: (7, {}), {1}: (8, {})} | custom-call | flops 1132462080 | bytes 4194304 | tf_op jit(solution)/shard_map/layer_1_0/pallas_call | solution.py:82
  28.8 0.7 %collective-permute-start.7 = (bf16[480,128]{1,0:T(8,128)(2,1)}, bf16[480,128]{1,0:T(8,128)(2,1)S(1)}, u32[]{:S(2)}, u32[]{:S(2)}) collective-permute-start(bf16[480,128]{1,0:T(8,128)(2,1)} %get-tuple-element.33), channel_id=1, source_target_pairs={{128,256},{129,257},{130,258},{131,259},{132,260},{133,261},{134,2... | collective-permute-start | bytes 368648 | tf_op jit(solution)/shard_map/ppermute | solution.py:160
  29.5 1.6 %layer_1_1.1 = (bf16[1,2,16,16,128]{4,3,2,1,0:T(8,128)(2,1)}, f32[1,2,16,16,128]{4,3,2,1,0:T(8,128)}, bf16[480,128]{1,0:T(8,128)(2,1)}) custom-call(s32[1]{0:T(128)} %bitcast.sec_ref, bf16[528,128]{1,0:T(8,128)(2,1)} %collective-permute-done.4.x_ref, bf16[2,576,128]{2,1,0:T(8,128)(2,1)S(1)} %bitcast.27, ...), custom_call_target="tpu_custom_call", output_to_operand_aliasing={{0}: (7, {}), {1}: (8, {})} | custom-call | flops 1132462080 | bytes 4194304 | tf_op jit(solution)/shard_map/layer_1_1/pallas_call | solution.py:82
  31.1 0.7 %collective-permute-start.6 = (bf16[480,128]{1,0:T(8,128)(2,1)}, bf16[480,128]{1,0:T(8,128)(2,1)S(1)}, u32[]{:S(2)}, u32[]{:S(2)}) collective-permute-start(bf16[480,128]{1,0:T(8,128)(2,1)} %get-tuple-element.32), channel_id=1, source_target_pairs={{128,256},{129,257},{130,258},{131,259},{132,260},{133,261},{134,2... | collective-permute-start | bytes 368648 | tf_op jit(solution)/shard_map/ppermute | solution.py:160
  31.8 0.1 reshape.66
  31.9 0.1 iota.81.m_ref
  32.0 0.7 %layer_2_0.1 = (bf16[1,2,16,16,128]{4,3,2,1,0:T(8,128)(2,1)}, f32[1,2,16,16,128]{4,3,2,1,0:T(8,128)}, bf16[432,128]{1,0:T(8,128)(2,1)}) custom-call(s32[1]{0:T(128)} %bitcast.sec_ref, bf16[480,128]{1,0:T(8,128)(2,1)S(1)} %collective-permute-done.7.x_ref, bf16[2,576,128]{2,1,0:T(8,128)(2,1)S(1)} %bitcast.28, ...), custom_call_target="tpu_custom_call", output_to_operand_aliasing={{0}: (7, {}), {1}: (8, {})} | custom-call | flops 1019215872 | bytes 4194304 | tf_op jit(solution)/shard_map/layer_2_0/pallas_call | solution.py:82
  32.7 1.3 %collective-permute-start.9 = (bf16[432,128]{1,0:T(8,128)(2,1)}, bf16[432,128]{1,0:T(8,128)(2,1)S(1)}, u32[]{:S(2)}, u32[]{:S(2)}) collective-permute-start(bf16[432,128]{1,0:T(8,128)(2,1)} %get-tuple-element.39), channel_id=1, source_target_pairs={{256,384},{257,385},{258,386},{259,387},{260,388},{261,389},{262,3... | collective-permute-start | bytes 331784 | tf_op jit(solution)/shard_map/ppermute | solution.py:160
  34.0 0.7 %layer_2_1.1 = (bf16[1,2,16,16,128]{4,3,2,1,0:T(8,128)(2,1)}, f32[1,2,16,16,128]{4,3,2,1,0:T(8,128)}, bf16[432,128]{1,0:T(8,128)(2,1)}) custom-call(s32[1]{0:T(128)} %bitcast.sec_ref, bf16[480,128]{1,0:T(8,128)(2,1)S(1)} %collective-permute-done.6.x_ref, bf16[2,576,128]{2,1,0:T(8,128)(2,1)S(1)} %bitcast.29, ...), custom_call_target="tpu_custom_call", output_to_operand_aliasing={{0}: (7, {}), {1}: (8, {})} | custom-call | flops 1019215872 | bytes 4194304 | tf_op jit(solution)/shard_map/layer_2_1/pallas_call | solution.py:82
  34.6 1.3 %collective-permute-start.8 = (bf16[432,128]{1,0:T(8,128)(2,1)}, bf16[432,128]{1,0:T(8,128)(2,1)S(1)}, u32[]{:S(2)}, u32[]{:S(2)}) collective-permute-start(bf16[432,128]{1,0:T(8,128)(2,1)} %get-tuple-element.38), channel_id=1, source_target_pairs={{256,384},{257,385},{258,386},{259,387},{260,388},{261,389},{262,3... | collective-permute-start | bytes 331784 | tf_op jit(solution)/shard_map/ppermute | solution.py:160
  35.9 0.1 and_convert_fusion.3
  36.0 0.1 reshape.67
  36.1 14.5 %collective-permute-done.9.x_ref = bf16[432,128]{1,0:T(8,128)(2,1)S(1)} collective-permute-done((bf16[432,128]{1,0:T(8,128)(2,1)}, bf16[432,128]{1,0:T(8,128)(2,1)S(1)}, u32[]{:S(2)}, u32[]{:S(2)}) %collective-permute-start.9) | collective-permute-done | bytes 110624 | tf_op jit(solution)/shard_map/ppermute | solution.py:160
  50.6 0.1 iota.87.m_ref
  50.7 2.5 %layer_3_0.1 = (bf16[1,2,16,16,128]{4,3,2,1,0:T(8,128)(2,1)}, f32[1,2,16,16,128]{4,3,2,1,0:T(8,128)}, bf16[384,128]{1,0:T(8,128)(2,1)}) custom-call(s32[1]{0:T(128)} %bitcast.sec_ref, bf16[432,128]{1,0:T(8,128)(2,1)S(1)} %collective-permute-done.9.x_ref, bf16[2,576,128]{2,1,0:T(8,128)(2,1)S(1)} %bitcast.30, ...), custom_call_target="tpu_custom_call", output_to_operand_aliasing={{0}: (7, {}), {1}: (8, {})} | custom-call | flops 905969664 | bytes 4194304 | tf_op jit(solution)/shard_map/layer_3_0/pallas_call | solution.py:82
  53.1 2.5 %collective-permute-done.8.x_ref = bf16[432,128]{1,0:T(8,128)(2,1)S(1)} collective-permute-done((bf16[432,128]{1,0:T(8,128)(2,1)}, bf16[432,128]{1,0:T(8,128)(2,1)S(1)}, u32[]{:S(2)}, u32[]{:S(2)}) %collective-permute-start.8) | collective-permute-done | bytes 110624 | tf_op jit(solution)/shard_map/ppermute | solution.py:160
  55.6 2.5 %layer_3_1.1 = (bf16[1,2,16,16,128]{4,3,2,1,0:T(8,128)(2,1)}, f32[1,2,16,16,128]{4,3,2,1,0:T(8,128)}, bf16[384,128]{1,0:T(8,128)(2,1)}) custom-call(s32[1]{0:T(128)} %bitcast.sec_ref, bf16[432,128]{1,0:T(8,128)(2,1)S(1)} %collective-permute-done.8.x_ref, bf16[2,576,128]{2,1,0:T(8,128)(2,1)S(1)} %bitcast.31, ...), custom_call_target="tpu_custom_call", output_to_operand_aliasing={{0}: (7, {}), {1}: (8, {})} | custom-call | flops 905969664 | bytes 4194304 | tf_op jit(solution)/shard_map/layer_3_1/pallas_call | solution.py:82
  (28 shorter events, 0.4 us)
Async XLA Ops:
  0.6 23.4 %copy-start.3 = (bf16[1,2,16,16,128]{4,3,2,1,0:T(8,128)(2,1)S(1)}, bf16[1,2,16,16,128]{4,3,2,1,0:T(8,128)(2,1)}, u32[]{:S(2)}) copy-start(bf16[1,2,16,16,128]{4,3,2,1,0:T(8,128)(2,1)} %param.6) | copy-start | bytes 393220
  0.6 23.5 %copy-start.4 = (bf16[2,16,16,128]{3,2,1,0:T(8,128)(2,1)S(1)}, bf16[2,16,16,128]{3,2,1,0:T(8,128)(2,1)}, u32[]{:S(2)}) copy-start(bf16[2,16,16,128]{3,2,1,0:T(8,128)(2,1)} %param.5) | copy-start | bytes 393220
  2.8 8.4 %collective-permute-start = (bf16[2,16,4,384]{3,2,1,0:T(4,128)(2,1)S(1)}, bf16[2,16,4,384]{3,2,1,0:T(4,128)(2,1)S(1)}, u32[]{:S(2)}, u32[]{:S(2)}) collective-permute-start(bf16[2,16,4,384]{3,2,1,0:T(4,128)(2,1)S(1)} %pad_maximum_fusion.5), channel_id=1, source_target_pairs={{0,1},{1,2},{2,3},{3,4},{4,5},{5,6},{6,7},{7,8},{8,9},{9,10},{10,1... | collective-permute-start | bytes 294920 | tf_op jit(solution)/shard_map/ppermute | solution.py:106
  7.9 7.7 %collective-permute-start.1 = (bf16[2,16,4,384]{3,2,1,0:T(4,128)(2,1)S(1)}, bf16[2,16,4,384]{3,2,1,0:T(4,128)(2,1)S(1)}, u32[]{:S(2)}, u32[]{:S(2)}) collective-permute-start(bf16[2,16,4,384]{3,2,1,0:T(4,128)(2,1)S(1)} %pad_maximum_fusion.6), channel_id=1, source_target_pairs={{1,0},{2,1},{3,2},{4,3},{5,4},{6,5},{7,6},{8,7},{9,8},{10,9},{11,1... | collective-permute-start | bytes 294920 | tf_op jit(solution)/shard_map/ppermute | solution.py:106
  10.7 13.8 %copy-start = (bf16[1,9,256,512]{3,2,1,0:T(8,128)(2,1)S(1)}, bf16[1,9,256,512]{3,2,1,0:T(8,128)(2,1)}, u32[]{:S(2)}) copy-start(bf16[1,9,256,512]{3,2,1,0:T(8,128)(2,1)} %param.8) | copy-start | bytes 7077892
  10.7 13.8 %copy-start.1 = (f32[1,512]{1,0:T(1,128)S(1)}, f32[1,512]{1,0:T(1,128)}, u32[]{:S(2)}) copy-start(f32[1,512]{1,0:T(1,128)} %b_ref.15) | copy-start | bytes 6148
  11.1 13.2 %copy-start.2 = (f32[1,2,16,16,128]{4,3,2,1,0:T(8,128)S(1)}, f32[1,2,16,16,128]{4,3,2,1,0:T(8,128)}, u32[]{:S(2)}) copy-start(f32[1,2,16,16,128]{4,3,2,1,0:T(8,128)} %param.7) | copy-start | bytes 786436
  15.7 6.5 %collective-permute-start.2 = (bf16[2,4,24,384]{3,2,1,0:T(8,128)(2,1)S(1)}, bf16[2,4,24,384]{3,2,1,0:T(8,128)(2,1)S(1)}, u32[]{:S(2)}, u32[]{:S(2)}) collective-permute-start(bf16[2,4,24,384]{3,2,1,0:T(8,128)(2,1)S(1)} %pad_maximum_fusion.3), channel_id=1, source_target_pairs={{0,16},{16,32},{32,48},{48,64},{64,80},{80,96},{96,112},{1,17},{17... | collective-permute-start | bytes 442376 | tf_op jit(solution)/shard_map/ppermute | solution.py:106
  17.7 6.3 %collective-permute-start.3 = (bf16[2,4,24,384]{3,2,1,0:T(8,128)(2,1)S(1)}, bf16[2,4,24,384]{3,2,1,0:T(8,128)(2,1)S(1)}, u32[]{:S(2)}, u32[]{:S(2)}) collective-permute-start(bf16[2,4,24,384]{3,2,1,0:T(8,128)(2,1)S(1)} %pad_maximum_fusion.4), channel_id=1, source_target_pairs={{16,0},{32,16},{48,32},{64,48},{80,64},{96,80},{112,96},{17,1},{33... | collective-permute-start | bytes 442376 | tf_op jit(solution)/shard_map/ppermute | solution.py:106
  25.2 2.8 %collective-permute-start.5 = (bf16[528,128]{1,0:T(8,128)(2,1)}, bf16[528,128]{1,0:T(8,128)(2,1)S(1)}, u32[]{:S(2)}, u32[]{:S(2)}) collective-permute-start(bf16[528,128]{1,0:T(8,128)(2,1)} %get-tuple-element.27), channel_id=1, source_target_pairs={{0,128},{1,129},{2,130},{3,131},{4,132},{5,133},{6,134},{7,135},{8... | collective-permute-start | bytes 405512 | tf_op jit(solution)/shard_map/ppermute | solution.py:160
  26.6 2.9 %collective-permute-start.4 = (bf16[528,128]{1,0:T(8,128)(2,1)}, bf16[528,128]{1,0:T(8,128)(2,1)}, u32[]{:S(2)}, u32[]{:S(2)}) collective-permute-start(bf16[528,128]{1,0:T(8,128)(2,1)} %get-tuple-element.26), channel_id=1, source_target_pairs={{0,128},{1,129},{2,130},{3,131},{4,132},{5,133},{6,134},{7,135},{8... | collective-permute-start | bytes 405512 | tf_op jit(solution)/shard_map/ppermute | solution.py:160
  28.8 3.0 %collective-permute-start.7 = (bf16[480,128]{1,0:T(8,128)(2,1)}, bf16[480,128]{1,0:T(8,128)(2,1)S(1)}, u32[]{:S(2)}, u32[]{:S(2)}) collective-permute-start(bf16[480,128]{1,0:T(8,128)(2,1)} %get-tuple-element.33), channel_id=1, source_target_pairs={{128,256},{129,257},{130,258},{131,259},{132,260},{133,261},{134,2... | collective-permute-start | bytes 368648 | tf_op jit(solution)/shard_map/ppermute | solution.py:160
  31.1 2.9 %collective-permute-start.6 = (bf16[480,128]{1,0:T(8,128)(2,1)}, bf16[480,128]{1,0:T(8,128)(2,1)S(1)}, u32[]{:S(2)}, u32[]{:S(2)}) collective-permute-start(bf16[480,128]{1,0:T(8,128)(2,1)} %get-tuple-element.32), channel_id=1, source_target_pairs={{128,256},{129,257},{130,258},{131,259},{132,260},{133,261},{134,2... | collective-permute-start | bytes 368648 | tf_op jit(solution)/shard_map/ppermute | solution.py:160
  32.7 17.9 %collective-permute-start.9 = (bf16[432,128]{1,0:T(8,128)(2,1)}, bf16[432,128]{1,0:T(8,128)(2,1)S(1)}, u32[]{:S(2)}, u32[]{:S(2)}) collective-permute-start(bf16[432,128]{1,0:T(8,128)(2,1)} %get-tuple-element.39), channel_id=1, source_target_pairs={{256,384},{257,385},{258,386},{259,387},{260,388},{261,389},{262,3... | collective-permute-start | bytes 331784 | tf_op jit(solution)/shard_map/ppermute | solution.py:160
  34.6 21.0 %collective-permute-start.8 = (bf16[432,128]{1,0:T(8,128)(2,1)}, bf16[432,128]{1,0:T(8,128)(2,1)S(1)}, u32[]{:S(2)}, u32[]{:S(2)}) collective-permute-start(bf16[432,128]{1,0:T(8,128)(2,1)} %get-tuple-element.38), channel_id=1, source_target_pairs={{256,384},{257,385},{258,386},{259,387},{260,388},{261,389},{262,3... | collective-permute-start | bytes 331784 | tf_op jit(solution)/shard_map/ppermute | solution.py:160

commit v2 on v0

v2 whole, which is shorter than its diff:
```python
import functools

import jax
import jax.numpy as jnp
from jax import lax
from jax.experimental import pallas as pl
from jax.experimental.pallas import tpu as pltpu
from jax.sharding import PartitionSpec as P

F32 = jnp.float32
BF16 = jnp.bfloat16
CH = 128
LAYERS = 4
WIDE = 4
VMEM = pl.BlockSpec(memory_space=pltpu.VMEM)
SMEM = pl.BlockSpec(memory_space=pltpu.SMEM)
ANY = pl.BlockSpec(memory_space=pl.ANY)


def sigmoid(x):
    return 0.5 * jnp.tanh(0.5 * x) + 0.5


def rolled(x, by):
    rows = x.shape[0]
    by = by % rows
    return x if by == 0 else pltpu.roll(x, rows - by, 0)


def swap_halves(x):
    tiles = x.shape[0]
    flat = x.reshape(tiles * 8, CH)
    up, down = pltpu.roll(flat, 4, 0), pltpu.roll(flat, tiles * 8 - 4, 0)
    return jnp.where(top_half(flat.shape), down, up).reshape(x.shape)


def top_half(shape):
    return lax.broadcasted_iota(jnp.int32, shape, len(shape) - 2) % 8 < 4


def call(kernel, ins, in_specs, outs, out_specs, scratch=(), aliases=None, name=None, flops=0, limit=16):
    return pl.pallas_call(
        kernel,
        out_shape=tuple(outs),
        in_specs=in_specs,
        out_specs=tuple(out_specs),
        scratch_shapes=list(scratch),
        input_output_aliases=aliases or {},
        compiler_params=pltpu.CompilerParams(vmem_limit_bytes=limit << 20),
        cost_estimate=pl.CostEstimate(flops=flops, bytes_accessed=1 << 20, transcendentals=0),
        name=name,
    )(*ins)


def pack_kernel(lat_ref, hid_ref, cell_ref, low_ref, high_ref):
    for k, ref in enumerate((lat_ref, hid_ref, cell_ref)):
        first, second = ref[0].astype(F32), ref[1].astype(F32)
        tile = first.shape[0]
        top = top_half((tile, 8, CH))
        lanes = slice(k * CH, (k + 1) * CH)
        low = jnp.where(top, first[:, :8], swap_halves(second[:, :8]))
        high = jnp.where(top, swap_halves(first[:, 8:]), second[:, 8:])
        low_ref[:, lanes] = low.reshape(tile * 8, CH).astype(BF16)
        high_ref[:, lanes] = high.reshape(tile * 8, CH).astype(BF16)


def middle(own, left, right, batch):
    tile = own.shape[0]
    left, right = (v.astype(F32).reshape(tile, 8, CH) for v in (left, right))
    if batch == 0:
        left = swap_halves(left)
    else:
        right = swap_halves(right)
    top = top_half((tile, 8, CH))
    zero = jnp.zeros((1, 8, CH), F32)
    side = jnp.where(top, right, jnp.concatenate([left[1:], zero], axis=0))
    rows = jnp.concatenate([own, side], axis=1).reshape(tile * (tile + 8), CH)
    return jnp.concatenate([left[0], rows], axis=0)


def middle_kernel(where_ref, lat_ref, hid_ref, cell_ref, left_ref, right_ref, far_ref, near_ref):
    odd = where_ref[1] == 1
    for batch in range(2):
        for k, ref in enumerate((lat_ref, hid_ref, cell_ref)):
            lanes = slice(k * CH, (k + 1) * CH)
            mid = middle(ref[batch].astype(F32), left_ref[:, lanes], right_ref[:, lanes], batch)
            up, down = mid[:104].astype(BF16), mid[288:].astype(BF16)
            rows = slice(104 * batch, 104 * (batch + 1))

            @pl.when(odd)
            def _():
                far_ref[rows, lanes] = down
                near_ref[rows, lanes] = up

            @pl.when(jnp.logical_not(odd))
            def _():
                far_ref[rows, lanes] = up
                near_ref[rows, lanes] = down


def taps(src, at, cols_ref, rows, stride, step, first):
    for dx in range(3):
        moved = rolled(src, at + dx)
        for dy in range(3):
            lane = (3 * dy + dx) * step + first
            start = dy * stride
            cols_ref[:rows, lane : lane + CH] = moved[start : start + rows].astype(BF16)


def activated(gates, cell_prev):
    cell = sigmoid(gates[:, CH : 2 * CH]) * cell_prev + sigmoid(gates[:, :CH]) * jnp.tanh(gates[:, 2 * CH : 3 * CH])
    return sigmoid(gates[:, 3 * CH :]) * jnp.tanh(cell), cell


def centre(v, edge, tile, stride):
    return rolled(v, edge)[edge * stride : (edge + tile) * stride].reshape(tile, stride, CH)[:, :tile]


def first_kernel(batch, blocks, where_ref, lat_ref, hid_ref, cell_ref, left_ref, right_ref, far_ref, near_ref,
                 w_ref, b_ref, m_ref, send_ref, htile_ref, ctile_ref, part_ref, prev_ref, win_ref, cols):
    tile = lat_ref.shape[1]
    stride = tile + 8
    sec = where_ref[0]
    odd = where_ref[1] == 1

    def full(k, ref):
        lanes = slice(k * CH, (k + 1) * CH)
        rows = slice(104 * batch, 104 * (batch + 1))
        far, near = far_ref[rows, lanes].astype(F32), near_ref[rows, lanes].astype(F32)
        above, below = jnp.where(odd, near, far), jnp.where(odd, far, near)
        mid = middle(ref[batch].astype(F32), left_ref[:, lanes], right_ref[:, lanes], batch)
        top = top_half((8, CH))
        return jnp.concatenate(
            [above[:96], jnp.where(top, above[96:], mid[:8]), mid[8:384], jnp.where(top, mid[384:], below[:8]), below[8:]],
            axis=0,
        )

    @pl.when(sec == 0)
    def _():
        rows = (tile + 6) * stride
        taps(full(0, lat_ref), WIDE, cols, rows, stride, 2 * CH, 0)
        taps(full(1, hid_ref), WIDE, cols, rows, stride, 2 * CH, CH)
        prev = rolled(full(2, cell_ref), WIDE + 1)[stride : stride + rows]
        size = rows // blocks
        hs, cs = [], []
        for k in range(blocks):
            part = slice(k * size, (k + 1) * size)
            gates = jnp.dot(cols[part, :], w_ref[...], preferred_element_type=F32) + b_ref[...]
            h, c = activated(gates, prev[part])
            hs.append(h * m_ref[part, :])
            cs.append(c)
        h, c = jnp.concatenate(hs, axis=0), jnp.concatenate(cs, axis=0)
        send_ref[...] = h.astype(BF16)
        htile_ref[...] = centre(h, 3, tile, stride).astype(BF16)
        ctile_ref[...] = centre(c, 3, tile, stride)

    for s in range(1, LAYERS):

        @pl.when(sec == s)
        def _():
            edge = 3 - s
            rows = (tile + 2 * edge) * stride
            hidden = full(1, hid_ref)[s * stride :]
            taps(hidden, WIDE + s, cols, rows, stride, CH, 0)
            prev_ref[:rows, :] = rolled(full(2, cell_ref), WIDE + 1 + s)[(s + 1) * stride : (s + 1) * stride + rows]
            own = jnp.concatenate([w_ref[(2 * t + 1) * CH : (2 * t + 2) * CH, :] for t in range(9)], axis=0)
            part_ref[:rows, :] = (
                jnp.dot(cols[:rows, : 9 * CH], own, preferred_element_type=F32) + b_ref[...]
            )
            for t in range(9):
                win_ref[t * CH : (t + 1) * CH, :] = w_ref[2 * t * CH : (2 * t + 1) * CH, :]


def next_kernel(tick, blocks, where_ref, x_ref, part_ref, prev_ref, win_ref, m_ref, *rest):
    last = tick == LAYERS - 1
    if last:
        batch, (_, _, hout_ref, cout_ref, cols, htile_ref, ctile_ref, sems) = rest[0], rest[1:]
    else:
        send_ref, htile_ref, ctile_ref, cols = rest
    tile = htile_ref.shape[0]
    stride = tile + 8
    edge = 3 - tick
    rows = (tile + 2 * edge) * stride

    @pl.when(where_ref[0] == tick)
    def _():
        taps(x_ref[...].astype(F32), 0, cols, rows, stride, CH, 0)
        size = rows // blocks
        hs, cs = [], []
        for k in range(blocks):
            part = slice(k * size, (k + 1) * size)
            gates = jnp.dot(cols[part, :], win_ref[...], preferred_element_type=F32) + part_ref[part, :]
            h, c = activated(gates, prev_ref[part, :])
            hs.append(h if last else h * m_ref[part, :])
            cs.append(c)
        h, c = jnp.concatenate(hs, axis=0), jnp.concatenate(cs, axis=0)
        if not last:
            send_ref[...] = h.astype(BF16)
        htile_ref[...] = centre(h, edge, tile, stride).astype(BF16)
        ctile_ref[...] = centre(c, edge, tile, stride)
        if last:
            copies = [
                pltpu.make_async_copy(htile_ref, hout_ref.at[0, batch], sems.at[0]),
                pltpu.make_async_copy(ctile_ref, cout_ref.at[0, batch], sems.at[1]),
            ]
            for copy in copies:
                copy.start()
            for copy in copies:
                copy.wait()


def last_kernel(batch, blocks, where_ref, x_ref, part_ref, prev_ref, win_ref, m_ref, *rest):
    next_kernel(LAYERS - 1, blocks, where_ref, x_ref, part_ref, prev_ref, win_ref, m_ref, batch, *rest)


def store_kernel(where_ref, *rest):
    tiles, (hout_ref, cout_ref, sems) = rest[:-3], rest[-3:]
    for tick in range(LAYERS - 1):

        @pl.when(where_ref[0] == tick)
        def _():
            copies = []
            for batch in range(2):
                h, c = tiles[4 * tick + 2 * batch : 4 * tick + 2 * batch + 2]
                copies.append(pltpu.make_async_copy(h, hout_ref.at[0, batch], sems.at[2 * batch]))
                copies.append(pltpu.make_async_copy(c, cout_ref.at[0, batch], sems.at[2 * batch + 1]))
            for copy in copies:
                copy.start()
            for copy in copies:
                copy.wait()


def on_device(latent, hidden_old, cell_old, weights, bias):
    tile = latent.shape[1]
    stride = tile + 8
    sec = lax.axis_index("section")
    row = lax.axis_index("row")
    col = lax.axis_index("col")
    n_row, n_col = lax.axis_size("row"), lax.axis_size("col")
    hid = hidden_old[0]
    cell = cell_old[0]
    w = weights.reshape(-1, weights.shape[-1])
    where = jnp.stack([sec, row % 2]).astype(jnp.int32)

    edge = 3 - sec
    r = row * tile - edge + lax.broadcasted_iota(jnp.int32, (tile + 6, stride, CH), 0)
    c = col * tile - edge + lax.broadcasted_iota(jnp.int32, (tile + 6, stride, CH), 1)
    inside = (r >= 0) & (r < n_row * tile) & (c >= 0) & (c < n_col * tile)
    mask = inside.astype(F32).reshape(-1, CH)

    vm = lambda shape, kind: pltpu.VMEM(shape, kind)
    low, high = call(
        pack_kernel, (latent, hid, cell), [VMEM] * 3, [vm((8 * tile, 3 * CH), BF16)] * 2, [VMEM] * 2, name="pack"
    )
    up = [(i, i + 1) for i in range(n_col - 1)]
    left = lax.ppermute(high, "col", up)
    right = lax.ppermute(low, "col", [(j, i) for i, j in up])

    far, near = call(
        middle_kernel,
        (where, latent, hid, cell, left, right),
        [SMEM] + [VMEM] * 5,
        [vm((208, 3 * CH), BF16)] * 2,
        [VMEM] * 2,
        name="middle",
    )
    odd = [(i, i + 1) for i in range(1, n_row - 1, 2)]
    even = [(i, i + 1) for i in range(0, n_row - 1, 2)]
    both = lambda pairs: pairs + [(j, i) for i, j in pairs]
    far = lax.ppermute(far, "row", both(odd))
    near = lax.ppermute(near, "row", both(even))

    most = (tile + 4) * stride
    xs, state, tiles = [], [], []
    for batch in range(2):
        send, htile, ctile, part, prev, win = call(
            functools.partial(first_kernel, batch, 3),
            (where, latent, hid, cell, left, right, far, near, w, bias, mask),
            [SMEM] + [VMEM] * 10,
            [
                vm(((tile + 6) * stride, CH), BF16),
                vm((tile, tile, CH), BF16),
                vm((tile, tile, CH), F32),
                vm((most, 4 * CH), F32),
                vm((most, CH), F32),
                vm((9 * CH, 4 * CH), BF16),
            ],
            [VMEM] * 6,
            [pltpu.VMEM(((tile + 6) * stride, 18 * CH), BF16)],
            name=f"first_{batch}",
            flops=2 * 528 * 2304 * 512,
        )
        xs.append(lax.ppermute(send, "section", [(0, 1)]))
        state.append((part, prev, win))
        tiles += [htile, ctile]

    for tick in range(1, LAYERS - 1):
        rows = (tile + 2 * (3 - tick)) * stride
        nxt = []
        for batch in range(2):
            send, htile, ctile = call(
                functools.partial(next_kernel, tick, 3),
                (where, xs[batch], *state[batch], mask),
                [SMEM] + [VMEM] * 5,
                [vm((rows, CH), BF16), vm((tile, tile, CH), BF16), vm((tile, tile, CH), F32)],
                [VMEM] * 3,
                [pltpu.VMEM((rows, 9 * CH), BF16)],
                name=f"layer_{tick}_{batch}",
                flops=2 * rows * 1152 * 512,
            )
            nxt.append(lax.ppermute(send, "section", [(tick, tick + 1)]))
            tiles += [htile, ctile]
        xs = nxt

    out_shapes = [
        jax.ShapeDtypeStruct((1, 2, tile, tile, CH), BF16),
        jax.ShapeDtypeStruct((1, 2, tile, tile, CH), F32),
    ]
    outs = call(
        store_kernel,
        (where, *tiles),
        [SMEM] + [VMEM] * len(tiles),
        out_shapes,
        [ANY, ANY],
        [pltpu.SemaphoreType.DMA((4,))],
        name="store",
    )
    for batch in range(2):
        rows = tile * stride
        outs = call(
            functools.partial(last_kernel, batch, 3),
            (where, xs[batch], *state[batch], mask, *outs),
            [SMEM] + [VMEM] * 5 + [ANY] * 2,
            out_shapes,
            [ANY, ANY],
            [
                pltpu.VMEM((rows, 9 * CH), BF16),
                pltpu.VMEM((tile, tile, CH), BF16),
                pltpu.VMEM((tile, tile, CH), F32),
                pltpu.SemaphoreType.DMA((2,)),
            ],
            aliases={6: 0, 7: 1},
            name=f"layer_3_{batch}",
            flops=2 * rows * 1152 * 512,
        )
    return tuple(outs)


def solution(mesh):
    in_specs = (
        P(None, "row", "col", None),
        P("section", None, "row", "col", None),
        P("section", None, "row", "col", None),
        P("section", None, None, None),
        P("section", None),
    )
    out_specs = (P("section", None, "row", "col", None), P("section", None, "row", "col", None))
    return jax.shard_map(
        on_device, mesh=mesh, in_specs=in_specs, out_specs=out_specs, check_vma=False
    )
```

time: 115 us -> 55.9 us (0.49)
  the two profiles are of different devices: /device:TPU:103 before, /device:TPU:230 now
where the time goes in v2:
time: 55.9 us; the launch traced here: 55.4 us
  waiting for transfers between devices  18.9 us (34%)
  starting transfers between devices  17.9 us (32%)
  Pallas kernels  10.2 us (18%)
  local copies, waits for them, and re-layouts  7.4 us (13%)
  between operations  0.94 us (2%)
    ppermute x4, waiting for transfers between devices, on_device(): nxt.append(lax.ppermute(send, 'section', [(tick, tick + 1)]))  12.4 us
    pallas_call x11, Pallas kernels, call(): pl.pallas_call(kernel, out_shape=tuple(outs), in_specs=in_specs, out_spec...  10.2 us
    unnamed x22, local copies, waits for them, and re-layouts  7.19 us
    ppermute x1, waiting for transfers between devices, on_device(): right = lax.ppermute(low, 'col', [(j, i) for i, j in up])  5.53 us
    ppermute x1, starting transfers between devices, on_device(): left = lax.ppermute(high, 'col', up)  5.17 us
    ppermute x1, starting transfers between devices, on_device(): near = lax.ppermute(near, 'row', both(even))  4.84 us
    ppermute x4, starting transfers between devices, on_device(): nxt.append(lax.ppermute(send, 'section', [(tick, tick + 1)]))  3.92 us
    ppermute x1, starting transfers between devices, on_device(): right = lax.ppermute(low, 'col', [(j, i) for i, j in up])  1.92 us
  transfers between devices with their start and end apart: 10, of which 5 were waited for; matrix products, arithmetic and copies ran while one was open for 0% of the time, Pallas kernels for 11%

profile of v2, /device:TPU:230, one launch (start us, length us, event | category | flops | bytes accessed | tf_op | source)
XLA Modules:
  0.0 55.4 jit_solution(10927998515243373267)
XLA Ops:
  0.6 0.0 copy-start.10
  0.6 0.0 copy-start
  0.7 0.9 %copy-done = f32[1,2,16,16,128]{4,3,2,1,0:T(8,128)S(1)} copy-done((f32[1,2,16,16,128]{4,3,2,1,0:T(8,128)S(1)}, f32[1,2,16,16,128]{4,3,2,1,0:T(8,128)}, u32[]{:S(2)}) %copy-start) | copy-done | bytes 262168
  1.6 0.9 %copy-done.3 = bf16[2,16,16,128]{3,2,1,0:T(8,128)(2,1)S(1)} copy-done((bf16[2,16,16,128]{3,2,1,0:T(8,128)(2,1)S(1)}, bf16[2,16,16,128]{3,2,1,0:T(8,128)(2,1)}, u32[]{:S(2)}) %copy-start.3) | copy-done | bytes 131096
  2.5 0.9 %copy-done.6 = bf16[1,2,16,16,128]{4,3,2,1,0:T(8,128)(2,1)S(1)} copy-done((bf16[1,2,16,16,128]{4,3,2,1,0:T(8,128)(2,1)S(1)}, bf16[1,2,16,16,128]{4,3,2,1,0:T(8,128)(2,1)}, u32[]{:S(2)}) %copy-start.6) | copy-done | bytes 131096
  3.4 0.1 pack.1
  3.5 5.2 %collective-permute-start = (bf16[128,384]{1,0:T(8,128)(2,1)S(1)}, bf16[128,384]{1,0:T(8,128)(2,1)S(1)}, u32[]{:S(2)}, u32[]{:S(2)}) collective-permute-start(bf16[128,384]{1,0:T(8,128)(2,1)S(1)} %get-tuple-element.34), channel_id=1, source_target_pairs={{0,1},{1,2},{2,3},{3,4},{4,5},{5,6},{6,7},{7,8},{8,9},{9,10},{10,1... | collective-permute-start | bytes 294920 | tf_op jit(solution)/shard_map/ppermute | solution.py:256
  8.7 1.9 %collective-permute-start.1 = (bf16[128,384]{1,0:T(8,128)(2,1)S(1)}, bf16[128,384]{1,0:T(8,128)(2,1)S(1)}, u32[]{:S(2)}, u32[]{:S(2)}) collective-permute-start(bf16[128,384]{1,0:T(8,128)(2,1)S(1)} %get-tuple-element.35), channel_id=1, source_target_pairs={{1,0},{2,1},{3,2},{4,3},{5,4},{6,5},{7,6},{8,7},{9,8},{10,9},{11,1... | collective-permute-start | bytes 294920 | tf_op jit(solution)/shard_map/ppermute | solution.py:257
  10.7 0.1 pad_add_fusion.where_ref
  10.7 0.1 collective-permute-done.left_ref
  10.9 5.5 %collective-permute-done.1.right_ref = bf16[128,384]{1,0:T(8,128)(2,1)S(1)} collective-permute-done((bf16[128,384]{1,0:T(8,128)(2,1)S(1)}, bf16[128,384]{1,0:T(8,128)(2,1)S(1)}, u32[]{:S(2)}, u32[]{:S(2)}) %collective-permute-start.1) | collective-permute-done | bytes 98336 | tf_op jit(solution)/shard_map/ppermute | solution.py:257
  16.4 0.9 %copy-done.1 = f32[1,2,16,16,128]{4,3,2,1,0:T(8,128)S(1)} copy-done((f32[1,2,16,16,128]{4,3,2,1,0:T(8,128)S(1)}, f32[1,2,16,16,128]{4,3,2,1,0:T(8,128)}, u32[]{:S(2)}) %copy-start.1) | copy-done | bytes 262168
  17.4 0.9 %copy-done.4 = bf16[2,16,16,128]{3,2,1,0:T(8,128)(2,1)S(1)} copy-done((bf16[2,16,16,128]{3,2,1,0:T(8,128)(2,1)S(1)}, bf16[2,16,16,128]{3,2,1,0:T(8,128)(2,1)}, u32[]{:S(2)}) %copy-start.4) | copy-done | bytes 131096
  18.3 0.9 %copy-done.7 = bf16[1,2,16,16,128]{4,3,2,1,0:T(8,128)(2,1)S(1)} copy-done((bf16[1,2,16,16,128]{4,3,2,1,0:T(8,128)(2,1)S(1)}, bf16[1,2,16,16,128]{4,3,2,1,0:T(8,128)(2,1)}, u32[]{:S(2)}) %copy-start.7) | copy-done | bytes 131096
  19.2 0.7 %middle.1 = (bf16[208,384]{1,0:T(8,128)(2,1)S(1)}, bf16[208,384]{1,0:T(8,128)(2,1)S(1)}) custom-call(s32[2]{0:T(128)S(1)} %pad_add_fusion.where_ref, bf16[2,16,16,128]{3,2,1,0:T(8,128)(2,1)S(1)} %copy-done.4, bf16[2,16,16,128]{3,2,1,0:T(8,128)(2,1)S(1)} %bitcast.10, f32[2,16,16,128]{3,2,1,0:T(8,128)S(1)} %bitcast.6, ...), custom_call_target="tpu_custom_call" | custom-call | bytes 1048576 | tf_op jit(solution)/shard_map/middle/pallas_call | solution.py:42
  19.8 0.7 %collective-permute-start.2 = (bf16[208,384]{1,0:T(8,128)(2,1)S(1)}, bf16[208,384]{1,0:T(8,128)(2,1)S(1)}, u32[]{:S(2)}, u32[]{:S(2)}) collective-permute-start(bf16[208,384]{1,0:T(8,128)(2,1)S(1)} %get-tuple-element.36), channel_id=1, source_target_pairs={{16,32},{48,64},{80,96},{32,16},{64,48},{96,80},{17,33},{49,65},{8... | collective-permute-start | bytes 479240 | tf_op jit(solution)/shard_map/ppermute | solution.py:270
  20.5 4.8 %collective-permute-start.3 = (bf16[208,384]{1,0:T(8,128)(2,1)S(1)}, bf16[208,384]{1,0:T(8,128)(2,1)S(1)}, u32[]{:S(2)}, u32[]{:S(2)}) collective-permute-start(bf16[208,384]{1,0:T(8,128)(2,1)S(1)} %get-tuple-element.37), channel_id=1, source_target_pairs={{0,16},{32,48},{64,80},{96,112},{16,0},{48,32},{80,64},{112,96},{1... | collective-permute-start | bytes 479240 | tf_op jit(solution)/shard_map/ppermute | solution.py:271
  25.4 0.1 and_convert_fusion
  25.4 0.1 reshape.18
  25.5 0.0 collective-permute-done.2.far_ref
  25.5 0.8 %collective-permute-done.3.near_ref = bf16[208,384]{1,0:T(8,128)(2,1)S(1)} collective-permute-done((bf16[208,384]{1,0:T(8,128)(2,1)S(1)}, bf16[208,384]{1,0:T(8,128)(2,1)S(1)}, u32[]{:S(2)}, u32[]{:S(2)}) %collective-permute-start.3) | collective-permute-done | bytes 159776 | tf_op jit(solution)/shard_map/ppermute | solution.py:271
  26.4 0.1 iota.21.m_ref
  26.5 0.0 copy-done.10
  26.5 0.0 copy-done.2
  26.5 0.0 copy-done.5
  26.5 0.0 copy-start.9
  26.5 1.7 %copy-done.9 = bf16[1,9,256,512]{3,2,1,0:T(8,128)(2,1)S(1)} copy-done((bf16[1,9,256,512]{3,2,1,0:T(8,128)(2,1)S(1)}, bf16[1,9,256,512]{3,2,1,0:T(8,128)(2,1)}, u32[]{:S(2)}) %copy-start.9) | copy-done | bytes 2359320
  28.2 1.3 %first_0.1 = (bf16[528,128]{1,0:T(8,128)(2,1)S(1)}, bf16[16,16,128]{2,1,0:T(8,128)(2,1)S(1)}, f32[16,16,128]{2,1,0:T(8,128)S(1)}, f32[480,512]{1,0:T(8,128)S(1)}...) custom-call(s32[2]{0:T(128)S(1)} %pad_add_fusion.where_ref, bf16[2,16,16,128]{3,2,1,0:T(8,128)(2,1)S(1)} %copy-done.5, ...), custom_call_target="tpu_custom_call" | custom-call | flops 1245708288 | bytes 1048576 | tf_op jit(solution)/shard_map/first_0/pallas_call | solution.py:42
  29.5 0.7 %collective-permute-start.7 = (bf16[528,128]{1,0:T(8,128)(2,1)S(1)}, bf16[528,128]{1,0:T(8,128)(2,1)S(1)}, u32[]{:S(2)}, u32[]{:S(2)}) collective-permute-start(bf16[528,128]{1,0:T(8,128)(2,1)S(1)} %get-tuple-element.44), channel_id=1, source_target_pairs={{0,128},{1,129},{2,130},{3,131},{4,132},{5,133},{6,134},{7,135},{8... | collective-permute-start | bytes 405512 | tf_op jit(solution)/shard_map/ppermute | solution.py:293
  30.2 1.3 %first_1.1 = (bf16[528,128]{1,0:T(8,128)(2,1)S(1)}, bf16[16,16,128]{2,1,0:T(8,128)(2,1)S(1)}, f32[16,16,128]{2,1,0:T(8,128)S(1)}, f32[480,512]{1,0:T(8,128)S(1)}...) custom-call(s32[2]{0:T(128)S(1)} %pad_add_fusion.where_ref, bf16[2,16,16,128]{3,2,1,0:T(8,128)(2,1)S(1)} %copy-done.5, ...), custom_call_target="tpu_custom_call" | custom-call | flops 1245708288 | bytes 1048576 | tf_op jit(solution)/shard_map/first_1/pallas_call | solution.py:42
  31.5 0.7 %collective-permute-start.4 = (bf16[528,128]{1,0:T(8,128)(2,1)S(1)}, bf16[528,128]{1,0:T(8,128)(2,1)S(1)}, u32[]{:S(2)}, u32[]{:S(2)}) collective-permute-start(bf16[528,128]{1,0:T(8,128)(2,1)S(1)} %get-tuple-element.38), channel_id=1, source_target_pairs={{0,128},{1,129},{2,130},{3,131},{4,132},{5,133},{6,134},{7,135},{8... | collective-permute-start | bytes 405512 | tf_op jit(solution)/shard_map/ppermute | solution.py:293
  32.2 0.0 collective-permute-done.7.x_ref
  32.2 0.6 layer_1_0.1
  32.7 0.7 %collective-permute-start.8 = (bf16[480,128]{1,0:T(8,128)(2,1)S(1)}, bf16[480,128]{1,0:T(8,128)(2,1)S(1)}, u32[]{:S(2)}, u32[]{:S(2)}) collective-permute-start(bf16[480,128]{1,0:T(8,128)(2,1)S(1)} %get-tuple-element.48), channel_id=1, source_target_pairs={{128,256},{129,257},{130,258},{131,259},{132,260},{133,261},{134,2... | collective-permute-start | bytes 368648 | tf_op jit(solution)/shard_map/ppermute | solution.py:311
  33.4 0.0 collective-permute-done.4.x_ref
  33.4 0.6 layer_1_1.1
  34.0 0.7 %collective-permute-start.5 = (bf16[480,128]{1,0:T(8,128)(2,1)S(1)}, bf16[480,128]{1,0:T(8,128)(2,1)S(1)}, u32[]{:S(2)}, u32[]{:S(2)}) collective-permute-start(bf16[480,128]{1,0:T(8,128)(2,1)S(1)} %get-tuple-element.42), channel_id=1, source_target_pairs={{128,256},{129,257},{130,258},{131,259},{132,260},{133,261},{134,2... | collective-permute-start | bytes 368648 | tf_op jit(solution)/shard_map/ppermute | solution.py:311
  34.7 0.0 collective-permute-done.8.x_ref
  34.7 0.6 layer_2_0.1
  35.2 1.3 %collective-permute-start.9 = (bf16[432,128]{1,0:T(8,128)(2,1)S(1)}, bf16[432,128]{1,0:T(8,128)(2,1)S(1)}, u32[]{:S(2)}, u32[]{:S(2)}) collective-permute-start(bf16[432,128]{1,0:T(8,128)(2,1)S(1)} %get-tuple-element.49), channel_id=1, source_target_pairs={{256,384},{257,385},{258,386},{259,387},{260,388},{261,389},{262,3... | collective-permute-start | bytes 331784 | tf_op jit(solution)/shard_map/ppermute | solution.py:311
  36.5 0.0 collective-permute-done.5.x_ref
  36.5 0.6 layer_2_1.1
  37.1 1.3 %collective-permute-start.6 = (bf16[432,128]{1,0:T(8,128)(2,1)S(1)}, bf16[432,128]{1,0:T(8,128)(2,1)S(1)}, u32[]{:S(2)}, u32[]{:S(2)}) collective-permute-start(bf16[432,128]{1,0:T(8,128)(2,1)S(1)} %get-tuple-element.43), channel_id=1, source_target_pairs={{256,384},{257,385},{258,386},{259,387},{260,388},{261,389},{262,3... | collective-permute-start | bytes 331784 | tf_op jit(solution)/shard_map/ppermute | solution.py:311
  38.4 0.6 %store.1 = (bf16[1,2,16,16,128]{4,3,2,1,0:T(8,128)(2,1)}, f32[1,2,16,16,128]{4,3,2,1,0:T(8,128)}) custom-call(s32[2]{0:T(128)S(1)} %pad_add_fusion.where_ref, bf16[16,16,128]{2,1,0:T(8,128)(2,1)S(1)} %get-tuple-element.50.rest_0_, f32[16,16,128]{2,1,0:T(8,128)S(1)} %get-tuple-element.51.rest_1_, bf16[16,16,128]{2,1,0:T(8,128)(2,1)S(1)} %get-tuple-element.52.rest_2_, ...), custom_call_target="tpu_custom_call" | custom-call | bytes 1048576 | tf_op jit(solution)/shard_map/store/pallas_call | solution.py:42
  39.0 10.9 %collective-permute-done.9.x_ref = bf16[432,128]{1,0:T(8,128)(2,1)S(1)} collective-permute-done((bf16[432,128]{1,0:T(8,128)(2,1)S(1)}, bf16[432,128]{1,0:T(8,128)(2,1)S(1)}, u32[]{:S(2)}, u32[]{:S(2)}) %collective-permute-start.9) | collective-permute-done | bytes 110624 | tf_op jit(solution)/shard_map/ppermute | solution.py:311
  49.9 2.0 %layer_3_0.1 = (bf16[1,2,16,16,128]{4,3,2,1,0:T(8,128)(2,1)}, f32[1,2,16,16,128]{4,3,2,1,0:T(8,128)}) custom-call(s32[2]{0:T(128)S(1)} %pad_add_fusion.where_ref, bf16[432,128]{1,0:T(8,128)(2,1)S(1)} %collective-permute-done.9.x_ref, f32[480,512]{1,0:T(8,128)S(1)} %get-tuple-element.45.part_ref, ...), custom_call_target="tpu_custom_call", output_to_operand_aliasing={{0}: (6, {}), {1}: (7, {})} | custom-call | flops 452984832 | bytes 1048576 | tf_op jit(solution)/shard_map/layer_3_0/pallas_call | solution.py:42
  51.9 1.5 %collective-permute-done.6.x_ref = bf16[432,128]{1,0:T(8,128)(2,1)S(1)} collective-permute-done((bf16[432,128]{1,0:T(8,128)(2,1)S(1)}, bf16[432,128]{1,0:T(8,128)(2,1)S(1)}, u32[]{:S(2)}, u32[]{:S(2)}) %collective-permute-start.6) | collective-permute-done | bytes 110624 | tf_op jit(solution)/shard_map/ppermute | solution.py:311
  53.4 2.0 %layer_3_1.1 = (bf16[1,2,16,16,128]{4,3,2,1,0:T(8,128)(2,1)}, f32[1,2,16,16,128]{4,3,2,1,0:T(8,128)}) custom-call(s32[2]{0:T(128)S(1)} %pad_add_fusion.where_ref, bf16[432,128]{1,0:T(8,128)(2,1)S(1)} %collective-permute-done.6.x_ref, f32[480,512]{1,0:T(8,128)S(1)} %get-tuple-element.39.part_ref, ...), custom_call_target="tpu_custom_call", output_to_operand_aliasing={{0}: (6, {}), {1}: (7, {})} | custom-call | flops 452984832 | bytes 1048576 | tf_op jit(solution)/shard_map/layer_3_1/pallas_call | solution.py:42
  (11 shorter events, 0.0 us)
Async XLA Ops:
  0.6 25.9 %copy-start.10 = (f32[1,512]{1,0:T(1,128)S(1)}, f32[1,512]{1,0:T(1,128)}, u32[]{:S(2)}) copy-start(f32[1,512]{1,0:T(1,128)} %b_ref.3) | copy-start | bytes 6148
  0.6 1.0 %copy-start = (f32[1,2,16,16,128]{4,3,2,1,0:T(8,128)S(1)}, f32[1,2,16,16,128]{4,3,2,1,0:T(8,128)}, u32[]{:S(2)}) copy-start(f32[1,2,16,16,128]{4,3,2,1,0:T(8,128)} %param.7) | copy-start | bytes 786436
  1.6 0.9 %copy-start.3 = (bf16[2,16,16,128]{3,2,1,0:T(8,128)(2,1)S(1)}, bf16[2,16,16,128]{3,2,1,0:T(8,128)(2,1)}, u32[]{:S(2)}) copy-start(bf16[2,16,16,128]{3,2,1,0:T(8,128)(2,1)} %lat_ref.7) | copy-start | bytes 393220
  2.5 0.9 %copy-start.6 = (bf16[1,2,16,16,128]{4,3,2,1,0:T(8,128)(2,1)S(1)}, bf16[1,2,16,16,128]{4,3,2,1,0:T(8,128)(2,1)}, u32[]{:S(2)}) copy-start(bf16[1,2,16,16,128]{4,3,2,1,0:T(8,128)(2,1)} %param.6) | copy-start | bytes 393220
  3.4 23.1 %copy-start.2 = (f32[1,2,16,16,128]{4,3,2,1,0:T(8,128)S(1)}, f32[1,2,16,16,128]{4,3,2,1,0:T(8,128)}, u32[]{:S(2)}) copy-start(f32[1,2,16,16,128]{4,3,2,1,0:T(8,128)} %param.7) | copy-start | bytes 786436
  3.4 23.1 %copy-start.5 = (bf16[2,16,16,128]{3,2,1,0:T(8,128)(2,1)S(1)}, bf16[2,16,16,128]{3,2,1,0:T(8,128)(2,1)}, u32[]{:S(2)}) copy-start(bf16[2,16,16,128]{3,2,1,0:T(8,128)(2,1)} %lat_ref.7) | copy-start | bytes 393220
  3.4 23.1 %copy-start.8 = (bf16[1,2,16,16,128]{4,3,2,1,0:T(8,128)(2,1)S(1)}, bf16[1,2,16,16,128]{4,3,2,1,0:T(8,128)(2,1)}, u32[]{:S(2)}) copy-start(bf16[1,2,16,16,128]{4,3,2,1,0:T(8,128)(2,1)} %param.6) | copy-start | bytes 393220
  3.5 7.4 %collective-permute-start = (bf16[128,384]{1,0:T(8,128)(2,1)S(1)}, bf16[128,384]{1,0:T(8,128)(2,1)S(1)}, u32[]{:S(2)}, u32[]{:S(2)}) collective-permute-start(bf16[128,384]{1,0:T(8,128)(2,1)S(1)} %get-tuple-element.34), channel_id=1, source_target_pairs={{0,1},{1,2},{2,3},{3,4},{4,5},{5,6},{6,7},{7,8},{8,9},{9,10},{10,1... | collective-permute-start | bytes 294920 | tf_op jit(solution)/shard_map/ppermute | solution.py:256
  8.7 7.7 %collective-permute-start.1 = (bf16[128,384]{1,0:T(8,128)(2,1)S(1)}, bf16[128,384]{1,0:T(8,128)(2,1)S(1)}, u32[]{:S(2)}, u32[]{:S(2)}) collective-permute-start(bf16[128,384]{1,0:T(8,128)(2,1)S(1)} %get-tuple-element.35), channel_id=1, source_target_pairs={{1,0},{2,1},{3,2},{4,3},{5,4},{6,5},{7,6},{8,7},{9,8},{10,9},{11,1... | collective-permute-start | bytes 294920 | tf_op jit(solution)/shard_map/ppermute | solution.py:257
  16.4 1.0 %copy-start.1 = (f32[1,2,16,16,128]{4,3,2,1,0:T(8,128)S(1)}, f32[1,2,16,16,128]{4,3,2,1,0:T(8,128)}, u32[]{:S(2)}) copy-start(f32[1,2,16,16,128]{4,3,2,1,0:T(8,128)} %param.7) | copy-start | bytes 786436
  17.4 0.9 %copy-start.4 = (bf16[2,16,16,128]{3,2,1,0:T(8,128)(2,1)S(1)}, bf16[2,16,16,128]{3,2,1,0:T(8,128)(2,1)}, u32[]{:S(2)}) copy-start(bf16[2,16,16,128]{3,2,1,0:T(8,128)(2,1)} %lat_ref.7) | copy-start | bytes 393220
  18.3 0.9 %copy-start.7 = (bf16[1,2,16,16,128]{4,3,2,1,0:T(8,128)(2,1)S(1)}, bf16[1,2,16,16,128]{4,3,2,1,0:T(8,128)(2,1)}, u32[]{:S(2)}) copy-start(bf16[1,2,16,16,128]{4,3,2,1,0:T(8,128)(2,1)} %param.6) | copy-start | bytes 393220
  19.8 5.7 %collective-permute-start.2 = (bf16[208,384]{1,0:T(8,128)(2,1)S(1)}, bf16[208,384]{1,0:T(8,128)(2,1)S(1)}, u32[]{:S(2)}, u32[]{:S(2)}) collective-permute-start(bf16[208,384]{1,0:T(8,128)(2,1)S(1)} %get-tuple-element.36), channel_id=1, source_target_pairs={{16,32},{48,64},{80,96},{32,16},{64,48},{96,80},{17,33},{49,65},{8... | collective-permute-start | bytes 479240 | tf_op jit(solution)/shard_map/ppermute | solution.py:270
  20.5 5.8 %collective-permute-start.3 = (bf16[208,384]{1,0:T(8,128)(2,1)S(1)}, bf16[208,384]{1,0:T(8,128)(2,1)S(1)}, u32[]{:S(2)}, u32[]{:S(2)}) collective-permute-start(bf16[208,384]{1,0:T(8,128)(2,1)S(1)} %get-tuple-element.37), channel_id=1, source_target_pairs={{0,16},{32,48},{64,80},{96,112},{16,0},{48,32},{80,64},{112,96},{1... | collective-permute-start | bytes 479240 | tf_op jit(solution)/shard_map/ppermute | solution.py:271
  26.5 1.7 %copy-start.9 = (bf16[1,9,256,512]{3,2,1,0:T(8,128)(2,1)S(1)}, bf16[1,9,256,512]{3,2,1,0:T(8,128)(2,1)}, u32[]{:S(2)}) copy-start(bf16[1,9,256,512]{3,2,1,0:T(8,128)(2,1)} %param.8) | copy-start | bytes 7077892
  29.5 2.7 %collective-permute-start.7 = (bf16[528,128]{1,0:T(8,128)(2,1)S(1)}, bf16[528,128]{1,0:T(8,128)(2,1)S(1)}, u32[]{:S(2)}, u32[]{:S(2)}) collective-permute-start(bf16[528,128]{1,0:T(8,128)(2,1)S(1)} %get-tuple-element.44), channel_id=1, source_target_pairs={{0,128},{1,129},{2,130},{3,131},{4,132},{5,133},{6,134},{7,135},{8... | collective-permute-start | bytes 405512 | tf_op jit(solution)/shard_map/ppermute | solution.py:293
  31.5 1.9 %collective-permute-start.4 = (bf16[528,128]{1,0:T(8,128)(2,1)S(1)}, bf16[528,128]{1,0:T(8,128)(2,1)S(1)}, u32[]{:S(2)}, u32[]{:S(2)}) collective-permute-start(bf16[528,128]{1,0:T(8,128)(2,1)S(1)} %get-tuple-element.38), channel_id=1, source_target_pairs={{0,128},{1,129},{2,130},{3,131},{4,132},{5,133},{6,134},{7,135},{8... | collective-permute-start | bytes 405512 | tf_op jit(solution)/shard_map/ppermute | solution.py:293
  32.7 1.9 %collective-permute-start.8 = (bf16[480,128]{1,0:T(8,128)(2,1)S(1)}, bf16[480,128]{1,0:T(8,128)(2,1)S(1)}, u32[]{:S(2)}, u32[]{:S(2)}) collective-permute-start(bf16[480,128]{1,0:T(8,128)(2,1)S(1)} %get-tuple-element.48), channel_id=1, source_target_pairs={{128,256},{129,257},{130,258},{131,259},{132,260},{133,261},{134,2... | collective-permute-start | bytes 368648 | tf_op jit(solution)/shard_map/ppermute | solution.py:311
  34.0 2.5 %collective-permute-start.5 = (bf16[480,128]{1,0:T(8,128)(2,1)S(1)}, bf16[480,128]{1,0:T(8,128)(2,1)S(1)}, u32[]{:S(2)}, u32[]{:S(2)}) collective-permute-start(bf16[480,128]{1,0:T(8,128)(2,1)S(1)} %get-tuple-element.42), channel_id=1, source_target_pairs={{128,256},{129,257},{130,258},{131,259},{132,260},{133,261},{134,2... | collective-permute-start | bytes 368648 | tf_op jit(solution)/shard_map/ppermute | solution.py:311
  35.2 14.7 %collective-permute-start.9 = (bf16[432,128]{1,0:T(8,128)(2,1)S(1)}, bf16[432,128]{1,0:T(8,128)(2,1)S(1)}, u32[]{:S(2)}, u32[]{:S(2)}) collective-permute-start(bf16[432,128]{1,0:T(8,128)(2,1)S(1)} %get-tuple-element.49), channel_id=1, source_target_pairs={{256,384},{257,385},{258,386},{259,387},{260,388},{261,389},{262,3... | collective-permute-start | bytes 331784 | tf_op jit(solution)/shard_map/ppermute | solution.py:311
  37.1 16.3 %collective-permute-start.6 = (bf16[432,128]{1,0:T(8,128)(2,1)S(1)}, bf16[432,128]{1,0:T(8,128)(2,1)S(1)}, u32[]{:S(2)}, u32[]{:S(2)}) collective-permute-start(bf16[432,128]{1,0:T(8,128)(2,1)S(1)} %get-tuple-element.43), channel_id=1, source_target_pairs={{256,384},{257,385},{258,386},{259,387},{260,388},{261,389},{262,3... | collective-permute-start | bytes 331784 | tf_op jit(solution)/shard_map/ppermute | solution.py:311

commit v3 on v2

--- a/solution.py
+++ b/solution.py
@@ -13,7 +13,6 @@
 LAYERS = 4
 WIDE = 4
 VMEM = pl.BlockSpec(memory_space=pltpu.VMEM)
-SMEM = pl.BlockSpec(memory_space=pltpu.SMEM)
 ANY = pl.BlockSpec(memory_space=pl.ANY)
 
 
@@ -52,21 +51,60 @@
     )(*ins)
 
 
-def pack_kernel(lat_ref, hid_ref, cell_ref, low_ref, high_ref):
+def pack_kernel(lat_hbm, hid_hbm, cell_hbm, lat_ref, hid_ref, cell_ref, far_ref, near_ref, sems):
+    odd = lax.axis_index("col") % 2 == 1
+    copies = [
+        pltpu.make_async_copy(src, dst, sems.at[k])
+        for k, (src, dst) in enumerate(((lat_hbm, lat_ref), (hid_hbm, hid_ref), (cell_hbm, cell_ref)))
+    ]
+    for copy in copies:
+        copy.start()
     for k, ref in enumerate((lat_ref, hid_ref, cell_ref)):
+        copies[k].wait()
         first, second = ref[0].astype(F32), ref[1].astype(F32)
         tile = first.shape[0]
         top = top_half((tile, 8, CH))
         lanes = slice(k * CH, (k + 1) * CH)
         low = jnp.where(top, first[:, :8], swap_halves(second[:, :8]))
         high = jnp.where(top, swap_halves(first[:, 8:]), second[:, 8:])
-        low_ref[:, lanes] = low.reshape(tile * 8, CH).astype(BF16)
-        high_ref[:, lanes] = high.reshape(tile * 8, CH).astype(BF16)
-
-
-def middle(own, left, right, batch):
+        low, high = (v.reshape(tile * 8, CH).astype(BF16) for v in (low, high))
+
+        @pl.when(odd)
+        def _():
+            far_ref[:, lanes] = high
+            near_ref[:, lanes] = low
+
+        @pl.when(jnp.logical_not(odd))
+        def _():
+            far_ref[:, lanes] = low
+            near_ref[:, lanes] = high
+
+
+def load_kernel(tile, _, w_hbm, b_hbm, w_ref, b_ref, win_ref, m_ref, sems):
+    copies = [pltpu.make_async_copy(w_hbm, w_ref, sems.at[0]), pltpu.make_async_copy(b_hbm, b_ref, sems.at[1])]
+    for copy in copies:
+        copy.start()
+    edge = 3 - lax.axis_index("section")
+    shape = (tile + 6, tile + 8, CH)
+    r = lax.axis_index("row") * tile - edge + lax.broadcasted_iota(jnp.int32, shape, 0)
+    c = lax.axis_index("col") * tile - edge + lax.broadcasted_iota(jnp.int32, shape, 1)
+    high, wide = lax.axis_size("row") * tile, lax.axis_size("col") * tile
+    inside = (r >= 0) & (r < high) & (c >= 0) & (c < wide)
+    m_ref[...] = jnp.where(inside, jnp.ones(shape, F32), jnp.zeros(shape, F32)).reshape(-1, CH)
+    for copy in copies:
+        copy.wait()
+
+    @pl.when(lax.axis_index("section") > 0)
+    def _():
+        for t in range(9):
+            win_ref[t * CH : (t + 1) * CH, :] = w_ref[2 * t * CH : (2 * t + 1) * CH, :]
+
+
+def middle(own, far, near, batch):
     tile = own.shape[0]
-    left, right = (v.astype(F32).reshape(tile, 8, CH) for v in (left, right))
+    far, near = (v.astype(F32).reshape(tile, 8, CH) for v in (far, near))
+    odd = lax.axis_index("col") % 2 == 1
+    left, right = jnp.where(odd, near, far), jnp.where(odd, far, near)
     if batch == 0:
         left = swap_halves(left)
     else:
@@ -78,8 +116,8 @@
     return jnp.concatenate([left[0], rows], axis=0)
 
 
-def middle_kernel(where_ref, lat_ref, hid_ref, cell_ref, left_ref, right_ref, far_ref, near_ref):
-    odd = where_ref[1] == 1
+def middle_kernel(lat_ref, hid_ref, cell_ref, left_ref, right_ref, _, far_ref, near_ref):
+    odd = lax.axis_index("row") % 2 == 1
     for batch in range(2):
         for k, ref in enumerate((lat_ref, hid_ref, cell_ref)):
             lanes = slice(k * CH, (k + 1) * CH)
@@ -116,12 +154,12 @@
     return rolled(v, edge)[edge * stride : (edge + tile) * stride].reshape(tile, stride, CH)[:, :tile]
 
 
-def first_kernel(batch, blocks, where_ref, lat_ref, hid_ref, cell_ref, left_ref, right_ref, far_ref, near_ref,
-                 w_ref, b_ref, m_ref, send_ref, htile_ref, ctile_ref, part_ref, prev_ref, win_ref, cols):
+def first_kernel(batch, blocks, lat_ref, hid_ref, cell_ref, left_ref, right_ref, far_ref, near_ref,
+                 w_ref, b_ref, m_ref, send_ref, htile_ref, ctile_ref, part_ref, prev_ref, cols):
     tile = lat_ref.shape[1]
     stride = tile + 8
-    sec = where_ref[0]
-    odd = where_ref[1] == 1
+    sec = lax.axis_index("section")
+    odd = lax.axis_index("row") % 2 == 1
 
     def full(k, ref):
         lanes = slice(k * CH, (k + 1) * CH)
@@ -167,11 +205,9 @@
             part_ref[:rows, :] = (
                 jnp.dot(cols[:rows, : 9 * CH], own, preferred_element_type=F32) + b_ref[...]
             )
-            for t in range(9):
-                win_ref[t * CH : (t + 1) * CH, :] = w_ref[2 * t * CH : (2 * t + 1) * CH, :]
-
-
-def next_kernel(tick, blocks, where_ref, x_ref, part_ref, prev_ref, win_ref, m_ref, *rest):
+
+
+def next_kernel(tick, blocks, x_ref, part_ref, prev_ref, win_ref, m_ref, *rest):
     last = tick == LAYERS - 1
     if last:
         batch, (_, _, hout_ref, cout_ref, cols, htile_ref, ctile_ref, sems) = rest[0], rest[1:]
@@ -182,7 +218,7 @@
     edge = 3 - tick
     rows = (tile + 2 * edge) * stride
 
-    @pl.when(where_ref[0] == tick)
+    @pl.when(lax.axis_index("section") == tick)
     def _():
         taps(x_ref[...].astype(F32), 0, cols, rows, stride, CH, 0)
         size = rows // blocks
@@ -209,15 +245,15 @@
                 copy.wait()
 
 
-def last_kernel(batch, blocks, where_ref, x_ref, part_ref, prev_ref, win_ref, m_ref, *rest):
-    next_kernel(LAYERS - 1, blocks, where_ref, x_ref, part_ref, prev_ref, win_ref, m_ref, batch, *rest)
-
-
-def store_kernel(where_ref, *rest):
+def last_kernel(batch, blocks, x_ref, part_ref, prev_ref, win_ref, m_ref, *rest):
+    next_kernel(LAYERS - 1, blocks, x_ref, part_ref, prev_ref, win_ref, m_ref, batch, *rest)
+
+
+def store_kernel(*rest):
     tiles, (hout_ref, cout_ref, sems) = rest[:-3], rest[-3:]
     for tick in range(LAYERS - 1):
 
-        @pl.when(where_ref[0] == tick)
+        @pl.when(lax.axis_index("section") == tick)
         def _():
             copies = []
             for batch in range(2):
@@ -233,59 +269,64 @@
 def on_device(latent, hidden_old, cell_old, weights, bias):
     tile = latent.shape[1]
     stride = tile + 8
-    sec = lax.axis_index("section")
-    row = lax.axis_index("row")
-    col = lax.axis_index("col")
     n_row, n_col = lax.axis_size("row"), lax.axis_size("col")
+    stay = lambda v: pltpu.with_memory_space_constraint(v, pltpu.HBM)
     hid = hidden_old[0]
     cell = cell_old[0]
     w = weights.reshape(-1, weights.shape[-1])
-    where = jnp.stack([sec, row % 2]).astype(jnp.int32)
-
-    edge = 3 - sec
-    r = row * tile - edge + lax.broadcasted_iota(jnp.int32, (tile + 6, stride, CH), 0)
-    c = col * tile - edge + lax.broadcasted_iota(jnp.int32, (tile + 6, stride, CH), 1)
-    inside = (r >= 0) & (r < n_row * tile) & (c >= 0) & (c < n_col * tile)
-    mask = inside.astype(F32).reshape(-1, CH)
 
     vm = lambda shape, kind: pltpu.VMEM(shape, kind)
-    low, high = call(
-        pack_kernel, (latent, hid, cell), [VMEM] * 3, [vm((8 * tile, 3 * CH), BF16)] * 2, [VMEM] * 2, name="pack"
-    )
-    up = [(i, i + 1) for i in range(n_col - 1)]
-    left = lax.ppermute(high, "col", up)
-    right = lax.ppermute(low, "col", [(j, i) for i, j in up])
+    odd = lambda n: [(i, i + 1) for i in range(1, n - 1, 2)]
+    even = lambda n: [(i, i + 1) for i in range(0, n - 1, 2)]
+    both = lambda pairs: pairs + [(j, i) for i, j in pairs]
+    lat, hid, cell, left, right = call(
+        pack_kernel,
+        (stay(latent), stay(hid), stay(cell)),
+        [ANY] * 3,
+        [vm(latent.shape, BF16), vm(hid.shape, BF16), vm(cell.shape, F32)] + [vm((8 * tile, 3 * CH), BF16)] * 2,
+        [VMEM] * 5,
+        [pltpu.SemaphoreType.DMA((3,))],
+        name="pack",
+    )
+    w, b, win, mask = call(
+        functools.partial(load_kernel, tile),
+        (right, stay(w), stay(bias)),
+        [VMEM, ANY, ANY],
+        [vm(w.shape, BF16), vm(bias.shape, F32), vm((9 * CH, 4 * CH), BF16), vm(((tile + 6) * stride, CH), F32)],
+        [VMEM] * 4,
+        [pltpu.SemaphoreType.DMA((2,))],
+        name="load",
+        flops=1 << 31,
+    )
+    left = lax.ppermute(left, "col", both(odd(n_col)))
+    right = lax.ppermute(right, "col", both(even(n_col)))
 
     far, near = call(
         middle_kernel,
-        (where, latent, hid, cell, left, right),
-        [SMEM] + [VMEM] * 5,
+        (lat, hid, cell, left, right, b),
+        [VMEM] * 6,
         [vm((208, 3 * CH), BF16)] * 2,
         [VMEM] * 2,
         name="middle",
     )
-    odd = [(i, i + 1) for i in range(1, n_row - 1, 2)]
-    even = [(i, i + 1) for i in range(0, n_row - 1, 2)]
-    both = lambda pairs: pairs + [(j, i) for i, j in pairs]
-    far = lax.ppermute(far, "row", both(odd))
-    near = lax.ppermute(near, "row", both(even))
+    far = lax.ppermute(far, "row", both(odd(n_row)))
+    near = lax.ppermute(near, "row", both(even(n_row)))
 
     most = (tile + 4) * stride
     xs, state, tiles = [], [], []
     for batch in range(2):
-        send, htile, ctile, part, prev, win = call(
+        send, htile, ctile, part, prev = call(
             functools.partial(first_kernel, batch, 3),
-            (where, latent, hid, cell, left, right, far, near, w, bias, mask),
-            [SMEM] + [VMEM] * 10,
+            (lat, hid, cell, left, right, far, near, w, b, mask),
+            [VMEM] * 10,
             [
                 vm(((tile + 6) * stride, CH), BF16),
                 vm((tile, tile, CH), BF16),
                 vm((tile, tile, CH), F32),
                 vm((most, 4 * CH), F32),
                 vm((most, CH), F32),
-                vm((9 * CH, 4 * CH), BF16),
             ],
-            [VMEM] * 6,
+            [VMEM] * 5,
             [pltpu.VMEM(((tile + 6) * stride, 18 * CH), BF16)],
             name=f"first_{batch}",
             flops=2 * 528 * 2304 * 512,
@@ -300,8 +341,8 @@
         for batch in range(2):
             send, htile, ctile = call(
                 functools.partial(next_kernel, tick, 3),
-                (where, xs[batch], *state[batch], mask),
-                [SMEM] + [VMEM] * 5,
+                (xs[batch], *state[batch], mask),
+                [VMEM] * 5,
                 [vm((rows, CH), BF16), vm((tile, tile, CH), BF16), vm((tile, tile, CH), F32)],
                 [VMEM] * 3,
                 [pltpu.VMEM((rows, 9 * CH), BF16)],
@@ -318,8 +359,8 @@
     ]
     outs = call(
         store_kernel,
-        (where, *tiles),
-        [SMEM] + [VMEM] * len(tiles),
+        (*tiles,),
+        [VMEM] * len(tiles),
         out_shapes,
         [ANY, ANY],
         [pltpu.SemaphoreType.DMA((4,))],
@@ -329,8 +370,8 @@
         rows = tile * stride
         outs = call(
             functools.partial(last_kernel, batch, 3),
-            (where, xs[batch], *state[batch], mask, *outs),
-            [SMEM] + [VMEM] * 5 + [ANY] * 2,
+            (xs[batch], *state[batch], mask, *outs),
+            [VMEM] * 5 + [ANY] * 2,
             out_shapes,
             [ANY, ANY],
             [
@@ -339,7 +380,7 @@
                 pltpu.VMEM((tile, tile, CH), F32),
                 pltpu.SemaphoreType.DMA((2,)),
             ],
-            aliases={6: 0, 7: 1},
+            aliases={5: 0, 6: 1},
             name=f"layer_3_{batch}",
             flops=2 * rows * 1152 * 512,
         )

time: 55.9 us -> 44.9 us (0.80)
  the two profiles are of different devices: /device:TPU:230 before, /device:TPU:254 now
where the time goes in v3:
time: 44.9 us; the launch traced here: 44.5 us
  waiting for transfers between devices  20.2 us (45%)
  starting transfers between devices  16.1 us (36%)
  Pallas kernels  7.47 us (17%)
  between operations  0.83 us (2%)
    ppermute x4, waiting for transfers between devices, on_device(): nxt.append(lax.ppermute(send, 'section', [(tick, tick + 1)]))  14.6 us
    pallas_call x12, Pallas kernels, call(): pl.pallas_call(kernel, out_shape=tuple(outs), in_specs=in_specs, out_spec...  7.47 us
    ppermute x1, starting transfers between devices, on_device(): left = lax.ppermute(left, 'col', both(odd(n_col)))  5.04 us
    ppermute x4, starting transfers between devices, on_device(): nxt.append(lax.ppermute(send, 'section', [(tick, tick + 1)]))  3.92 us
    ppermute x1, waiting for transfers between devices, on_device(): right = lax.ppermute(right, 'col', both(even(n_col)))  2.8 us
    ppermute x1, waiting for transfers between devices, on_device(): far = lax.ppermute(far, 'row', both(odd(n_row)))  2.74 us
    ppermute x1, starting transfers between devices, on_device(): right = lax.ppermute(right, 'col', both(even(n_col)))  1.92 us
    ppermute x1, starting transfers between devices, on_device(): far = lax.ppermute(far, 'row', both(odd(n_row)))  1.92 us
  transfers between devices with their start and end apart: 10, of which 4 were waited for; matrix products, arithmetic and copies ran while one was open for 0% of the time, Pallas kernels for 9%

profile of v3, /device:TPU:254, one launch (start us, length us, event | category | flops | bytes accessed | tf_op | source)
XLA Modules:
  0.0 44.5 jit_solution(18230226641476608278)
XLA Ops:
  0.6 1.1 %pack.1 = (bf16[2,16,16,128]{3,2,1,0:T(8,128)(2,1)S(1)}, bf16[2,16,16,128]{3,2,1,0:T(8,128)(2,1)S(1)}, f32[2,16,16,128]{3,2,1,0:T(8,128)S(1)}, bf16[128,384]{1,0:T(8,128)(2,1)S(1)}, bf16[128,384]{1,0:T(8,128)(2,1)S(1)}) custom-call(bf16[2,16,16,128]{3,2,1,0:T(8,128)(2,1)} %lat_hbm.1, bf16[2,16,16,128]{3,2,1,0:T(8,128)(2,1)} %bitcast.4, ...), custom_call_target="tpu_custom_call" | custom-call | bytes 1048576 | tf_op jit(solution)/shard_map/pack/pallas_call | solution.py:41
  1.8 5.0 %collective-permute-start = (bf16[128,384]{1,0:T(8,128)(2,1)S(1)}, bf16[128,384]{1,0:T(8,128)(2,1)S(1)}, u32[]{:S(2)}, u32[]{:S(2)}) collective-permute-start(bf16[128,384]{1,0:T(8,128)(2,1)S(1)} %get-tuple-element.42), channel_id=1, source_target_pairs={{1,2},{3,4},{5,6},{7,8},{9,10},{11,12},{13,14},{2,1},{4,3},{6,5},{... | collective-permute-start | bytes 294920 | tf_op jit(solution)/shard_map/ppermute | solution.py:301
  6.8 1.9 %collective-permute-start.1 = (bf16[128,384]{1,0:T(8,128)(2,1)S(1)}, bf16[128,384]{1,0:T(8,128)(2,1)S(1)}, u32[]{:S(2)}, u32[]{:S(2)}) collective-permute-start(bf16[128,384]{1,0:T(8,128)(2,1)S(1)} %get-tuple-element.43._), channel_id=1, source_target_pairs={{0,1},{2,3},{4,5},{6,7},{8,9},{10,11},{12,13},{14,15},{1,0},{3,2},... | collective-permute-start | bytes 294920 | tf_op jit(solution)/shard_map/ppermute | solution.py:302
  8.8 1.8 %load.1 = (bf16[2304,512]{1,0:T(8,128)(2,1)S(1)}, f32[1,512]{1,0:T(1,128)S(1)}, bf16[1152,512]{1,0:T(8,128)(2,1)S(1)}, f32[528,128]{1,0:T(8,128)S(1)}) custom-call(bf16[128,384]{1,0:T(8,128)(2,1)S(1)} %get-tuple-element.43._, bf16[2304,512]{1,0:T(8,128)(2,1)} %bitcast.5, f32[1,512]{1,0:T(1,128)} %b_hbm.1), custom_call_target="tpu_custom_call" | custom-call | flops 2147483648 | bytes 1048576 | tf_op jit(solution)/shard_map/load/pallas_call | solution.py:41
  10.5 0.0 collective-permute-done.left_ref
  10.5 2.8 %collective-permute-done.1.right_ref = bf16[128,384]{1,0:T(8,128)(2,1)S(1)} collective-permute-done((bf16[128,384]{1,0:T(8,128)(2,1)S(1)}, bf16[128,384]{1,0:T(8,128)(2,1)S(1)}, u32[]{:S(2)}, u32[]{:S(2)}) %collective-permute-start.1) | collective-permute-done | bytes 98336 | tf_op jit(solution)/shard_map/ppermute | solution.py:302
  13.3 0.1 middle.1
  13.5 1.9 %collective-permute-start.2 = (bf16[208,384]{1,0:T(8,128)(2,1)S(1)}, bf16[208,384]{1,0:T(8,128)(2,1)S(1)}, u32[]{:S(2)}, u32[]{:S(2)}) collective-permute-start(bf16[208,384]{1,0:T(8,128)(2,1)S(1)} %get-tuple-element.45), channel_id=1, source_target_pairs={{16,32},{48,64},{80,96},{32,16},{64,48},{96,80},{17,33},{49,65},{8... | collective-permute-start | bytes 479240 | tf_op jit(solution)/shard_map/ppermute | solution.py:312
  15.4 1.9 %collective-permute-start.3 = (bf16[208,384]{1,0:T(8,128)(2,1)S(1)}, bf16[208,384]{1,0:T(8,128)(2,1)S(1)}, u32[]{:S(2)}, u32[]{:S(2)}) collective-permute-start(bf16[208,384]{1,0:T(8,128)(2,1)S(1)} %get-tuple-element.46), channel_id=1, source_target_pairs={{0,16},{32,48},{64,80},{96,112},{16,0},{48,32},{80,64},{112,96},{1... | collective-permute-start | bytes 479240 | tf_op jit(solution)/shard_map/ppermute | solution.py:313
  17.3 2.7 %collective-permute-done.2.far_ref = bf16[208,384]{1,0:T(8,128)(2,1)S(1)} collective-permute-done((bf16[208,384]{1,0:T(8,128)(2,1)S(1)}, bf16[208,384]{1,0:T(8,128)(2,1)S(1)}, u32[]{:S(2)}, u32[]{:S(2)}) %collective-permute-start.2) | collective-permute-done | bytes 159776 | tf_op jit(solution)/shard_map/ppermute | solution.py:312
  20.1 0.0 collective-permute-done.3.near_ref
  20.1 0.7 %first_0.1 = (bf16[528,128]{1,0:T(8,128)(2,1)S(1)}, bf16[16,16,128]{2,1,0:T(8,128)(2,1)S(1)}, f32[16,16,128]{2,1,0:T(8,128)S(1)}, f32[480,512]{1,0:T(8,128)S(1)}, f32[480,128]{1,0:T(8,128)S(1)}) custom-call(bf16[2,16,16,128]{3,2,1,0:T(8,128)(2,1)S(1)} %get-tuple-element.39.lat_ref, bf16[2,16,16,128]{3,2,1,0:T(8,128)(2,1)S(1)} %get-tuple-element.40.hid_ref, ...), custom_call_target="tpu_custom_call" | custom-call | flops 1245708288 | bytes 1048576 | tf_op jit(solution)/shard_map/first_0/pallas_call | solution.py:41
  20.8 0.7 %collective-permute-start.7 = (bf16[528,128]{1,0:T(8,128)(2,1)S(1)}, bf16[528,128]{1,0:T(8,128)(2,1)S(1)}, u32[]{:S(2)}, u32[]{:S(2)}) collective-permute-start(bf16[528,128]{1,0:T(8,128)(2,1)S(1)} %get-tuple-element.55), channel_id=1, source_target_pairs={{0,128},{1,129},{2,130},{3,131},{4,132},{5,133},{6,134},{7,135},{8... | collective-permute-start | bytes 405512 | tf_op jit(solution)/shard_map/ppermute | solution.py:334
  21.5 0.7 %first_1.1 = (bf16[528,128]{1,0:T(8,128)(2,1)S(1)}, bf16[16,16,128]{2,1,0:T(8,128)(2,1)S(1)}, f32[16,16,128]{2,1,0:T(8,128)S(1)}, f32[480,512]{1,0:T(8,128)S(1)}, f32[480,128]{1,0:T(8,128)S(1)}) custom-call(bf16[2,16,16,128]{3,2,1,0:T(8,128)(2,1)S(1)} %get-tuple-element.39.lat_ref, bf16[2,16,16,128]{3,2,1,0:T(8,128)(2,1)S(1)} %get-tuple-element.40.hid_ref, ...), custom_call_target="tpu_custom_call" | custom-call | flops 1245708288 | bytes 1048576 | tf_op jit(solution)/shard_map/first_1/pallas_call | solution.py:41
  22.2 0.7 %collective-permute-start.4 = (bf16[528,128]{1,0:T(8,128)(2,1)S(1)}, bf16[528,128]{1,0:T(8,128)(2,1)S(1)}, u32[]{:S(2)}, u32[]{:S(2)}) collective-permute-start(bf16[528,128]{1,0:T(8,128)(2,1)S(1)} %get-tuple-element.49), channel_id=1, source_target_pairs={{0,128},{1,129},{2,130},{3,131},{4,132},{5,133},{6,134},{7,135},{8... | collective-permute-start | bytes 405512 | tf_op jit(solution)/shard_map/ppermute | solution.py:334
  22.9 0.0 collective-permute-done.7.x_ref
  23.0 0.7 %collective-permute-start.8 = (bf16[480,128]{1,0:T(8,128)(2,1)S(1)}, bf16[480,128]{1,0:T(8,128)(2,1)S(1)}, u32[]{:S(2)}, u32[]{:S(2)}) collective-permute-start(bf16[480,128]{1,0:T(8,128)(2,1)S(1)} %get-tuple-element.58), channel_id=1, source_target_pairs={{128,256},{129,257},{130,258},{131,259},{132,260},{133,261},{134,2... | collective-permute-start | bytes 368648 | tf_op jit(solution)/shard_map/ppermute | solution.py:352
  23.6 0.0 collective-permute-done.4.x_ref
  23.7 0.7 %collective-permute-start.5 = (bf16[480,128]{1,0:T(8,128)(2,1)S(1)}, bf16[480,128]{1,0:T(8,128)(2,1)S(1)}, u32[]{:S(2)}, u32[]{:S(2)}) collective-permute-start(bf16[480,128]{1,0:T(8,128)(2,1)S(1)} %get-tuple-element.53), channel_id=1, source_target_pairs={{128,256},{129,257},{130,258},{131,259},{132,260},{133,261},{134,2... | collective-permute-start | bytes 368648 | tf_op jit(solution)/shard_map/ppermute | solution.py:352
  24.3 0.0 collective-permute-done.8.x_ref
  24.4 1.3 %collective-permute-start.9 = (bf16[432,128]{1,0:T(8,128)(2,1)S(1)}, bf16[432,128]{1,0:T(8,128)(2,1)S(1)}, u32[]{:S(2)}, u32[]{:S(2)}) collective-permute-start(bf16[432,128]{1,0:T(8,128)(2,1)S(1)} %get-tuple-element.59), channel_id=1, source_target_pairs={{256,384},{257,385},{258,386},{259,387},{260,388},{261,389},{262,3... | collective-permute-start | bytes 331784 | tf_op jit(solution)/shard_map/ppermute | solution.py:352
  25.7 0.0 collective-permute-done.5.x_ref
  25.7 1.3 %collective-permute-start.6 = (bf16[432,128]{1,0:T(8,128)(2,1)S(1)}, bf16[432,128]{1,0:T(8,128)(2,1)S(1)}, u32[]{:S(2)}, u32[]{:S(2)}) collective-permute-start(bf16[432,128]{1,0:T(8,128)(2,1)S(1)} %get-tuple-element.54), channel_id=1, source_target_pairs={{256,384},{257,385},{258,386},{259,387},{260,388},{261,389},{262,3... | collective-permute-start | bytes 331784 | tf_op jit(solution)/shard_map/ppermute | solution.py:352
  27.0 0.1 store.1
  27.1 14.4 %collective-permute-done.9.x_ref = bf16[432,128]{1,0:T(8,128)(2,1)S(1)} collective-permute-done((bf16[432,128]{1,0:T(8,128)(2,1)S(1)}, bf16[432,128]{1,0:T(8,128)(2,1)S(1)}, u32[]{:S(2)}, u32[]{:S(2)}) %collective-permute-start.9) | collective-permute-done | bytes 110624 | tf_op jit(solution)/shard_map/ppermute | solution.py:352
  41.5 1.4 %layer_3_0.1 = (bf16[1,2,16,16,128]{4,3,2,1,0:T(8,128)(2,1)}, f32[1,2,16,16,128]{4,3,2,1,0:T(8,128)}) custom-call(bf16[432,128]{1,0:T(8,128)(2,1)S(1)} %collective-permute-done.9.x_ref, f32[480,512]{1,0:T(8,128)S(1)} %get-tuple-element.56.part_ref, f32[480,128]{1,0:T(8,128)S(1)} %get-tuple-element.57.prev_ref, ...), custom_call_target="tpu_custom_call", output_to_operand_aliasing={{0}: (5, {}), {1}: (6, {})} | custom-call | flops 452984832 | bytes 1048576 | tf_op jit(solution)/shard_map/layer_3_0/pallas_call | solution.py:41
  42.9 0.2 collective-permute-done.6.x_ref
  43.1 1.4 %layer_3_1.1 = (bf16[1,2,16,16,128]{4,3,2,1,0:T(8,128)(2,1)}, f32[1,2,16,16,128]{4,3,2,1,0:T(8,128)}) custom-call(bf16[432,128]{1,0:T(8,128)(2,1)S(1)} %collective-permute-done.6.x_ref, f32[480,512]{1,0:T(8,128)S(1)} %get-tuple-element.50.part_ref, f32[480,128]{1,0:T(8,128)S(1)} %get-tuple-element.51.prev_ref, ...), custom_call_target="tpu_custom_call", output_to_operand_aliasing={{0}: (5, {}), {1}: (6, {})} | custom-call | flops 452984832 | bytes 1048576 | tf_op jit(solution)/shard_map/layer_3_1/pallas_call | solution.py:41
  (4 shorter events, 0.1 us)
Async XLA Ops:
  1.8 8.7 %collective-permute-start = (bf16[128,384]{1,0:T(8,128)(2,1)S(1)}, bf16[128,384]{1,0:T(8,128)(2,1)S(1)}, u32[]{:S(2)}, u32[]{:S(2)}) collective-permute-start(bf16[128,384]{1,0:T(8,128)(2,1)S(1)} %get-tuple-element.42), channel_id=1, source_target_pairs={{1,2},{3,4},{5,6},{7,8},{9,10},{11,12},{13,14},{2,1},{4,3},{6,5},{... | collective-permute-start | bytes 294920 | tf_op jit(solution)/shard_map/ppermute | solution.py:301
  6.8 6.5 %collective-permute-start.1 = (bf16[128,384]{1,0:T(8,128)(2,1)S(1)}, bf16[128,384]{1,0:T(8,128)(2,1)S(1)}, u32[]{:S(2)}, u32[]{:S(2)}) collective-permute-start(bf16[128,384]{1,0:T(8,128)(2,1)S(1)} %get-tuple-element.43._), channel_id=1, source_target_pairs={{0,1},{2,3},{4,5},{6,7},{8,9},{10,11},{12,13},{14,15},{1,0},{3,2},... | collective-permute-start | bytes 294920 | tf_op jit(solution)/shard_map/ppermute | solution.py:302
  13.5 6.6 %collective-permute-start.2 = (bf16[208,384]{1,0:T(8,128)(2,1)S(1)}, bf16[208,384]{1,0:T(8,128)(2,1)S(1)}, u32[]{:S(2)}, u32[]{:S(2)}) collective-permute-start(bf16[208,384]{1,0:T(8,128)(2,1)S(1)} %get-tuple-element.45), channel_id=1, source_target_pairs={{16,32},{48,64},{80,96},{32,16},{64,48},{96,80},{17,33},{49,65},{8... | collective-permute-start | bytes 479240 | tf_op jit(solution)/shard_map/ppermute | solution.py:312
  15.4 4.7 %collective-permute-start.3 = (bf16[208,384]{1,0:T(8,128)(2,1)S(1)}, bf16[208,384]{1,0:T(8,128)(2,1)S(1)}, u32[]{:S(2)}, u32[]{:S(2)}) collective-permute-start(bf16[208,384]{1,0:T(8,128)(2,1)S(1)} %get-tuple-element.46), channel_id=1, source_target_pairs={{0,16},{32,48},{64,80},{96,112},{16,0},{48,32},{80,64},{112,96},{1... | collective-permute-start | bytes 479240 | tf_op jit(solution)/shard_map/ppermute | solution.py:313
  20.8 2.1 %collective-permute-start.7 = (bf16[528,128]{1,0:T(8,128)(2,1)S(1)}, bf16[528,128]{1,0:T(8,128)(2,1)S(1)}, u32[]{:S(2)}, u32[]{:S(2)}) collective-permute-start(bf16[528,128]{1,0:T(8,128)(2,1)S(1)} %get-tuple-element.55), channel_id=1, source_target_pairs={{0,128},{1,129},{2,130},{3,131},{4,132},{5,133},{6,134},{7,135},{8... | collective-permute-start | bytes 405512 | tf_op jit(solution)/shard_map/ppermute | solution.py:334
  22.2 1.4 %collective-permute-start.4 = (bf16[528,128]{1,0:T(8,128)(2,1)S(1)}, bf16[528,128]{1,0:T(8,128)(2,1)S(1)}, u32[]{:S(2)}, u32[]{:S(2)}) collective-permute-start(bf16[528,128]{1,0:T(8,128)(2,1)S(1)} %get-tuple-element.49), channel_id=1, source_target_pairs={{0,128},{1,129},{2,130},{3,131},{4,132},{5,133},{6,134},{7,135},{8... | collective-permute-start | bytes 405512 | tf_op jit(solution)/shard_map/ppermute | solution.py:334
  23.0 1.4 %collective-permute-start.8 = (bf16[480,128]{1,0:T(8,128)(2,1)S(1)}, bf16[480,128]{1,0:T(8,128)(2,1)S(1)}, u32[]{:S(2)}, u32[]{:S(2)}) collective-permute-start(bf16[480,128]{1,0:T(8,128)(2,1)S(1)} %get-tuple-element.58), channel_id=1, source_target_pairs={{128,256},{129,257},{130,258},{131,259},{132,260},{133,261},{134,2... | collective-permute-start | bytes 368648 | tf_op jit(solution)/shard_map/ppermute | solution.py:352
  23.7 2.0 %collective-permute-start.5 = (bf16[480,128]{1,0:T(8,128)(2,1)S(1)}, bf16[480,128]{1,0:T(8,128)(2,1)S(1)}, u32[]{:S(2)}, u32[]{:S(2)}) collective-permute-start(bf16[480,128]{1,0:T(8,128)(2,1)S(1)} %get-tuple-element.53), channel_id=1, source_target_pairs={{128,256},{129,257},{130,258},{131,259},{132,260},{133,261},{134,2... | collective-permute-start | bytes 368648 | tf_op jit(solution)/shard_map/ppermute | solution.py:352
  24.4 17.1 %collective-permute-start.9 = (bf16[432,128]{1,0:T(8,128)(2,1)S(1)}, bf16[432,128]{1,0:T(8,128)(2,1)S(1)}, u32[]{:S(2)}, u32[]{:S(2)}) collective-permute-start(bf16[432,128]{1,0:T(8,128)(2,1)S(1)} %get-tuple-element.59), channel_id=1, source_target_pairs={{256,384},{257,385},{258,386},{259,387},{260,388},{261,389},{262,3... | collective-permute-start | bytes 331784 | tf_op jit(solution)/shard_map/ppermute | solution.py:352
  25.7 17.4 %collective-permute-start.6 = (bf16[432,128]{1,0:T(8,128)(2,1)S(1)}, bf16[432,128]{1,0:T(8,128)(2,1)S(1)}, u32[]{:S(2)}, u32[]{:S(2)}) collective-permute-start(bf16[432,128]{1,0:T(8,128)(2,1)S(1)} %get-tuple-element.54), channel_id=1, source_target_pairs={{256,384},{257,385},{258,386},{259,387},{260,388},{261,389},{262,3... | collective-permute-start | bytes 331784 | tf_op jit(solution)/shard_map/ppermute | solution.py:352

commit v4 on v3

v4 whole, which is shorter than its diff:
```python
import functools

import jax
import jax.numpy as jnp
from jax import lax
from jax.experimental import pallas as pl
from jax.experimental.pallas import tpu as pltpu
from jax.sharding import PartitionSpec as P


F32 = jnp.float32
BF16 = jnp.bfloat16
CH = 128
LAYERS = 4
BLOCKS = 1
EDGE = 6
WIDE = 4
VMEM = pl.BlockSpec(memory_space=pltpu.VMEM)
ANY = pl.BlockSpec(memory_space=pl.ANY)


def sigmoid(x):
    return 0.5 * jnp.tanh(0.5 * x) + 0.5


def rolled(x, by):
    rows = x.shape[0]
    by = by % rows
    return x if by == 0 else pltpu.roll(x, rows - by, 0)


def swap_halves(x):
    tiles = x.shape[0]
    flat = x.reshape(tiles * 8, CH)
    up, down = pltpu.roll(flat, 4, 0), pltpu.roll(flat, tiles * 8 - 4, 0)
    return jnp.where(top_half(flat.shape), down, up).reshape(x.shape)


def top_half(shape):
    return lax.broadcasted_iota(jnp.int32, shape, len(shape) - 2) % 8 < 4


def call(kernel, ins, in_specs, outs, out_specs, scratch=(), aliases=None, flops=0, limit=16, after=None):
    body = kernel
    if after is not None:
        ins, in_specs = (*ins, after), [*in_specs, VMEM]
        body = lambda *refs: kernel(*refs[: len(ins) - 1], *refs[len(ins) :])
    return pl.pallas_call(
        body,
        out_shape=tuple(outs),
        in_specs=in_specs,
        out_specs=tuple(out_specs),
        scratch_shapes=list(scratch),
        input_output_aliases=aliases or {},
        compiler_params=pltpu.CompilerParams(vmem_limit_bytes=limit << 20),
        cost_estimate=pl.CostEstimate(flops=flops, bytes_accessed=1 << 20, transcendentals=0),
    )(*ins)


def pack_kernel(lat_hbm, hid_hbm, cell_hbm, lat_ref, hid_ref, cell_ref, far_ref, near_ref, sems):
    odd = lax.axis_index("col") % 2 == 1
    copies = [
        pltpu.make_async_copy(src, dst, sems.at[k])
        for k, (src, dst) in enumerate(((lat_hbm, lat_ref), (hid_hbm, hid_ref), (cell_hbm, cell_ref)))
    ]
    for copy in copies:
        copy.start()
    for k, ref in enumerate((lat_ref, hid_ref, cell_ref)):
        copies[k].wait()
        first, second = ref[0].astype(F32), ref[1].astype(F32)
        tile = first.shape[0]
        top = top_half((tile, 8, CH))
        lanes = slice(k * CH, (k + 1) * CH)
        low = jnp.where(top, first[:, :8], swap_halves(second[:, :8]))
        high = jnp.where(top, swap_halves(first[:, 8:]), second[:, 8:])
        low, high = (v.reshape(tile * 8, CH).astype(BF16) for v in (low, high))

        @pl.when(odd)
        def _():
            far_ref[:, lanes] = high
            near_ref[:, lanes] = low

        @pl.when(jnp.logical_not(odd))
        def _():
            far_ref[:, lanes] = low
            near_ref[:, lanes] = high


def load_kernel(tile, _, w_hbm, b_hbm, w_ref, b_ref, win_ref, m_ref, sems):
    copies = [pltpu.make_async_copy(w_hbm, w_ref, sems.at[0]), pltpu.make_async_copy(b_hbm, b_ref, sems.at[1])]
    for copy in copies:
        copy.start()
    edge = 3 - lax.axis_index("section")
    shape = (tile + 6, tile + 8, CH)
    r = lax.axis_index("row") * tile - edge + lax.broadcasted_iota(jnp.int32, shape, 0)
    c = lax.axis_index("col") * tile - edge + lax.broadcasted_iota(jnp.int32, shape, 1)
    high, wide = lax.axis_size("row") * tile, lax.axis_size("col") * tile
    inside = (r >= 0) & (r < high) & (c >= 0) & (c < wide)
    m_ref[...] = jnp.where(inside, jnp.ones(shape, F32), jnp.zeros(shape, F32)).reshape(-1, CH)
    for copy in copies:
        copy.wait()

    @pl.when(lax.axis_index("section") > 0)
    def _():
        for t in range(9):
            win_ref[t * CH : (t + 1) * CH, :] = w_ref[2 * t * CH : (2 * t + 1) * CH, :]


def middle(own, far, near, batch):
    tile = own.shape[0]
    far, near = (v.astype(F32).reshape(tile, 8, CH) for v in (far, near))
    odd = lax.axis_index("col") % 2 == 1
    left, right = jnp.where(odd, near, far), jnp.where(odd, far, near)
    if batch == 0:
        left = swap_halves(left)
    else:
        right = swap_halves(right)
    top = top_half((tile, 8, CH))
    zero = jnp.zeros((1, 8, CH), F32)
    side = jnp.where(top, right, jnp.concatenate([left[1:], zero], axis=0))
    rows = jnp.concatenate([own, side], axis=1).reshape(tile * (tile + 8), CH)
    return jnp.concatenate([left[0], rows], axis=0)


def middle_kernel(lat_ref, hid_ref, cell_ref, left_ref, right_ref, _, far_ref, near_ref):
    odd = lax.axis_index("row") % 2 == 1
    for batch in range(2):
        for k, ref in enumerate((lat_ref, hid_ref, cell_ref)):
            lanes = slice(k * CH, (k + 1) * CH)
            mid = middle(ref[batch].astype(F32), left_ref[:, lanes], right_ref[:, lanes], batch)
            up, down = mid[:104].astype(BF16), mid[288:].astype(BF16)
            rows = slice(104 * batch, 104 * (batch + 1))

            @pl.when(odd)
            def _():
                far_ref[rows, lanes] = down
                near_ref[rows, lanes] = up

            @pl.when(jnp.logical_not(odd))
            def _():
                far_ref[rows, lanes] = up
                near_ref[rows, lanes] = down


def taps(src, at, cols_ref, rows, stride, step, first, row=0):
    for dx in range(3):
        moved = rolled(src, at + dx)
        for dy in range(3):
            lane = (3 * dy + dx) * step + first
            start = dy * stride
            cols_ref[row : row + rows, lane : lane + CH] = moved[start : start + rows].astype(BF16)


def activated(gates, cell_prev):
    cell = sigmoid(gates[:, CH : 2 * CH]) * cell_prev + sigmoid(gates[:, :CH]) * jnp.tanh(gates[:, 2 * CH : 3 * CH])
    return sigmoid(gates[:, 3 * CH :]) * jnp.tanh(cell), cell


def updated(cols, blocks, weight, extra, prev, mask):
    rows = prev.shape[0]
    size = rows // blocks
    hs, cs = [], []
    for k in range(blocks):
        part = slice(k * size, (k + 1) * size)
        add = extra if extra.shape[0] == 1 else extra[part]
        h, c = activated(jnp.dot(cols[part, :], weight[...], preferred_element_type=F32) + add, prev[part])
        hs.append(h if mask is None else h * mask[part])
        cs.append(c)
    return jnp.concatenate(hs, axis=0), jnp.concatenate(cs, axis=0)


def trimmed(v, edge, tile, stride):
    return rolled(v, edge).reshape(v.shape[0] // stride, stride, CH)[:, :tile]


def edge_rows(v, edge, tile, stride):
    v = trimmed(v, edge, tile, stride)
    return jnp.concatenate([v[edge:EDGE], v[EDGE : 2 * EDGE - edge]], axis=0)


def outer(v, stride):
    return jnp.concatenate([v[: EDGE * stride], v[-EDGE * stride :]], axis=0)


def middle_of(batch, k, ref, left_ref, right_ref):
    lanes = slice(k * CH, (k + 1) * CH)
    return middle(ref[batch].astype(F32), left_ref[:, lanes], right_ref[:, lanes], batch)


def first_middle_kernel(blocks, lat_ref, hid_ref, cell_ref, left_ref, right_ref, w_ref, b_ref, m_ref,
                        send_ref, htile_ref, ctile_ref, cols):
    tile = lat_ref.shape[1]
    stride = tile + 8

    @pl.when(lax.axis_index("section") == 0)
    def _():
        rows = (tile + 6 - 2 * EDGE) * stride
        skip = (EDGE - WIDE) * stride
        prev = []
        for batch in range(2):
            for k, ref in enumerate((lat_ref, hid_ref)):
                src = middle_of(batch, k, ref, left_ref, right_ref)[skip:]
                taps(src, WIDE, cols, rows, stride, 2 * CH, k * CH, batch * rows)
            state = rolled(middle_of(batch, 2, cell_ref, left_ref, right_ref), WIDE + 1)
            prev.append(state[skip + stride : skip + stride + rows])
        mask = m_ref[EDGE * stride : EDGE * stride + rows, :]
        h, c = updated(cols, blocks, w_ref, b_ref[...], jnp.concatenate(prev), jnp.concatenate([mask, mask]))
        send_ref[...] = h.astype(BF16)
        for batch in range(2):
            own = slice(batch * rows, (batch + 1) * rows)
            htile_ref[batch] = trimmed(h[own], 3, tile, stride).astype(BF16)
            ctile_ref[batch] = trimmed(c[own], 3, tile, stride)


def own_weight(w_ref):
    return jnp.concatenate([w_ref[(2 * t + 1) * CH : (2 * t + 2) * CH, :] for t in range(9)], axis=0)


def bordered(k, ref, batch, left_ref, right_ref, far_ref, near_ref):
    odd = lax.axis_index("row") % 2 == 1
    lanes = slice(k * CH, (k + 1) * CH)
    rows = slice(104 * batch, 104 * (batch + 1))
    far, near = far_ref[rows, lanes].astype(F32), near_ref[rows, lanes].astype(F32)
    above, below = jnp.where(odd, near, far), jnp.where(odd, far, near)
    mid = middle(ref[batch].astype(F32), left_ref[:, lanes], right_ref[:, lanes], batch)
    top = top_half((8, CH))
    first = jnp.where(top, above[96:], mid[:8])
    last = jnp.where(top, mid[384:], below[:8])
    return above[:96], first, mid, last, below[8:]


def first_edge_kernel(blocks, lat_ref, hid_ref, cell_ref, left_ref, right_ref, far_ref, near_ref,
                      w_ref, b_ref, m_ref, _, mid_part_ref, mid_prev_ref, part_ref, prev_ref, *rest):
    sends, tiles, cols = rest[:2], rest[2:6], rest[6]
    tile = lat_ref.shape[1]
    stride = tile + 8
    size = EDGE * stride
    rows = 2 * size

    for s in range(LAYERS):

        @pl.when(lax.axis_index("section") == s)
        def _():
            step = 2 * CH if s == 0 else CH
            starts = (s * stride, (s + tile + 6 - 2 * s - EDGE) * stride)
            prev = []

            def full(batch, k, ref):
                above, first, mid, last, below = bordered(k, ref, batch, left_ref, right_ref, far_ref, near_ref)
                return jnp.concatenate([above, first, mid[8:384], last, below], axis=0)

            for batch in range(2):
                for k, ref in enumerate((lat_ref, hid_ref)):
                    if k == 0 and s > 0:
                        continue
                    whole = full(batch, k, ref)
                    lane = step - CH if k else 0
                    for half, start in enumerate(starts):
                        src = whole[start : min(start + size + 3 * stride, whole.shape[0])]
                        taps(src, WIDE + s, cols, size, stride, step, lane, batch * rows + half * size)
                state = rolled(full(batch, 2, cell_ref), WIDE + 1 + s)
                prev += [state[start + stride : start + stride + size] for start in starts]
            if s == 0:
                mask = outer(m_ref[...], stride)
                h, c = updated(cols, blocks, w_ref, b_ref[...], jnp.concatenate(prev), jnp.concatenate([mask, mask]))
                for batch in range(2):
                    own = slice(batch * rows, (batch + 1) * rows)
                    sends[batch][...] = h[own].astype(BF16)
                    tiles[2 * batch][...] = edge_rows(h[own], 3, tile, stride).astype(BF16)
                    tiles[2 * batch + 1][...] = edge_rows(c[own], 3, tile, stride)
            else:
                prev_ref[...] = jnp.concatenate(prev)
                inner = (tile + 6 - 2 * s - 2 * EDGE) * stride
                skip = (s + EDGE - WIDE) * stride
                for batch in range(2):
                    src = middle_of(batch, 1, hid_ref, left_ref, right_ref)[skip:]
                    taps(src, WIDE + s, cols, inner, stride, CH, 0, 2 * rows + batch * inner)
                    state = rolled(middle_of(batch, 2, cell_ref, left_ref, right_ref), WIDE + 1 + s)
                    mid_prev_ref[batch * inner : (batch + 1) * inner, :] = state[skip + stride : skip + stride + inner]
                total = 2 * rows + 2 * inner
                gates = (
                    jnp.dot(cols[:total, : 9 * CH], own_weight(w_ref), preferred_element_type=F32) + b_ref[...]
                )
                part_ref[...] = gates[: 2 * rows]
                mid_part_ref[: 2 * inner, :] = gates[2 * rows :]


def next_middle_kernel(tick, blocks, x_ref, part_ref, prev_ref, win_ref, m_ref, *rest):
    send_ref, (htile_ref, ctile_ref, cols) = rest[0], rest[-3:]
    tile = htile_ref.shape[2]
    stride = tile + 8
    rows = (tile + 6 - 2 * tick - 2 * EDGE) * stride
    taken = rows + 2 * stride

    @pl.when(lax.axis_index("section") == tick)
    def _():
        for batch in range(2):
            x = x_ref[batch * taken : (batch + 1) * taken, :].astype(F32)
            taps(x, 0, cols, rows, stride, CH, 0, batch * rows)
        mask = None
        if tick < LAYERS - 1:
            mask = m_ref[EDGE * stride : EDGE * stride + rows, :]
            mask = jnp.concatenate([mask, mask])
        h, c = updated(cols, blocks, win_ref, part_ref[: 2 * rows, :], prev_ref[: 2 * rows, :], mask)
        if tick < LAYERS - 1:
            send_ref[...] = h.astype(BF16)
        for batch in range(2):
            own = slice(batch * rows, (batch + 1) * rows)
            htile_ref[batch] = trimmed(h[own], 3 - tick, tile, stride).astype(BF16)
            ctile_ref[batch] = trimmed(c[own], 3 - tick, tile, stride)


def next_edge(tick, batch, blocks, tile, x_ref, inner_ref, part_ref, prev_ref, win_ref, m_ref, cols):
    stride = tile + 8
    size, two = EDGE * stride, 2 * stride
    taken = inner_ref.shape[0] // 2
    x, inner = x_ref[...].astype(F32), inner_ref[batch * taken : (batch + 1) * taken, :].astype(F32)
    taps(jnp.concatenate([x[:size], inner[:two]], axis=0), 0, cols, size, stride, CH, 0)
    taps(jnp.concatenate([inner[-two:], x[size:]], axis=0), 0, cols, size, stride, CH, 0, size)
    mask = None if tick == LAYERS - 1 else outer(m_ref[: (tile + 6 - 2 * tick) * stride, :], stride)
    own = slice(2 * size * batch, 2 * size * (batch + 1))
    return updated(cols, blocks, win_ref, part_ref[own, :], prev_ref[own, :], mask)


def next_edge_kernel(tick, batch, blocks, x_ref, inner_ref, part_ref, prev_ref, win_ref, m_ref,
                     send_ref, htile_ref, ctile_ref, cols):
    tile = htile_ref.shape[1]

    @pl.when(lax.axis_index("section") == tick)
    def _():
        h, c = next_edge(tick, batch, blocks, tile, x_ref, inner_ref, part_ref, prev_ref, win_ref, m_ref, cols)
        send_ref[...] = h.astype(BF16)
        htile_ref[...] = edge_rows(h, 3 - tick, tile, tile + 8).astype(BF16)
        ctile_ref[...] = edge_rows(c, 3 - tick, tile, tile + 8)


def stores(tick, batch, tile_ref, out_ref, sems, k):
    tile = out_ref.shape[2]
    part = EDGE - 3 + tick
    if batch is None:
        return [pltpu.make_async_copy(tile_ref, out_ref.at[0, :, pl.ds(part, tile - 2 * part)], sems.at[k])]
    return [
        pltpu.make_async_copy(tile_ref.at[pl.ds(0, part)], out_ref.at[0, batch, pl.ds(0, part)], sems.at[k]),
        pltpu.make_async_copy(
            tile_ref.at[pl.ds(part, part)], out_ref.at[0, batch, pl.ds(tile - part, part)], sems.at[k + 1]
        ),
    ]


def last_kernel(batch, blocks, x_ref, inner_ref, part_ref, prev_ref, win_ref, m_ref, *rest):
    done, (_, _, hout_ref, cout_ref, cols, htile_ref, ctile_ref, sems) = rest[:-8], rest[-8:]
    tick = LAYERS - 1
    tile = htile_ref.shape[1]

    @pl.when(lax.axis_index("section") == tick)
    def _():
        copies = []
        if batch == 0:
            copies += stores(tick, None, done[0], hout_ref, sems, 4) + stores(tick, None, done[1], cout_ref, sems, 5)
        for copy in copies:
            copy.start()
        h, c = next_edge(tick, batch, blocks, tile, x_ref, inner_ref, part_ref, prev_ref, win_ref, m_ref, cols)
        ctile_ref[...] = edge_rows(c, 0, tile, tile + 8)
        htile_ref[...] = edge_rows(h, 0, tile, tile + 8).astype(BF16)
        mine = stores(tick, batch, ctile_ref, cout_ref, sems, 0) + stores(tick, batch, htile_ref, hout_ref, sems, 2)
        for copy in mine:
            copy.start()
        for copy in copies + mine:
            copy.wait()


def store_kernel(*rest):
    tiles, (hout_ref, cout_ref, sems) = rest[:-3], rest[-3:]
    for tick in range(LAYERS - 1):

        @pl.when(lax.axis_index("section") == tick)
        def _():
            copies = []
            for n, batch in enumerate((None, 0, 1)):
                h, c = tiles[6 * tick + 2 * n : 6 * tick + 2 * n + 2]
                copies += stores(tick, batch, h, hout_ref, sems, 4 * n)
                copies += stores(tick, batch, c, cout_ref, sems, 4 * n + 2)
            for copy in copies:
                copy.start()
            for copy in copies:
                copy.wait()


def on_device(latent, hidden_old, cell_old, weights, bias):
    tile = latent.shape[1]
    stride = tile + 8
    n_row, n_col = lax.axis_size("row"), lax.axis_size("col")
    stay = lambda v: pltpu.with_memory_space_constraint(v, pltpu.HBM)
    hid = hidden_old[0]
    cell = cell_old[0]
    w = weights.reshape(-1, weights.shape[-1])

    vm = lambda shape, kind: pltpu.VMEM(shape, kind)
    odd = lambda n: [(i, i + 1) for i in range(1, n - 1, 2)]
    even = lambda n: [(i, i + 1) for i in range(0, n - 1, 2)]
    both = lambda pairs: pairs + [(j, i) for i, j in pairs]
    lat, hid, cell, left, right = call(
        pack_kernel,
        (stay(latent), stay(hid), stay(cell)),
        [ANY] * 3,
        [vm(latent.shape, BF16), vm(hid.shape, BF16), vm(cell.shape, F32)] + [vm((8 * tile, 3 * CH), BF16)] * 2,
        [VMEM] * 5,
        [pltpu.SemaphoreType.DMA((3,))],
    )
    w, b, win, mask = call(
        functools.partial(load_kernel, tile),
        (right, stay(w), stay(bias)),
        [VMEM, ANY, ANY],
        [vm(w.shape, BF16), vm(bias.shape, F32), vm((9 * CH, 4 * CH), BF16), vm(((tile + 6) * stride, CH), F32)],
        [VMEM] * 4,
        [pltpu.SemaphoreType.DMA((2,))],
        flops=1 << 31,
    )
    left = lax.ppermute(left, "col", both(odd(n_col)))
    right = lax.ppermute(right, "col", both(even(n_col)))

    far, near = call(
        middle_kernel, (lat, hid, cell, left, right, b), [VMEM] * 6, [vm((208, 3 * CH), BF16)] * 2, [VMEM] * 2
    )
    far = lax.ppermute(far, "row", both(odd(n_row)))
    near = lax.ppermute(near, "row", both(even(n_row)))

    def height(tick):
        return tile + 6 - 2 * tick - 2 * EDGE

    def tiles_of(tick, kind):
        part = EDGE - 3 + tick
        shape = (2 * part, tile, CH) if kind else (2, tile - 2 * part, tile, CH)
        return [vm(shape, BF16), vm(shape, F32)]

    def hop(v, tick):
        return lax.ppermute(v, "section", [(tick, tick + 1)])

    edge = 2 * EDGE * stride
    rows = 2 * height(0) * stride
    send, htile, ctile = call(
        functools.partial(first_middle_kernel, BLOCKS),
        (lat, hid, cell, left, right, w, b, mask),
        [VMEM] * 8,
        [vm((rows, CH), BF16)] + tiles_of(0, 0),
        [VMEM] * 3,
        [pltpu.VMEM((rows, 18 * CH), BF16)],
        flops=2 * rows * 2304 * 512,
    )
    xs, tiles = [hop(send, 0)], [htile, ctile]
    inner = 2 * height(1) * stride
    *state, first, second, h0, c0, h1, c1 = call(
        functools.partial(first_edge_kernel, BLOCKS),
        (lat, hid, cell, left, right, far, near, w, b, mask, htile),
        [VMEM] * 11,
        [vm((rows, width), F32) for rows in (inner, 2 * edge) for width in (4 * CH, CH)]
        + [vm((edge, CH), BF16)] * 2
        + tiles_of(0, 1) * 2,
        [VMEM] * 10,
        [pltpu.VMEM((2 * edge + inner, 18 * CH), BF16)],
        flops=4 * edge * 2304 * 512,
    )
    state = (state[:2], state[2:])
    xs += [hop(first, 0), hop(second, 0)]
    tiles += [h0, c0, h1, c1]

    out_shapes = [
        jax.ShapeDtypeStruct((1, 2, tile, tile, CH), BF16),
        jax.ShapeDtypeStruct((1, 2, tile, tile, CH), F32),
    ]
    for tick in range(1, LAYERS):
        last = tick == LAYERS - 1
        rows = 2 * height(tick) * stride
        result = call(
            functools.partial(next_middle_kernel, tick, BLOCKS),
            (xs[0], *state[0], win, mask),
            [VMEM] * 5,
            ([] if last else [vm((rows, CH), BF16)]) + tiles_of(tick, 0),
            [VMEM] * (2 if last else 3),
            [pltpu.VMEM((rows, 9 * CH), BF16)],
            flops=2 * rows * 1152 * 512,
        )
        mine = list(result[-2:])
        nxt = [] if last else [hop(result[0], tick)]
        for batch in range(2):
            ins = (xs[1 + batch], xs[0], *state[1], win, mask)
            cols = pltpu.VMEM((edge, 9 * CH), BF16)
            if last:
                done = tuple(mine) if batch == 0 else ()
                count = len(ins) + len(done)
                outs = call(
                    functools.partial(last_kernel, batch, BLOCKS),
                    (*ins, *done, *outs),
                    [VMEM] * count + [ANY] * 2,
                    out_shapes,
                    [ANY, ANY],
                    [cols] + tiles_of(tick, 1) + [pltpu.SemaphoreType.DMA((6,))],
                    aliases={count: 0, count + 1: 1},
                    flops=2 * edge * 1152 * 512,
                )
                continue
            send, *result = call(
                functools.partial(next_edge_kernel, tick, batch, BLOCKS),
                ins,
                [VMEM] * len(ins),
                [vm((edge, CH), BF16)] + tiles_of(tick, 1),
                [VMEM] * 3,
                [cols],
                flops=2 * edge * 1152 * 512,
                after=mine[-2],
            )
            mine += result
            nxt.append(hop(send, tick))
        xs = nxt
        tiles += mine
        if tick == LAYERS - 2:
            outs = call(
                store_kernel, (*tiles,), [VMEM] * len(tiles), out_shapes, [ANY, ANY], [pltpu.SemaphoreType.DMA((12,))]
            )
    return tuple(outs)


def solution(mesh):
    in_specs = (
        P(None, "row", "col", None),
        P("section", None, "row", "col", None),
        P("section", None, "row", "col", None),
        P("section", None, None, None),
        P("section", None),
    )
    out_specs = (P("section", None, "row", "col", None), P("section", None, "row", "col", None))

    return jax.shard_map(on_device, mesh=mesh, in_specs=in_specs, out_specs=out_specs, check_vma=False)
```

time: 44.9 us -> 43.1 us (0.960)
  the two profiles are of different devices: /device:TPU:254 before, /device:TPU:110 now
where the time goes in v4:
time: 43.1 us; the launch traced here: 42.8 us
  starting transfers between devices  20.3 us (47%)
  waiting for transfers between devices  13.9 us (32%)
  Pallas kernels  7.65 us (18%)
  between operations  0.9 us (2%)
    ppermute x9, waiting for transfers between devices, hop(): return lax.ppermute(v, 'section', [(tick, tick + 1)])  10.7 us
    ppermute x9, starting transfers between devices, hop(): return lax.ppermute(v, 'section', [(tick, tick + 1)])  7.87 us
    pallas_call x15, Pallas kernels, call(): pl.pallas_call(body, out_shape=tuple(outs), in_specs=in_specs, out_specs=...  7.65 us
    ppermute x1, starting transfers between devices, on_device(): left = lax.ppermute(left, 'col', both(odd(n_col)))  5.04 us
    ppermute x1, starting transfers between devices, on_device(): near = lax.ppermute(near, 'row', both(even(n_row)))  3.59 us
    ppermute x1, waiting for transfers between devices, on_device(): right = lax.ppermute(right, 'col', both(even(n_col)))  2.8 us
    ppermute x1, starting transfers between devices, on_device(): right = lax.ppermute(right, 'col', both(even(n_col)))  1.92 us
    ppermute x1, starting transfers between devices, on_device(): far = lax.ppermute(far, 'row', both(odd(n_row)))  1.92 us
  transfers between devices with their start and end apart: 13, of which 5 were waited for; matrix products, arithmetic and copies ran while one was open for 0% of the time, Pallas kernels for 12%

profile of v4, /device:TPU:110, one launch (start us, length us, event | category | flops | bytes accessed | tf_op | source)
XLA Modules:
  0.0 42.8 jit_solution(1001989755592450111)
XLA Ops:
  0.6 1.1 %shard_map.68 = (bf16[2,16,16,128]{3,2,1,0:T(8,128)(2,1)S(1)}, bf16[2,16,16,128]{3,2,1,0:T(8,128)(2,1)S(1)}, f32[2,16,16,128]{3,2,1,0:T(8,128)S(1)}, bf16[128,384]{1,0:T(8,128)(2,1)S(1)}, bf16[128,384]{1,0:T(8,128)(2,1)S(1)}) custom-call(bf16[2,16,16,128]{3,2,1,0:T(8,128)(2,1)} %lat_hbm.1, bf16[2,16,16,128]{3,2,1,0:T(8,128)(2,1)} %bitcast.4, ...), custom_call_target="tpu_custom_call" | custom-call | bytes 1048576 | tf_op jit(solution)/shard_map/pallas_call | solution.py:48
  1.8 5.0 %collective-permute-start = (bf16[128,384]{1,0:T(8,128)(2,1)S(1)}, bf16[128,384]{1,0:T(8,128)(2,1)S(1)}, u32[]{:S(2)}, u32[]{:S(2)}) collective-permute-start(bf16[128,384]{1,0:T(8,128)(2,1)S(1)} %get-tuple-element.53), channel_id=1, source_target_pairs={{1,2},{3,4},{5,6},{7,8},{9,10},{11,12},{13,14},{2,1},{4,3},{6,5},{... | collective-permute-start | bytes 294920 | tf_op jit(solution)/shard_map/ppermute | solution.py:419
  6.8 1.9 %collective-permute-start.1 = (bf16[128,384]{1,0:T(8,128)(2,1)S(1)}, bf16[128,384]{1,0:T(8,128)(2,1)S(1)}, u32[]{:S(2)}, u32[]{:S(2)}) collective-permute-start(bf16[128,384]{1,0:T(8,128)(2,1)S(1)} %get-tuple-element.54._), channel_id=1, source_target_pairs={{0,1},{2,3},{4,5},{6,7},{8,9},{10,11},{12,13},{14,15},{1,0},{3,2},... | collective-permute-start | bytes 294920 | tf_op jit(solution)/shard_map/ppermute | solution.py:420
  8.8 1.8 %shard_map.69 = (bf16[2304,512]{1,0:T(8,128)(2,1)S(1)}, f32[1,512]{1,0:T(1,128)S(1)}, bf16[1152,512]{1,0:T(8,128)(2,1)S(1)}, f32[528,128]{1,0:T(8,128)S(1)}) custom-call(bf16[128,384]{1,0:T(8,128)(2,1)S(1)} %get-tuple-element.54._, bf16[2304,512]{1,0:T(8,128)(2,1)} %bitcast.5, f32[1,512]{1,0:T(1,128)} %b_hbm.1), custom_call_target="tpu_custom_call" | custom-call | flops 2147483648 | bytes 1048576 | tf_op jit(solution)/shard_map/pallas_call | solution.py:48
  10.5 0.0 collective-permute-done.left_ref
  10.5 2.8 %collective-permute-done.1.right_ref = bf16[128,384]{1,0:T(8,128)(2,1)S(1)} collective-permute-done((bf16[128,384]{1,0:T(8,128)(2,1)S(1)}, bf16[128,384]{1,0:T(8,128)(2,1)S(1)}, u32[]{:S(2)}, u32[]{:S(2)}) %collective-permute-start.1) | collective-permute-done | bytes 98336 | tf_op jit(solution)/shard_map/ppermute | solution.py:420
  13.3 0.1 shard_map.70
  13.5 1.9 %collective-permute-start.2 = (bf16[208,384]{1,0:T(8,128)(2,1)S(1)}, bf16[208,384]{1,0:T(8,128)(2,1)S(1)}, u32[]{:S(2)}, u32[]{:S(2)}) collective-permute-start(bf16[208,384]{1,0:T(8,128)(2,1)S(1)} %get-tuple-element.56), channel_id=1, source_target_pairs={{16,32},{48,64},{80,96},{32,16},{64,48},{96,80},{17,33},{49,65},{8... | collective-permute-start | bytes 479240 | tf_op jit(solution)/shard_map/ppermute | solution.py:425
  15.4 3.6 %collective-permute-start.3 = (bf16[208,384]{1,0:T(8,128)(2,1)S(1)}, bf16[208,384]{1,0:T(8,128)(2,1)S(1)}, u32[]{:S(2)}, u32[]{:S(2)}) collective-permute-start(bf16[208,384]{1,0:T(8,128)(2,1)S(1)} %get-tuple-element.57), channel_id=1, source_target_pairs={{0,16},{32,48},{64,80},{96,112},{16,0},{48,32},{80,64},{112,96},{1... | collective-permute-start | bytes 479240 | tf_op jit(solution)/shard_map/ppermute | solution.py:426
  19.0 0.7 %collective-permute-start.5 = (bf16[480,128]{1,0:T(8,128)(2,1)S(1)}, bf16[480,128]{1,0:T(8,128)(2,1)S(1)}, u32[]{:S(2)}, u32[]{:S(2)}) collective-permute-start(bf16[480,128]{1,0:T(8,128)(2,1)S(1)} %get-tuple-element.62), channel_id=1, source_target_pairs={{0,128},{1,129},{2,130},{3,131},{4,132},{5,133},{6,134},{7,135},{8... | collective-permute-start | bytes 368648 | tf_op jit(solution)/shard_map/ppermute | solution.py:437
  19.7 0.4 collective-permute-done.2.far_ref
  20.1 0.0 collective-permute-done.3.near_ref
  20.1 1.3 %shard_map.72 = (f32[384,512]{1,0:T(8,128)S(1)}, f32[384,128]{1,0:T(8,128)S(1)}, f32[576,512]{1,0:T(8,128)S(1)}, f32[576,128]{1,0:T(8,128)S(1)}, bf16[288,128]{1...) custom-call(bf16[2,16,16,128]{3,2,1,0:T(8,128)(2,1)S(1)} %get-tuple-, ...), custom_call_target="tpu_custom_call" | custom-call | flops 1358954496 | bytes 1048576 | tf_op jit(solution)/shard_map/pallas_call | solution.py:48
  21.3 0.7 %collective-permute-start.6 = (bf16[288,128]{1,0:T(8,128)(2,1)S(1)}, bf16[288,128]{1,0:T(8,128)(2,1)S(1)}, u32[]{:S(2)}, u32[]{:S(2)}) collective-permute-start(bf16[288,128]{1,0:T(8,128)(2,1)S(1)} %get-tuple-element.66), channel_id=1, source_target_pairs={{0,128},{1,129},{2,130},{3,131},{4,132},{5,133},{6,134},{7,135},{8... | collective-permute-start | bytes 221192 | tf_op jit(solution)/shard_map/ppermute | solution.py:437
  22.0 0.7 %collective-permute-start.4 = (bf16[288,128]{1,0:T(8,128)(2,1)S(1)}, bf16[288,128]{1,0:T(8,128)(2,1)S(1)}, u32[]{:S(2)}, u32[]{:S(2)}) collective-permute-start(bf16[288,128]{1,0:T(8,128)(2,1)S(1)} %get-tuple-element.61), channel_id=1, source_target_pairs={{0,128},{1,129},{2,130},{3,131},{4,132},{5,133},{6,134},{7,135},{8... | collective-permute-start | bytes 221192 | tf_op jit(solution)/shard_map/ppermute | solution.py:437
  22.7 0.0 collective-permute-done.5.x_ref.refs_1_
  22.7 0.7 %collective-permute-start.8 = (bf16[384,128]{1,0:T(8,128)(2,1)S(1)}, bf16[384,128]{1,0:T(8,128)(2,1)S(1)}, u32[]{:S(2)}, u32[]{:S(2)}) collective-permute-start(bf16[384,128]{1,0:T(8,128)(2,1)S(1)} %get-tuple-element.72), channel_id=1, source_target_pairs={{128,256},{129,257},{130,258},{131,259},{132,260},{133,261},{134,2... | collective-permute-start | bytes 294920 | tf_op jit(solution)/shard_map/ppermute | solution.py:437
  23.4 0.0 collective-permute-done.6.refs_0_
  23.4 0.7 %collective-permute-start.9 = (bf16[288,128]{1,0:T(8,128)(2,1)S(1)}, bf16[288,128]{1,0:T(8,128)(2,1)S(1)}, u32[]{:S(2)}, u32[]{:S(2)}) collective-permute-start(bf16[288,128]{1,0:T(8,128)(2,1)S(1)} %get-tuple-element.73), channel_id=1, source_target_pairs={{128,256},{129,257},{130,258},{131,259},{132,260},{133,261},{134,2... | collective-permute-start | bytes 221192 | tf_op jit(solution)/shard_map/ppermute | solution.py:437
  24.1 0.0 collective-permute-done.4.refs_0_
  24.1 0.7 %collective-permute-start.7 = (bf16[288,128]{1,0:T(8,128)(2,1)S(1)}, bf16[288,128]{1,0:T(8,128)(2,1)S(1)}, u32[]{:S(2)}, u32[]{:S(2)}) collective-permute-start(bf16[288,128]{1,0:T(8,128)(2,1)S(1)} %get-tuple-element.71), channel_id=1, source_target_pairs={{128,256},{129,257},{130,258},{131,259},{132,260},{133,261},{134,2... | collective-permute-start | bytes 221192 | tf_op jit(solution)/shard_map/ppermute | solution.py:437
  24.8 0.0 collective-permute-done.8.x_ref.refs_1_
  24.9 1.3 %collective-permute-start.11 = (bf16[288,128]{1,0:T(8,128)(2,1)S(1)}, bf16[288,128]{1,0:T(8,128)(2,1)S(1)}, u32[]{:S(2)}, u32[]{:S(2)}) collective-permute-start(bf16[288,128]{1,0:T(8,128)(2,1)S(1)} %get-tuple-element.77), channel_id=1, source_target_pairs={{256,384},{257,385},{258,386},{259,387},{260,388},{261,389},{262,3... | collective-permute-start | bytes 221192 | tf_op jit(solution)/shard_map/ppermute | solution.py:437
  26.2 0.0 collective-permute-done.9.refs_0_
  26.2 1.3 %collective-permute-start.12 = (bf16[288,128]{1,0:T(8,128)(2,1)S(1)}, bf16[288,128]{1,0:T(8,128)(2,1)S(1)}, u32[]{:S(2)}, u32[]{:S(2)}) collective-permute-start(bf16[288,128]{1,0:T(8,128)(2,1)S(1)} %get-tuple-element.78), channel_id=1, source_target_pairs={{256,384},{257,385},{258,386},{259,387},{260,388},{261,389},{262,3... | collective-permute-start | bytes 221192 | tf_op jit(solution)/shard_map/ppermute | solution.py:437
  27.5 0.0 collective-permute-done.7.refs_0_
  27.5 1.3 %collective-permute-start.10 = (bf16[288,128]{1,0:T(8,128)(2,1)S(1)}, bf16[288,128]{1,0:T(8,128)(2,1)S(1)}, u32[]{:S(2)}, u32[]{:S(2)}) collective-permute-start(bf16[288,128]{1,0:T(8,128)(2,1)S(1)} %get-tuple-element.76), channel_id=1, source_target_pairs={{256,384},{257,385},{258,386},{259,387},{260,388},{261,389},{262,3... | collective-permute-start | bytes 221192 | tf_op jit(solution)/shard_map/ppermute | solution.py:437
  28.8 0.2 shard_map.80
  29.0 8.2 %collective-permute-done.11.x_ref.inner_ref = bf16[288,128]{1,0:T(8,128)(2,1)S(1)} collective-permute-done((bf16[288,128]{1,0:T(8,128)(2,1)S(1)}, bf16[288,128]{1,0:T(8,128)(2,1)S(1)}, u32[]{:S(2)}, u32[]{:S(2)}) %collective-permute-start.11) | collective-permute-done | bytes 73760 | tf_op jit(solution)/shard_map/ppermute | solution.py:437
  37.3 0.5 %shard_map.79 = (bf16[2,4,16,128]{3,2,1,0:T(8,128)(2,1)S(1)}, f32[2,4,16,128]{3,2,1,0:T(8,128)S(1)}) custom-call(bf16[288,128]{1,0:T(8,128)(2,1)S(1)} %collective-permute-done.11.x_ref.inner_ref, f32[384,512]{1,0:T(8,128)S(1)} %get-tuple-element.67.part_ref, f32[384,128]{1,0:T(8,128)S(1)} %get-tuple-element.68.prev_ref, ...), custom_call_target="tpu_custom_call" | custom-call | flops 226492416 | bytes 1048576 | tf_op jit(solution)/shard_map/pallas_call | solution.py:48
  37.7 2.0 %collective-permute-done.12.x_ref = bf16[288,128]{1,0:T(8,128)(2,1)S(1)} collective-permute-done((bf16[288,128]{1,0:T(8,128)(2,1)S(1)}, bf16[288,128]{1,0:T(8,128)(2,1)S(1)}, u32[]{:S(2)}, u32[]{:S(2)}) %collective-permute-start.12) | collective-permute-done | bytes 73760 | tf_op jit(solution)/shard_map/ppermute | solution.py:437
  39.7 1.3 %shard_map.81 = (bf16[1,2,16,16,128]{4,3,2,1,0:T(8,128)(2,1)}, f32[1,2,16,16,128]{4,3,2,1,0:T(8,128)}) custom-call(bf16[288,128]{1,0:T(8,128)(2,1)S(1)} %collective-permute-done.12.x_ref, bf16[288,128]{1,0:T(8,128)(2,1)S(1)} %collective-permute-done.11.x_ref.inner_ref, ...), custom_call_target="tpu_custom_call", output_to_operand_aliasing={{0}: (8, {}), {1}: (9, {})} | custom-call | flops 339738624 | bytes 1048576 | tf_op jit(solution)/shard_map/pallas_call | solution.py:48
  41.0 0.5 %collective-permute-done.10.x_ref = bf16[288,128]{1,0:T(8,128)(2,1)S(1)} collective-permute-done((bf16[288,128]{1,0:T(8,128)(2,1)S(1)}, bf16[288,128]{1,0:T(8,128)(2,1)S(1)}, u32[]{:S(2)}, u32[]{:S(2)}) %collective-permute-start.10) | collective-permute-done | bytes 73760 | tf_op jit(solution)/shard_map/ppermute | solution.py:437
  41.5 1.3 %shard_map.82 = (bf16[1,2,16,16,128]{4,3,2,1,0:T(8,128)(2,1)}, f32[1,2,16,16,128]{4,3,2,1,0:T(8,128)}) custom-call(bf16[288,128]{1,0:T(8,128)(2,1)S(1)} %collective-permute-done.10.x_ref, bf16[288,128]{1,0:T(8,128)(2,1)S(1)} %collective-permute-done.11.x_ref.inner_ref, ...), custom_call_target="tpu_custom_call", output_to_operand_aliasing={{0}: (6, {}), {1}: (7, {})} | custom-call | flops 339738624 | bytes 1048576 | tf_op jit(solution)/shard_map/pallas_call | solution.py:48
  (7 shorter events, 0.1 us)
Async XLA Ops:
  1.8 8.7 %collective-permute-start = (bf16[128,384]{1,0:T(8,128)(2,1)S(1)}, bf16[128,384]{1,0:T(8,128)(2,1)S(1)}, u32[]{:S(2)}, u32[]{:S(2)}) collective-permute-start(bf16[128,384]{1,0:T(8,128)(2,1)S(1)} %get-tuple-element.53), channel_id=1, source_target_pairs={{1,2},{3,4},{5,6},{7,8},{9,10},{11,12},{13,14},{2,1},{4,3},{6,5},{... | collective-permute-start | bytes 294920 | tf_op jit(solution)/shard_map/ppermute | solution.py:419
  6.8 6.5 %collective-permute-start.1 = (bf16[128,384]{1,0:T(8,128)(2,1)S(1)}, bf16[128,384]{1,0:T(8,128)(2,1)S(1)}, u32[]{:S(2)}, u32[]{:S(2)}) collective-permute-start(bf16[128,384]{1,0:T(8,128)(2,1)S(1)} %get-tuple-element.54._), channel_id=1, source_target_pairs={{0,1},{2,3},{4,5},{6,7},{8,9},{10,11},{12,13},{14,15},{1,0},{3,2},... | collective-permute-start | bytes 294920 | tf_op jit(solution)/shard_map/ppermute | solution.py:420
  13.5 6.6 %collective-permute-start.2 = (bf16[208,384]{1,0:T(8,128)(2,1)S(1)}, bf16[208,384]{1,0:T(8,128)(2,1)S(1)}, u32[]{:S(2)}, u32[]{:S(2)}) collective-permute-start(bf16[208,384]{1,0:T(8,128)(2,1)S(1)} %get-tuple-element.56), channel_id=1, source_target_pairs={{16,32},{48,64},{80,96},{32,16},{64,48},{96,80},{17,33},{49,65},{8... | collective-permute-start | bytes 479240 | tf_op jit(solution)/shard_map/ppermute | solution.py:425
  15.4 4.7 %collective-permute-start.3 = (bf16[208,384]{1,0:T(8,128)(2,1)S(1)}, bf16[208,384]{1,0:T(8,128)(2,1)S(1)}, u32[]{:S(2)}, u32[]{:S(2)}) collective-permute-start(bf16[208,384]{1,0:T(8,128)(2,1)S(1)} %get-tuple-element.57), channel_id=1, source_target_pairs={{0,16},{32,48},{64,80},{96,112},{16,0},{48,32},{80,64},{112,96},{1... | collective-permute-start | bytes 479240 | tf_op jit(solution)/shard_map/ppermute | solution.py:426
  19.0 3.7 %collective-permute-start.5 = (bf16[480,128]{1,0:T(8,128)(2,1)S(1)}, bf16[480,128]{1,0:T(8,128)(2,1)S(1)}, u32[]{:S(2)}, u32[]{:S(2)}) collective-permute-start(bf16[480,128]{1,0:T(8,128)(2,1)S(1)} %get-tuple-element.62), channel_id=1, source_target_pairs={{0,128},{1,129},{2,130},{3,131},{4,132},{5,133},{6,134},{7,135},{8... | collective-permute-start | bytes 368648 | tf_op jit(solution)/shard_map/ppermute | solution.py:437
  21.3 2.1 %collective-permute-start.6 = (bf16[288,128]{1,0:T(8,128)(2,1)S(1)}, bf16[288,128]{1,0:T(8,128)(2,1)S(1)}, u32[]{:S(2)}, u32[]{:S(2)}) collective-permute-start(bf16[288,128]{1,0:T(8,128)(2,1)S(1)} %get-tuple-element.66), channel_id=1, source_target_pairs={{0,128},{1,129},{2,130},{3,131},{4,132},{5,133},{6,134},{7,135},{8... | collective-permute-start | bytes 221192 | tf_op jit(solution)/shard_map/ppermute | solution.py:437
  22.0 2.1 %collective-permute-start.4 = (bf16[288,128]{1,0:T(8,128)(2,1)S(1)}, bf16[288,128]{1,0:T(8,128)(2,1)S(1)}, u32[]{:S(2)}, u32[]{:S(2)}) collective-permute-start(bf16[288,128]{1,0:T(8,128)(2,1)S(1)} %get-tuple-element.61), channel_id=1, source_target_pairs={{0,128},{1,129},{2,130},{3,131},{4,132},{5,133},{6,134},{7,135},{8... | collective-permute-start | bytes 221192 | tf_op jit(solution)/shard_map/ppermute | solution.py:437
  22.7 2.1 %collective-permute-start.8 = (bf16[384,128]{1,0:T(8,128)(2,1)S(1)}, bf16[384,128]{1,0:T(8,128)(2,1)S(1)}, u32[]{:S(2)}, u32[]{:S(2)}) collective-permute-start(bf16[384,128]{1,0:T(8,128)(2,1)S(1)} %get-tuple-element.72), channel_id=1, source_target_pairs={{128,256},{129,257},{130,258},{131,259},{132,260},{133,261},{134,2... | collective-permute-start | bytes 294920 | tf_op jit(solution)/shard_map/ppermute | solution.py:437
  23.4 2.7 %collective-permute-start.9 = (bf16[288,128]{1,0:T(8,128)(2,1)S(1)}, bf16[288,128]{1,0:T(8,128)(2,1)S(1)}, u32[]{:S(2)}, u32[]{:S(2)}) collective-permute-start(bf16[288,128]{1,0:T(8,128)(2,1)S(1)} %get-tuple-element.73), channel_id=1, source_target_pairs={{128,256},{129,257},{130,258},{131,259},{132,260},{133,261},{134,2... | collective-permute-start | bytes 221192 | tf_op jit(solution)/shard_map/ppermute | solution.py:437
  24.1 3.3 %collective-permute-start.7 = (bf16[288,128]{1,0:T(8,128)(2,1)S(1)}, bf16[288,128]{1,0:T(8,128)(2,1)S(1)}, u32[]{:S(2)}, u32[]{:S(2)}) collective-permute-start(bf16[288,128]{1,0:T(8,128)(2,1)S(1)} %get-tuple-element.71), channel_id=1, source_target_pairs={{128,256},{129,257},{130,258},{131,259},{132,260},{133,261},{134,2... | collective-permute-start | bytes 221192 | tf_op jit(solution)/shard_map/ppermute | solution.py:437
  24.9 12.4 %collective-permute-start.11 = (bf16[288,128]{1,0:T(8,128)(2,1)S(1)}, bf16[288,128]{1,0:T(8,128)(2,1)S(1)}, u32[]{:S(2)}, u32[]{:S(2)}) collective-permute-start(bf16[288,128]{1,0:T(8,128)(2,1)S(1)} %get-tuple-element.77), channel_id=1, source_target_pairs={{256,384},{257,385},{258,386},{259,387},{260,388},{261,389},{262,3... | collective-permute-start | bytes 221192 | tf_op jit(solution)/shard_map/ppermute | solution.py:437
  26.2 13.5 %collective-permute-start.12 = (bf16[288,128]{1,0:T(8,128)(2,1)S(1)}, bf16[288,128]{1,0:T(8,128)(2,1)S(1)}, u32[]{:S(2)}, u32[]{:S(2)}) collective-permute-start(bf16[288,128]{1,0:T(8,128)(2,1)S(1)} %get-tuple-element.78), channel_id=1, source_target_pairs={{256,384},{257,385},{258,386},{259,387},{260,388},{261,389},{262,3... | collective-permute-start | bytes 221192 | tf_op jit(solution)/shard_map/ppermute | solution.py:437
  27.5 14.0 %collective-permute-start.10 = (bf16[288,128]{1,0:T(8,128)(2,1)S(1)}, bf16[288,128]{1,0:T(8,128)(2,1)S(1)}, u32[]{:S(2)}, u32[]{:S(2)}) collective-permute-start(bf16[288,128]{1,0:T(8,128)(2,1)S(1)} %get-tuple-element.76), channel_id=1, source_target_pairs={{256,384},{257,385},{258,386},{259,387},{260,388},{261,389},{262,3... | collective-permute-start | bytes 221192 | tf_op jit(solution)/shard_map/ppermute | solution.py:437

commit v5 on v4

--- a/solution.py
+++ b/solution.py
@@ -90,13 +90,21 @@
     copies = [pltpu.make_async_copy(w_hbm, w_ref, sems.at[0]), pltpu.make_async_copy(b_hbm, b_ref, sems.at[1])]
     for copy in copies:
         copy.start()
-    edge = 3 - lax.axis_index("section")
-    shape = (tile + 6, tile + 8, CH)
-    r = lax.axis_index("row") * tile - edge + lax.broadcasted_iota(jnp.int32, shape, 0)
-    c = lax.axis_index("col") * tile - edge + lax.broadcasted_iota(jnp.int32, shape, 1)
-    high, wide = lax.axis_size("row") * tile, lax.axis_size("col") * tile
-    inside = (r >= 0) & (r < high) & (c >= 0) & (c < wide)
-    m_ref[...] = jnp.where(inside, jnp.ones(shape, F32), jnp.zeros(shape, F32)).reshape(-1, CH)
+    high, width = lax.axis_size("row") * tile, lax.axis_size("col") * tile
+    for s in range(LAYERS - 1):
+
+        @pl.when(lax.axis_index("section") == s)
+        def _():
+            n = tile + 6 - 2 * s
+            shape = (n, tile + 8, CH)
+            r = lax.axis_index("row") * tile - (3 - s) + lax.broadcasted_iota(jnp.int32, shape, 0)
+            c = lax.axis_index("col") * tile - (3 - s) + lax.broadcasted_iota(jnp.int32, shape, 1)
+            inside = (r >= 0) & (r < high) & (c >= 0) & (c < width)
+            wide = jnp.where(inside, jnp.ones(shape, F32), jnp.zeros(shape, F32))
+            m_ref[n * n :, :] = jnp.zeros((m_ref.shape[0] - n * n, CH), F32)
+            for k in range(n):
+                m_ref[k * n : (k + 1) * n, :] = wide[k][:n]
+
     for copy in copies:
         copy.wait()
 
@@ -156,30 +164,63 @@
     return sigmoid(gates[:, 3 * CH :]) * jnp.tanh(cell), cell
 
 
-def updated(cols, blocks, weight, extra, prev, mask):
+def updated(cols, blocks, weight, extra, prev):
     rows = prev.shape[0]
     size = rows // blocks
     hs, cs = [], []
     for k in range(blocks):
         part = slice(k * size, (k + 1) * size)
         add = extra if extra.shape[0] == 1 else extra[part]
-        h, c = activated(jnp.dot(cols[part, :], weight[...], preferred_element_type=F32) + add, prev[part])
-        hs.append(h if mask is None else h * mask[part])
+        h, c = activated(jnp.dot(cols[part, : weight.shape[0]], weight[...], preferred_element_type=F32) + add, prev[part])
+        hs.append(h)
         cs.append(c)
     return jnp.concatenate(hs, axis=0), jnp.concatenate(cs, axis=0)
 
 
-def trimmed(v, edge, tile, stride):
-    return rolled(v, edge).reshape(v.shape[0] // stride, stride, CH)[:, :tile]
-
-
-def edge_rows(v, edge, tile, stride):
-    v = trimmed(v, edge, tile, stride)
-    return jnp.concatenate([v[edge:EDGE], v[EDGE : 2 * EDGE - edge]], axis=0)
-
-
-def outer(v, stride):
-    return jnp.concatenate([v[: EDGE * stride], v[-EDGE * stride :]], axis=0)
+def up_to(v, to):
+    return -(-v // to) * to
+
+
+def geometry(tile, tick, kind):
+    n = tile + 6 - 2 * tick
+    stride = n + 2
+    rows = EDGE if kind else n - 2 * EDGE
+    return n, stride, rows, up_to(rows * stride, 16), up_to(rows * n, 8)
+
+
+def window_taps(src, base, cols_ref, slots, stride, step, first, row):
+    for dx in range(3):
+        for dy in range(3):
+            lane = (3 * dy + dx) * step + first
+            start = base + dy * stride + dx
+            cols_ref[row : row + slots, lane : lane + CH] = src[start : start + slots, :].astype(BF16)
+
+
+def sent(tile, tick, kind, h_scr, at, out_scr, send_ref, m_ref):
+    n, stride, rows, slots, packed = geometry(tile, tick, kind)
+    firsts = (0, n - EDGE) if kind else (EDGE, EDGE)
+    for seg, first in enumerate(firsts):
+        for r in range(rows):
+            src = at + seg * slots + r * stride
+            out_scr[seg * packed + r * n : seg * packed + (r + 1) * n, :] = h_scr[src : src + n, :]
+        mask = m_ref[first * n : first * n + packed, :]
+        send_ref[seg * packed : (seg + 1) * packed, :] = (
+            out_scr[seg * packed : (seg + 1) * packed, :] * mask
+        ).astype(BF16)
+
+
+def kept(tile, tick, kind, scr, at, tile_ref):
+    _, stride, rows, slots, _ = geometry(tile, tick, kind)
+    edge = 3 - tick
+    for seg in range(2):
+        low, high = (edge, rows) if kind and seg == 0 else (0, rows - edge) if kind else (0, rows)
+        for r in range(low, high):
+            src = at + seg * slots + r * stride + edge
+            v = scr[src : src + tile, :].astype(tile_ref.dtype)
+            if kind:
+                tile_ref[seg * (rows - edge) + r - low] = v
+            else:
+                tile_ref[seg, r] = v
 
 
 def middle_of(batch, k, ref, left_ref, right_ref):
@@ -188,7 +229,7 @@
 
 
 def first_middle_kernel(blocks, lat_ref, hid_ref, cell_ref, left_ref, right_ref, w_ref, b_ref, m_ref,
-                        send_ref, htile_ref, ctile_ref, cols):
+                        send_ref, htile_ref, ctile_ref, cols, h_scr, c_scr, out_scr):
     tile = lat_ref.shape[1]
     stride = tile + 8
 
@@ -203,13 +244,12 @@
                 taps(src, WIDE, cols, rows, stride, 2 * CH, k * CH, batch * rows)
             state = rolled(middle_of(batch, 2, cell_ref, left_ref, right_ref), WIDE + 1)
             prev.append(state[skip + stride : skip + stride + rows])
-        mask = m_ref[EDGE * stride : EDGE * stride + rows, :]
-        h, c = updated(cols, blocks, w_ref, b_ref[...], jnp.concatenate(prev), jnp.concatenate([mask, mask]))
-        send_ref[...] = h.astype(BF16)
-        for batch in range(2):
-            own = slice(batch * rows, (batch + 1) * rows)
-            htile_ref[batch] = trimmed(h[own], 3, tile, stride).astype(BF16)
-            ctile_ref[batch] = trimmed(c[own], 3, tile, stride)
+        h, c = updated(cols, blocks, w_ref, b_ref[...], jnp.concatenate(prev))
+        h_scr[...] = h
+        c_scr[...] = c
+        sent(tile, 0, 0, h_scr, 0, out_scr, send_ref, m_ref)
+        kept(tile, 0, 0, h_scr, 0, htile_ref)
+        kept(tile, 0, 0, c_scr, 0, ctile_ref)
 
 
 def own_weight(w_ref):
@@ -231,107 +271,113 @@
 
 def first_edge_kernel(blocks, lat_ref, hid_ref, cell_ref, left_ref, right_ref, far_ref, near_ref,
                       w_ref, b_ref, m_ref, _, mid_part_ref, mid_prev_ref, part_ref, prev_ref, *rest):
-    sends, tiles, cols = rest[:2], rest[2:6], rest[6]
+    sends, tiles, (cols, h_scr, c_scr, out_scr) = rest[:2], rest[2:6], rest[6:]
     tile = lat_ref.shape[1]
-    stride = tile + 8
-    size = EDGE * stride
-    rows = 2 * size
-
-    for s in range(LAYERS):
+    wide = tile + 8
+    size = EDGE * wide
+
+    def full(batch, k, ref):
+        above, first, mid, last, below = bordered(k, ref, batch, left_ref, right_ref, far_ref, near_ref)
+        return jnp.concatenate([above, first, mid[8:384], last, below], axis=0)
+
+    @pl.when(lax.axis_index("section") == 0)
+    def _():
+        starts = (0, (tile + 6 - EDGE) * wide)
+        prev = []
+        for batch in range(2):
+            for k, ref in enumerate((lat_ref, hid_ref)):
+                whole = full(batch, k, ref)
+                for half, start in enumerate(starts):
+                    src = whole[start : min(start + size + 3 * wide, whole.shape[0])]
+                    taps(src, WIDE, cols, size, wide, 2 * CH, k * CH, (2 * batch + half) * size)
+            state = rolled(full(batch, 2, cell_ref), WIDE + 1)
+            prev += [state[start + wide : start + wide + size] for start in starts]
+        h, c = updated(cols.at[: 4 * size], blocks, w_ref, b_ref[...], jnp.concatenate(prev))
+        h_scr[: 4 * size, :] = h
+        c_scr[: 4 * size, :] = c
+        for batch in range(2):
+            sent(tile, 0, 1, h_scr, 2 * batch * size, out_scr, sends[batch], m_ref)
+            kept(tile, 0, 1, h_scr, 2 * batch * size, tiles[2 * batch])
+            kept(tile, 0, 1, c_scr, 2 * batch * size, tiles[2 * batch + 1])
+
+    for s in range(1, LAYERS):
 
         @pl.when(lax.axis_index("section") == s)
         def _():
-            step = 2 * CH if s == 0 else CH
-            starts = (s * stride, (s + tile + 6 - 2 * s - EDGE) * stride)
-            prev = []
-
-            def full(batch, k, ref):
-                above, first, mid, last, below = bordered(k, ref, batch, left_ref, right_ref, far_ref, near_ref)
-                return jnp.concatenate([above, first, mid[8:384], last, below], axis=0)
-
+            n, stride, _, slots, _ = geometry(tile, s, 1)
+            _, _, inner, mid_slots, _ = geometry(tile, s, 0)
             for batch in range(2):
-                for k, ref in enumerate((lat_ref, hid_ref)):
-                    if k == 0 and s > 0:
-                        continue
-                    whole = full(batch, k, ref)
-                    lane = step - CH if k else 0
-                    for half, start in enumerate(starts):
-                        src = whole[start : min(start + size + 3 * stride, whole.shape[0])]
-                        taps(src, WIDE + s, cols, size, stride, step, lane, batch * rows + half * size)
-                state = rolled(full(batch, 2, cell_ref), WIDE + 1 + s)
-                prev += [state[start + stride : start + stride + size] for start in starts]
-            if s == 0:
-                mask = outer(m_ref[...], stride)
-                h, c = updated(cols, blocks, w_ref, b_ref[...], jnp.concatenate(prev), jnp.concatenate([mask, mask]))
-                for batch in range(2):
-                    own = slice(batch * rows, (batch + 1) * rows)
-                    sends[batch][...] = h[own].astype(BF16)
-                    tiles[2 * batch][...] = edge_rows(h[own], 3, tile, stride).astype(BF16)
-                    tiles[2 * batch + 1][...] = edge_rows(c[own], 3, tile, stride)
-            else:
-                prev_ref[...] = jnp.concatenate(prev)
-                inner = (tile + 6 - 2 * s - 2 * EDGE) * stride
-                skip = (s + EDGE - WIDE) * stride
-                for batch in range(2):
-                    src = middle_of(batch, 1, hid_ref, left_ref, right_ref)[skip:]
-                    taps(src, WIDE + s, cols, inner, stride, CH, 0, 2 * rows + batch * inner)
-                    state = rolled(middle_of(batch, 2, cell_ref, left_ref, right_ref), WIDE + 1 + s)
-                    mid_prev_ref[batch * inner : (batch + 1) * inner, :] = state[skip + stride : skip + stride + inner]
-                total = 2 * rows + 2 * inner
-                gates = (
-                    jnp.dot(cols[:total, : 9 * CH], own_weight(w_ref), preferred_element_type=F32) + b_ref[...]
+                whole = full(batch, 1, hid_ref)
+                h_scr[: whole.shape[0], :] = whole
+                c_scr[: whole.shape[0], :] = full(batch, 2, cell_ref)
+                segs = (
+                    (0, EDGE, slots, 2 * batch * slots, prev_ref, 2 * batch * slots),
+                    (n - EDGE, EDGE, slots, (2 * batch + 1) * slots, prev_ref, (2 * batch + 1) * slots),
+                    (EDGE, inner, mid_slots, 4 * slots + batch * mid_slots, mid_prev_ref, batch * mid_slots),
                 )
-                part_ref[...] = gates[: 2 * rows]
-                mid_part_ref[: 2 * inner, :] = gates[2 * rows :]
+                for k, (first, rows, count, row, state_ref, at) in enumerate(segs):
+                    base = 320 * k
+                    for r in range(rows + 2):
+                        src = (s + first + r) * wide + WIDE + s
+                        out_scr[base + r * stride : base + (r + 1) * stride, :] = h_scr[src : src + stride, :]
+                    window_taps(out_scr, base, cols, count, stride, CH, 0, row)
+                    for r in range(rows):
+                        src = (s + first + r + 1) * wide + WIDE + 1 + s
+                        state_ref[at + r * stride : at + r * stride + n, :] = c_scr[src : src + n, :]
+            total = 4 * slots + 2 * mid_slots
+            gates = jnp.dot(cols[:total, : 9 * CH], own_weight(w_ref), preferred_element_type=F32) + b_ref[...]
+            part_ref[: 4 * slots, :] = gates[: 4 * slots]
+            mid_part_ref[: 2 * mid_slots, :] = gates[4 * slots :]
 
 
 def next_middle_kernel(tick, blocks, x_ref, part_ref, prev_ref, win_ref, m_ref, *rest):
-    send_ref, (htile_ref, ctile_ref, cols) = rest[0], rest[-3:]
+    send_ref, (htile_ref, ctile_ref, cols, h_scr, c_scr, out_scr) = rest[0], rest[-6:]
     tile = htile_ref.shape[2]
-    stride = tile + 8
-    rows = (tile + 6 - 2 * tick - 2 * EDGE) * stride
-    taken = rows + 2 * stride
+    _, stride, _, slots, _ = geometry(tile, tick, 0)
+    taken = x_ref.shape[0]
 
     @pl.when(lax.axis_index("section") == tick)
     def _():
+        out_scr[:taken, :] = x_ref[...].astype(F32)
         for batch in range(2):
-            x = x_ref[batch * taken : (batch + 1) * taken, :].astype(F32)
-            taps(x, 0, cols, rows, stride, CH, 0, batch * rows)
-        mask = None
+            window_taps(out_scr, batch * taken // 2, cols, slots, stride, CH, 0, batch * slots)
+        h, c = updated(cols, blocks, win_ref, part_ref[: 2 * slots, :], prev_ref[: 2 * slots, :])
+        h_scr[...] = h
+        c_scr[...] = c
         if tick < LAYERS - 1:
-            mask = m_ref[EDGE * stride : EDGE * stride + rows, :]
-            mask = jnp.concatenate([mask, mask])
-        h, c = updated(cols, blocks, win_ref, part_ref[: 2 * rows, :], prev_ref[: 2 * rows, :], mask)
-        if tick < LAYERS - 1:
-            send_ref[...] = h.astype(BF16)
-        for batch in range(2):
-            own = slice(batch * rows, (batch + 1) * rows)
-            htile_ref[batch] = trimmed(h[own], 3 - tick, tile, stride).astype(BF16)
-            ctile_ref[batch] = trimmed(c[own], 3 - tick, tile, stride)
-
-
-def next_edge(tick, batch, blocks, tile, x_ref, inner_ref, part_ref, prev_ref, win_ref, m_ref, cols):
-    stride = tile + 8
-    size, two = EDGE * stride, 2 * stride
-    taken = inner_ref.shape[0] // 2
-    x, inner = x_ref[...].astype(F32), inner_ref[batch * taken : (batch + 1) * taken, :].astype(F32)
-    taps(jnp.concatenate([x[:size], inner[:two]], axis=0), 0, cols, size, stride, CH, 0)
-    taps(jnp.concatenate([inner[-two:], x[size:]], axis=0), 0, cols, size, stride, CH, 0, size)
-    mask = None if tick == LAYERS - 1 else outer(m_ref[: (tile + 6 - 2 * tick) * stride, :], stride)
-    own = slice(2 * size * batch, 2 * size * (batch + 1))
-    return updated(cols, blocks, win_ref, part_ref[own, :], prev_ref[own, :], mask)
+            sent(tile, tick, 0, h_scr, 0, out_scr, send_ref, m_ref)
+        kept(tile, tick, 0, h_scr, 0, htile_ref)
+        kept(tile, tick, 0, c_scr, 0, ctile_ref)
+
+
+def next_edge(tick, batch, blocks, tile, x_ref, inner_ref, part_ref, prev_ref, win_ref, cols, h_scr, c_scr, out_scr):
+    _, stride, rows, slots, _ = geometry(tile, tick, 1)
+    _, _, inner_rows, _, taken = geometry(tile, tick - 1, 0)
+    half, two = x_ref.shape[0] // 2, 2 * stride
+    x = x_ref[...].astype(F32)
+    h_scr[:taken, :] = inner_ref[batch * taken : (batch + 1) * taken, :].astype(F32)
+    out_scr[:half, :] = x[:half]
+    out_scr[rows * stride : rows * stride + two, :] = h_scr[:two, :]
+    out_scr[320 : 320 + two, :] = h_scr[(inner_rows - 2) * stride : inner_rows * stride, :]
+    out_scr[320 + two : 320 + two + half, :] = x[half:]
+    for seg in range(2):
+        window_taps(out_scr, 320 * seg, cols, slots, stride, CH, 0, seg * slots)
+    own = slice(2 * slots * batch, 2 * slots * (batch + 1))
+    h, c = updated(cols, blocks, win_ref, part_ref[own, :], prev_ref[own, :])
+    h_scr[: 2 * slots, :] = h
+    c_scr[: 2 * slots, :] = c
 
 
 def next_edge_kernel(tick, batch, blocks, x_ref, inner_ref, part_ref, prev_ref, win_ref, m_ref,
-                     send_ref, htile_ref, ctile_ref, cols):
+                     send_ref, htile_ref, ctile_ref, cols, *scr):
     tile = htile_ref.shape[1]
 
     @pl.when(lax.axis_index("section") == tick)
     def _():
-        h, c = next_edge(tick, batch, blocks, tile, x_ref, inner_ref, part_ref, prev_ref, win_ref, m_ref, cols)
-        send_ref[...] = h.astype(BF16)
-        htile_ref[...] = edge_rows(h, 3 - tick, tile, tile + 8).astype(BF16)
-        ctile_ref[...] = edge_rows(c, 3 - tick, tile, tile + 8)
+        next_edge(tick, batch, blocks, tile, x_ref, inner_ref, part_ref, prev_ref, win_ref, cols, *scr)
+        sent(tile, tick, 1, scr[0], 0, scr[2], send_ref, m_ref)
+        kept(tile, tick, 1, scr[0], 0, htile_ref)
+        kept(tile, tick, 1, scr[1], 0, ctile_ref)
 
 
 def stores(tick, batch, tile_ref, out_ref, sems, k):
@@ -348,7 +394,7 @@
 
 
 def last_kernel(batch, blocks, x_ref, inner_ref, part_ref, prev_ref, win_ref, m_ref, *rest):
-    done, (_, _, hout_ref, cout_ref, cols, htile_ref, ctile_ref, sems) = rest[:-8], rest[-8:]
+    done, (_, _, hout_ref, cout_ref, cols, *scr, htile_ref, ctile_ref, sems) = rest[:-11], rest[-11:]
     tick = LAYERS - 1
     tile = htile_ref.shape[1]
 
@@ -359,9 +405,9 @@
             copies += stores(tick, None, done[0], hout_ref, sems, 4) + stores(tick, None, done[1], cout_ref, sems, 5)
         for copy in copies:
             copy.start()
-        h, c = next_edge(tick, batch, blocks, tile, x_ref, inner_ref, part_ref, prev_ref, win_ref, m_ref, cols)
-        ctile_ref[...] = edge_rows(c, 0, tile, tile + 8)
-        htile_ref[...] = edge_rows(h, 0, tile, tile + 8).astype(BF16)
+        next_edge(tick, batch, blocks, tile, x_ref, inner_ref, part_ref, prev_ref, win_ref, cols, *scr)
+        kept(tile, tick, 1, scr[1], 0, ctile_ref)
+        kept(tile, tick, 1, scr[0], 0, htile_ref)
         mine = stores(tick, batch, ctile_ref, cout_ref, sems, 0) + stores(tick, batch, htile_ref, hout_ref, sems, 2)
         for copy in mine:
             copy.start()
@@ -388,7 +434,6 @@
 
 def on_device(latent, hidden_old, cell_old, weights, bias):
     tile = latent.shape[1]
-    stride = tile + 8
     n_row, n_col = lax.axis_size("row"), lax.axis_size("col")
     stay = lambda v: pltpu.with_memory_space_constraint(v, pltpu.HBM)
     hid = hidden_old[0]
@@ -411,7 +456,7 @@
         functools.partial(load_kernel, tile),
         (right, stay(w), stay(bias)),
         [VMEM, ANY, ANY],
-        [vm(w.shape, BF16), vm(bias.shape, F32), vm((9 * CH, 4 * CH), BF16), vm(((tile + 6) * stride, CH), F32)],
+        [vm(w.shape, BF16), vm(bias.shape, F32), vm((9 * CH, 4 * CH), BF16), vm((up_to((tile + 6) ** 2, 8) + 16, CH), F32)],
         [VMEM] * 4,
         [pltpu.SemaphoreType.DMA((2,))],
         flops=1 << 31,
@@ -425,8 +470,12 @@
     far = lax.ppermute(far, "row", both(odd(n_row)))
     near = lax.ppermute(near, "row", both(even(n_row)))
 
-    def height(tick):
-        return tile + 6 - 2 * tick - 2 * EDGE
+    def scratch(slots, lanes, work=0):
+        sizes = (work or slots, work or slots, max(960, slots))
+        return [pltpu.VMEM((slots, lanes), BF16)] + [pltpu.VMEM((size, CH), F32) for size in sizes]
+
+    def sizes(tick, kind):
+        return tuple(2 * v for v in geometry(tile, tick, kind)[3:])
 
     def tiles_of(tick, kind):
         part = EDGE - 3 + tick
@@ -436,29 +485,29 @@
     def hop(v, tick):
         return lax.ppermute(v, "section", [(tick, tick + 1)])
 
-    edge = 2 * EDGE * stride
-    rows = 2 * height(0) * stride
+    slots, packed = sizes(0, 0)
     send, htile, ctile = call(
         functools.partial(first_middle_kernel, BLOCKS),
         (lat, hid, cell, left, right, w, b, mask),
         [VMEM] * 8,
-        [vm((rows, CH), BF16)] + tiles_of(0, 0),
+        [vm((packed, CH), BF16)] + tiles_of(0, 0),
         [VMEM] * 3,
-        [pltpu.VMEM((rows, 18 * CH), BF16)],
-        flops=2 * rows * 2304 * 512,
+        scratch(slots, 18 * CH),
+        flops=2 * slots * 2304 * 512,
     )
     xs, tiles = [hop(send, 0)], [htile, ctile]
-    inner = 2 * height(1) * stride
+    slots, packed = sizes(0, 1)
+    inner, outer = sizes(1, 0)[0], 2 * sizes(1, 1)[0]
     *state, first, second, h0, c0, h1, c1 = call(
         functools.partial(first_edge_kernel, BLOCKS),
         (lat, hid, cell, left, right, far, near, w, b, mask, htile),
         [VMEM] * 11,
-        [vm((rows, width), F32) for rows in (inner, 2 * edge) for width in (4 * CH, CH)]
-        + [vm((edge, CH), BF16)] * 2
+        [vm((rows, width), F32) for rows in (inner, outer) for width in (4 * CH, CH)]
+        + [vm((packed, CH), BF16)] * 2
         + tiles_of(0, 1) * 2,
         [VMEM] * 10,
-        [pltpu.VMEM((2 * edge + inner, 18 * CH), BF16)],
-        flops=4 * edge * 2304 * 512,
+        scratch(max(2 * slots, outer + inner), 18 * CH, 640),
+        flops=4 * slots * 2304 * 512,
     )
     state = (state[:2], state[2:])
     xs += [hop(first, 0), hop(second, 0)]
@@ -470,21 +519,22 @@
     ]
     for tick in range(1, LAYERS):
         last = tick == LAYERS - 1
-        rows = 2 * height(tick) * stride
+        slots, packed = sizes(tick, 0)
         result = call(
             functools.partial(next_middle_kernel, tick, BLOCKS),
             (xs[0], *state[0], win, mask),
             [VMEM] * 5,
-            ([] if last else [vm((rows, CH), BF16)]) + tiles_of(tick, 0),
+            ([] if last else [vm((packed, CH), BF16)]) + tiles_of(tick, 0),
             [VMEM] * (2 if last else 3),
-            [pltpu.VMEM((rows, 9 * CH), BF16)],
-            flops=2 * rows * 1152 * 512,
+            scratch(slots, 9 * CH),
+            flops=2 * slots * 1152 * 512,
         )
+        slots, packed = sizes(tick, 1)
         mine = list(result[-2:])
         nxt = [] if last else [hop(result[0], tick)]
         for batch in range(2):
             ins = (xs[1 + batch], xs[0], *state[1], win, mask)
-            cols = pltpu.VMEM((edge, 9 * CH), BF16)
+            scr = scratch(slots, 9 * CH, 320)
             if last:
                 done = tuple(mine) if batch == 0 else ()
                 count = len(ins) + len(done)
@@ -494,19 +544,19 @@
                     [VMEM] * count + [ANY] * 2,
                     out_shapes,
                     [ANY, ANY],
-                    [cols] + tiles_of(tick, 1) + [pltpu.SemaphoreType.DMA((6,))],
+                    scr + tiles_of(tick, 1) + [pltpu.SemaphoreType.DMA((6,))],
                     aliases={count: 0, count + 1: 1},
-                    flops=2 * edge * 1152 * 512,
+                    flops=2 * slots * 1152 * 512,
                 )
                 continue
             send, *result = call(
                 functools.partial(next_edge_kernel, tick, batch, BLOCKS),
                 ins,
                 [VMEM] * len(ins),
-                [vm((edge, CH), BF16)] + tiles_of(tick, 1),
+                [vm((packed, CH), BF16)] + tiles_of(tick, 1),
                 [VMEM] * 3,
-                [cols],
-                flops=2 * edge * 1152 * 512,
+                scr,
+                flops=2 * slots * 1152 * 512,
                 after=mine[-2],
             )
             mine += result

time: 43.1 us -> 42.7 us (level)
  no operation moved by 1% of the time
where the time goes in v5:
time: 42.7 us; the launch traced here: 42.3 us
  starting transfers between devices  20.3 us (48%)
  waiting for transfers between devices  13.5 us (32%)
  Pallas kernels  7.51 us (18%)
  between operations  0.89 us (2%)
    ppermute x9, waiting for transfers between devices, hop(): return lax.ppermute(v, 'section', [(tick, tick + 1)])  10.4 us
    ppermute x9, starting transfers between devices, hop(): return lax.ppermute(v, 'section', [(tick, tick + 1)])  7.87 us
    pallas_call x15, Pallas kernels, call(): pl.pallas_call(body, out_shape=tuple(outs), in_specs=in_specs, out_specs=...  7.51 us
    ppermute x1, starting transfers between devices, on_device(): left = lax.ppermute(left, 'col', both(odd(n_col)))  5.04 us
    ppermute x1, starting transfers between devices, on_device(): near = lax.ppermute(near, 'row', both(even(n_row)))  3.59 us
    ppermute x1, waiting for transfers between devices, on_device(): right = lax.ppermute(right, 'col', both(even(n_col)))  2.8 us
    ppermute x1, starting transfers between devices, on_device(): right = lax.ppermute(right, 'col', both(even(n_col)))  1.92 us
    ppermute x1, starting transfers between devices, on_device(): far = lax.ppermute(far, 'row', both(odd(n_row)))  1.92 us
  transfers between devices with their start and end apart: 13, of which 5 were waited for; matrix products, arithmetic and copies ran while one was open for 0% of the time, Pallas kernels for 12%

profile of v5, /device:TPU:110, one launch (start us, length us, event | category | flops | bytes accessed | tf_op | source)
XLA Modules:
  0.0 42.3 jit_solution(14831826747218660117)
XLA Ops:
  0.6 1.1 %shard_map.68 = (bf16[2,16,16,128]{3,2,1,0:T(8,128)(2,1)S(1)}, bf16[2,16,16,128]{3,2,1,0:T(8,128)(2,1)S(1)}, f32[2,16,16,128]{3,2,1,0:T(8,128)S(1)}, bf16[128,384]{1,0:T(8,128)(2,1)S(1)}, bf16[128,384]{1,0:T(8,128)(2,1)S(1)}) custom-call(bf16[2,16,16,128]{3,2,1,0:T(8,128)(2,1)} %lat_hbm.1, bf16[2,16,16,128]{3,2,1,0:T(8,128)(2,1)} %bitcast.4, ...), custom_call_target="tpu_custom_call" | custom-call | bytes 1048576 | tf_op jit(solution)/shard_map/pallas_call | solution.py:48
  1.8 5.0 %collective-permute-start = (bf16[128,384]{1,0:T(8,128)(2,1)S(1)}, bf16[128,384]{1,0:T(8,128)(2,1)S(1)}, u32[]{:S(2)}, u32[]{:S(2)}) collective-permute-start(bf16[128,384]{1,0:T(8,128)(2,1)S(1)} %get-tuple-element.53), channel_id=1, source_target_pairs={{1,2},{3,4},{5,6},{7,8},{9,10},{11,12},{13,14},{2,1},{4,3},{6,5},{... | collective-permute-start | bytes 294920 | tf_op jit(solution)/shard_map/ppermute | solution.py:464
  6.8 1.9 %collective-permute-start.1 = (bf16[128,384]{1,0:T(8,128)(2,1)S(1)}, bf16[128,384]{1,0:T(8,128)(2,1)S(1)}, u32[]{:S(2)}, u32[]{:S(2)}) collective-permute-start(bf16[128,384]{1,0:T(8,128)(2,1)S(1)} %get-tuple-element.54._), channel_id=1, source_target_pairs={{0,1},{2,3},{4,5},{6,7},{8,9},{10,11},{12,13},{14,15},{1,0},{3,2},... | collective-permute-start | bytes 294920 | tf_op jit(solution)/shard_map/ppermute | solution.py:465
  8.8 1.8 %shard_map.69 = (bf16[2304,512]{1,0:T(8,128)(2,1)S(1)}, f32[1,512]{1,0:T(1,128)S(1)}, bf16[1152,512]{1,0:T(8,128)(2,1)S(1)}, f32[504,128]{1,0:T(8,128)S(1)}) custom-call(bf16[128,384]{1,0:T(8,128)(2,1)S(1)} %get-tuple-element.54._, bf16[2304,512]{1,0:T(8,128)(2,1)} %bitcast.5, f32[1,512]{1,0:T(1,128)} %b_hbm.1), custom_call_target="tpu_custom_call" | custom-call | flops 2147483648 | bytes 1048576 | tf_op jit(solution)/shard_map/pallas_call | solution.py:48
  10.5 0.0 collective-permute-done.left_ref
  10.5 2.8 %collective-permute-done.1.right_ref = bf16[128,384]{1,0:T(8,128)(2,1)S(1)} collective-permute-done((bf16[128,384]{1,0:T(8,128)(2,1)S(1)}, bf16[128,384]{1,0:T(8,128)(2,1)S(1)}, u32[]{:S(2)}, u32[]{:S(2)}) %collective-permute-start.1) | collective-permute-done | bytes 98336 | tf_op jit(solution)/shard_map/ppermute | solution.py:465
  13.3 0.1 shard_map.70
  13.5 1.9 %collective-permute-start.2 = (bf16[208,384]{1,0:T(8,128)(2,1)S(1)}, bf16[208,384]{1,0:T(8,128)(2,1)S(1)}, u32[]{:S(2)}, u32[]{:S(2)}) collective-permute-start(bf16[208,384]{1,0:T(8,128)(2,1)S(1)} %get-tuple-element.56), channel_id=1, source_target_pairs={{16,32},{48,64},{80,96},{32,16},{64,48},{96,80},{17,33},{49,65},{8... | collective-permute-start | bytes 479240 | tf_op jit(solution)/shard_map/ppermute | solution.py:470
  15.4 3.6 %collective-permute-start.3 = (bf16[208,384]{1,0:T(8,128)(2,1)S(1)}, bf16[208,384]{1,0:T(8,128)(2,1)S(1)}, u32[]{:S(2)}, u32[]{:S(2)}) collective-permute-start(bf16[208,384]{1,0:T(8,128)(2,1)S(1)} %get-tuple-element.57), channel_id=1, source_target_pairs={{0,16},{32,48},{64,80},{96,112},{16,0},{48,32},{80,64},{112,96},{1... | collective-permute-start | bytes 479240 | tf_op jit(solution)/shard_map/ppermute | solution.py:471
  19.0 0.7 %collective-permute-start.5 = (bf16[448,128]{1,0:T(8,128)(2,1)S(1)}, bf16[448,128]{1,0:T(8,128)(2,1)S(1)}, u32[]{:S(2)}, u32[]{:S(2)}) collective-permute-start(bf16[448,128]{1,0:T(8,128)(2,1)S(1)} %get-tuple-element.62), channel_id=1, source_target_pairs={{0,128},{1,129},{2,130},{3,131},{4,132},{5,133},{6,134},{7,135},{8... | collective-permute-start | bytes 344072 | tf_op jit(solution)/shard_map/ppermute | solution.py:486
  19.7 0.4 collective-permute-done.2.far_ref
  20.1 0.0 collective-permute-done.3.near_ref
  20.1 1.2 %shard_map.72 = (f32[352,512]{1,0:T(8,128)S(1)}, f32[352,128]{1,0:T(8,128)S(1)}, f32[576,512]{1,0:T(8,128)S(1)}, f32[576,128]{1,0:T(8,128)S(1)}, bf16[272,128]{1...) custom-call(bf16[2,16,16,128]{3,2,1,0:T(8,128)(2,1)S(1)} %get-tuple-, ...), custom_call_target="tpu_custom_call" | custom-call | flops 1358954496 | bytes 1048576 | tf_op jit(solution)/shard_map/pallas_call | solution.py:48
  21.2 0.7 %collective-permute-start.6 = (bf16[272,128]{1,0:T(8,128)(2,1)S(1)}, bf16[272,128]{1,0:T(8,128)(2,1)S(1)}, u32[]{:S(2)}, u32[]{:S(2)}) collective-permute-start(bf16[272,128]{1,0:T(8,128)(2,1)S(1)} %get-tuple-element.66), channel_id=1, source_target_pairs={{0,128},{1,129},{2,130},{3,131},{4,132},{5,133},{6,134},{7,135},{8... | collective-permute-start | bytes 208904 | tf_op jit(solution)/shard_map/ppermute | solution.py:486
  21.9 0.7 %collective-permute-start.4 = (bf16[272,128]{1,0:T(8,128)(2,1)S(1)}, bf16[272,128]{1,0:T(8,128)(2,1)S(1)}, u32[]{:S(2)}, u32[]{:S(2)}) collective-permute-start(bf16[272,128]{1,0:T(8,128)(2,1)S(1)} %get-tuple-element.61), channel_id=1, source_target_pairs={{0,128},{1,129},{2,130},{3,131},{4,132},{5,133},{6,134},{7,135},{8... | collective-permute-start | bytes 208904 | tf_op jit(solution)/shard_map/ppermute | solution.py:486
  22.6 0.0 collective-permute-done.5.x_ref.refs_1_
  22.6 0.7 %collective-permute-start.8 = (bf16[320,128]{1,0:T(8,128)(2,1)S(1)}, bf16[320,128]{1,0:T(8,128)(2,1)S(1)}, u32[]{:S(2)}, u32[]{:S(2)}) collective-permute-start(bf16[320,128]{1,0:T(8,128)(2,1)S(1)} %get-tuple-element.72), channel_id=1, source_target_pairs={{128,256},{129,257},{130,258},{131,259},{132,260},{133,261},{134,2... | collective-permute-start | bytes 245768 | tf_op jit(solution)/shard_map/ppermute | solution.py:486
  23.3 0.0 collective-permute-done.6.refs_0_
  23.3 0.7 %collective-permute-start.9 = (bf16[240,128]{1,0:T(8,128)(2,1)S(1)}, bf16[240,128]{1,0:T(8,128)(2,1)S(1)}, u32[]{:S(2)}, u32[]{:S(2)}) collective-permute-start(bf16[240,128]{1,0:T(8,128)(2,1)S(1)} %get-tuple-element.73), channel_id=1, source_target_pairs={{128,256},{129,257},{130,258},{131,259},{132,260},{133,261},{134,2... | collective-permute-start | bytes 184328 | tf_op jit(solution)/shard_map/ppermute | solution.py:486
  24.0 0.0 collective-permute-done.4.refs_0_
  24.0 0.7 %collective-permute-start.7 = (bf16[240,128]{1,0:T(8,128)(2,1)S(1)}, bf16[240,128]{1,0:T(8,128)(2,1)S(1)}, u32[]{:S(2)}, u32[]{:S(2)}) collective-permute-start(bf16[240,128]{1,0:T(8,128)(2,1)S(1)} %get-tuple-element.71), channel_id=1, source_target_pairs={{128,256},{129,257},{130,258},{131,259},{132,260},{133,261},{134,2... | collective-permute-start | bytes 184328 | tf_op jit(solution)/shard_map/ppermute | solution.py:486
  24.7 0.0 collective-permute-done.8.x_ref.refs_1_
  24.8 1.3 %collective-permute-start.11 = (bf16[224,128]{1,0:T(8,128)(2,1)S(1)}, bf16[224,128]{1,0:T(8,128)(2,1)S(1)}, u32[]{:S(2)}, u32[]{:S(2)}) collective-permute-start(bf16[224,128]{1,0:T(8,128)(2,1)S(1)} %get-tuple-element.77), channel_id=1, source_target_pairs={{256,384},{257,385},{258,386},{259,387},{260,388},{261,389},{262,3... | collective-permute-start | bytes 172040 | tf_op jit(solution)/shard_map/ppermute | solution.py:486
  26.1 0.0 collective-permute-done.9.refs_0_
  26.1 1.3 %collective-permute-start.12 = (bf16[224,128]{1,0:T(8,128)(2,1)S(1)}, bf16[224,128]{1,0:T(8,128)(2,1)S(1)}, u32[]{:S(2)}, u32[]{:S(2)}) collective-permute-start(bf16[224,128]{1,0:T(8,128)(2,1)S(1)} %get-tuple-element.78), channel_id=1, source_target_pairs={{256,384},{257,385},{258,386},{259,387},{260,388},{261,389},{262,3... | collective-permute-start | bytes 172040 | tf_op jit(solution)/shard_map/ppermute | solution.py:486
  27.4 0.0 collective-permute-done.7.refs_0_
  27.4 1.3 %collective-permute-start.10 = (bf16[224,128]{1,0:T(8,128)(2,1)S(1)}, bf16[224,128]{1,0:T(8,128)(2,1)S(1)}, u32[]{:S(2)}, u32[]{:S(2)}) collective-permute-start(bf16[224,128]{1,0:T(8,128)(2,1)S(1)} %get-tuple-element.76), channel_id=1, source_target_pairs={{256,384},{257,385},{258,386},{259,387},{260,388},{261,389},{262,3... | collective-permute-start | bytes 172040 | tf_op jit(solution)/shard_map/ppermute | solution.py:486
  28.7 0.2 shard_map.80
  28.9 7.4 %collective-permute-done.11.x_ref.inner_ref = bf16[224,128]{1,0:T(8,128)(2,1)S(1)} collective-permute-done((bf16[224,128]{1,0:T(8,128)(2,1)S(1)}, bf16[224,128]{1,0:T(8,128)(2,1)S(1)}, u32[]{:S(2)}, u32[]{:S(2)}) %collective-permute-start.11) | collective-permute-done | bytes 57376 | tf_op jit(solution)/shard_map/ppermute | solution.py:486
  36.3 0.5 %shard_map.79 = (bf16[2,4,16,128]{3,2,1,0:T(8,128)(2,1)S(1)}, f32[2,4,16,128]{3,2,1,0:T(8,128)S(1)}) custom-call(bf16[224,128]{1,0:T(8,128)(2,1)S(1)} %collective-permute-done.11.x_ref.inner_ref, f32[352,512]{1,0:T(8,128)S(1)} %get-tuple-element.67.part_ref, f32[352,128]{1,0:T(8,128)S(1)} %get-tuple-element.68.prev_ref, ...), custom_call_target="tpu_custom_call" | custom-call | flops 188743680 | bytes 1048576 | tf_op jit(solution)/shard_map/pallas_call | solution.py:48
  36.8 2.2 %collective-permute-done.12.x_ref = bf16[224,128]{1,0:T(8,128)(2,1)S(1)} collective-permute-done((bf16[224,128]{1,0:T(8,128)(2,1)S(1)}, bf16[224,128]{1,0:T(8,128)(2,1)S(1)}, u32[]{:S(2)}, u32[]{:S(2)}) %collective-permute-start.12) | collective-permute-done | bytes 57376 | tf_op jit(solution)/shard_map/ppermute | solution.py:486
  39.0 1.3 %shard_map.81 = (bf16[1,2,16,16,128]{4,3,2,1,0:T(8,128)(2,1)}, f32[1,2,16,16,128]{4,3,2,1,0:T(8,128)}) custom-call(bf16[224,128]{1,0:T(8,128)(2,1)S(1)} %collective-permute-done.12.x_ref, bf16[224,128]{1,0:T(8,128)(2,1)S(1)} %collective-permute-done.11.x_ref.inner_ref, ...), custom_call_target="tpu_custom_call", output_to_operand_aliasing={{0}: (8, {}), {1}: (9, {})} | custom-call | flops 264241152 | bytes 1048576 | tf_op jit(solution)/shard_map/pallas_call | solution.py:48
  40.3 0.7 %collective-permute-done.10.x_ref = bf16[224,128]{1,0:T(8,128)(2,1)S(1)} collective-permute-done((bf16[224,128]{1,0:T(8,128)(2,1)S(1)}, bf16[224,128]{1,0:T(8,128)(2,1)S(1)}, u32[]{:S(2)}, u32[]{:S(2)}) %collective-permute-start.10) | collective-permute-done | bytes 57376 | tf_op jit(solution)/shard_map/ppermute | solution.py:486
  41.0 1.3 %shard_map.82 = (bf16[1,2,16,16,128]{4,3,2,1,0:T(8,128)(2,1)}, f32[1,2,16,16,128]{4,3,2,1,0:T(8,128)}) custom-call(bf16[224,128]{1,0:T(8,128)(2,1)S(1)} %collective-permute-done.10.x_ref, bf16[224,128]{1,0:T(8,128)(2,1)S(1)} %collective-permute-done.11.x_ref.inner_ref, ...), custom_call_target="tpu_custom_call", output_to_operand_aliasing={{0}: (6, {}), {1}: (7, {})} | custom-call | flops 264241152 | bytes 1048576 | tf_op jit(solution)/shard_map/pallas_call | solution.py:48
  (7 shorter events, 0.1 us)
Async XLA Ops:
  1.8 8.7 %collective-permute-start = (bf16[128,384]{1,0:T(8,128)(2,1)S(1)}, bf16[128,384]{1,0:T(8,128)(2,1)S(1)}, u32[]{:S(2)}, u32[]{:S(2)}) collective-permute-start(bf16[128,384]{1,0:T(8,128)(2,1)S(1)} %get-tuple-element.53), channel_id=1, source_target_pairs={{1,2},{3,4},{5,6},{7,8},{9,10},{11,12},{13,14},{2,1},{4,3},{6,5},{... | collective-permute-start | bytes 294920 | tf_op jit(solution)/shard_map/ppermute | solution.py:464
  6.8 6.5 %collective-permute-start.1 = (bf16[128,384]{1,0:T(8,128)(2,1)S(1)}, bf16[128,384]{1,0:T(8,128)(2,1)S(1)}, u32[]{:S(2)}, u32[]{:S(2)}) collective-permute-start(bf16[128,384]{1,0:T(8,128)(2,1)S(1)} %get-tuple-element.54._), channel_id=1, source_target_pairs={{0,1},{2,3},{4,5},{6,7},{8,9},{10,11},{12,13},{14,15},{1,0},{3,2},... | collective-permute-start | bytes 294920 | tf_op jit(solution)/shard_map/ppermute | solution.py:465
  13.5 6.6 %collective-permute-start.2 = (bf16[208,384]{1,0:T(8,128)(2,1)S(1)}, bf16[208,384]{1,0:T(8,128)(2,1)S(1)}, u32[]{:S(2)}, u32[]{:S(2)}) collective-permute-start(bf16[208,384]{1,0:T(8,128)(2,1)S(1)} %get-tuple-element.56), channel_id=1, source_target_pairs={{16,32},{48,64},{80,96},{32,16},{64,48},{96,80},{17,33},{49,65},{8... | collective-permute-start | bytes 479240 | tf_op jit(solution)/shard_map/ppermute | solution.py:470
  15.4 4.7 %collective-permute-start.3 = (bf16[208,384]{1,0:T(8,128)(2,1)S(1)}, bf16[208,384]{1,0:T(8,128)(2,1)S(1)}, u32[]{:S(2)}, u32[]{:S(2)}) collective-permute-start(bf16[208,384]{1,0:T(8,128)(2,1)S(1)} %get-tuple-element.57), channel_id=1, source_target_pairs={{0,16},{32,48},{64,80},{96,112},{16,0},{48,32},{80,64},{112,96},{1... | collective-permute-start | bytes 479240 | tf_op jit(solution)/shard_map/ppermute | solution.py:471
  19.0 3.6 %collective-permute-start.5 = (bf16[448,128]{1,0:T(8,128)(2,1)S(1)}, bf16[448,128]{1,0:T(8,128)(2,1)S(1)}, u32[]{:S(2)}, u32[]{:S(2)}) collective-permute-start(bf16[448,128]{1,0:T(8,128)(2,1)S(1)} %get-tuple-element.62), channel_id=1, source_target_pairs={{0,128},{1,129},{2,130},{3,131},{4,132},{5,133},{6,134},{7,135},{8... | collective-permute-start | bytes 344072 | tf_op jit(solution)/shard_map/ppermute | solution.py:486
  21.2 2.1 %collective-permute-start.6 = (bf16[272,128]{1,0:T(8,128)(2,1)S(1)}, bf16[272,128]{1,0:T(8,128)(2,1)S(1)}, u32[]{:S(2)}, u32[]{:S(2)}) collective-permute-start(bf16[272,128]{1,0:T(8,128)(2,1)S(1)} %get-tuple-element.66), channel_id=1, source_target_pairs={{0,128},{1,129},{2,130},{3,131},{4,132},{5,133},{6,134},{7,135},{8... | collective-permute-start | bytes 208904 | tf_op jit(solution)/shard_map/ppermute | solution.py:486
  21.9 2.1 %collective-permute-start.4 = (bf16[272,128]{1,0:T(8,128)(2,1)S(1)}, bf16[272,128]{1,0:T(8,128)(2,1)S(1)}, u32[]{:S(2)}, u32[]{:S(2)}) collective-permute-start(bf16[272,128]{1,0:T(8,128)(2,1)S(1)} %get-tuple-element.61), channel_id=1, source_target_pairs={{0,128},{1,129},{2,130},{3,131},{4,132},{5,133},{6,134},{7,135},{8... | collective-permute-start | bytes 208904 | tf_op jit(solution)/shard_map/ppermute | solution.py:486
  22.6 2.1 %collective-permute-start.8 = (bf16[320,128]{1,0:T(8,128)(2,1)S(1)}, bf16[320,128]{1,0:T(8,128)(2,1)S(1)}, u32[]{:S(2)}, u32[]{:S(2)}) collective-permute-start(bf16[320,128]{1,0:T(8,128)(2,1)S(1)} %get-tuple-element.72), channel_id=1, source_target_pairs={{128,256},{129,257},{130,258},{131,259},{132,260},{133,261},{134,2... | collective-permute-start | bytes 245768 | tf_op jit(solution)/shard_map/ppermute | solution.py:486
  23.3 2.7 %collective-permute-start.9 = (bf16[240,128]{1,0:T(8,128)(2,1)S(1)}, bf16[240,128]{1,0:T(8,128)(2,1)S(1)}, u32[]{:S(2)}, u32[]{:S(2)}) collective-permute-start(bf16[240,128]{1,0:T(8,128)(2,1)S(1)} %get-tuple-element.73), channel_id=1, source_target_pairs={{128,256},{129,257},{130,258},{131,259},{132,260},{133,261},{134,2... | collective-permute-start | bytes 184328 | tf_op jit(solution)/shard_map/ppermute | solution.py:486
  24.0 3.3 %collective-permute-start.7 = (bf16[240,128]{1,0:T(8,128)(2,1)S(1)}, bf16[240,128]{1,0:T(8,128)(2,1)S(1)}, u32[]{:S(2)}, u32[]{:S(2)}) collective-permute-start(bf16[240,128]{1,0:T(8,128)(2,1)S(1)} %get-tuple-element.71), channel_id=1, source_target_pairs={{128,256},{129,257},{130,258},{131,259},{132,260},{133,261},{134,2... | collective-permute-start | bytes 184328 | tf_op jit(solution)/shard_map/ppermute | solution.py:486
  24.8 11.6 %collective-permute-start.11 = (bf16[224,128]{1,0:T(8,128)(2,1)S(1)}, bf16[224,128]{1,0:T(8,128)(2,1)S(1)}, u32[]{:S(2)}, u32[]{:S(2)}) collective-permute-start(bf16[224,128]{1,0:T(8,128)(2,1)S(1)} %get-tuple-element.77), channel_id=1, source_target_pairs={{256,384},{257,385},{258,386},{259,387},{260,388},{261,389},{262,3... | collective-permute-start | bytes 172040 | tf_op jit(solution)/shard_map/ppermute | solution.py:486
  26.1 12.9 %collective-permute-start.12 = (bf16[224,128]{1,0:T(8,128)(2,1)S(1)}, bf16[224,128]{1,0:T(8,128)(2,1)S(1)}, u32[]{:S(2)}, u32[]{:S(2)}) collective-permute-start(bf16[224,128]{1,0:T(8,128)(2,1)S(1)} %get-tuple-element.78), channel_id=1, source_target_pairs={{256,384},{257,385},{258,386},{259,387},{260,388},{261,389},{262,3... | collective-permute-start | bytes 172040 | tf_op jit(solution)/shard_map/ppermute | solution.py:486
  27.4 13.6 %collective-permute-start.10 = (bf16[224,128]{1,0:T(8,128)(2,1)S(1)}, bf16[224,128]{1,0:T(8,128)(2,1)S(1)}, u32[]{:S(2)}, u32[]{:S(2)}) collective-permute-start(bf16[224,128]{1,0:T(8,128)(2,1)S(1)} %get-tuple-element.76), channel_id=1, source_target_pairs={{256,384},{257,385},{258,386},{259,387},{260,388},{261,389},{262,3... | collective-permute-start | bytes 172040 | tf_op jit(solution)/shard_map/ppermute | solution.py:486

commit v6 on v5

--- a/solution.py
+++ b/solution.py
@@ -269,9 +269,9 @@
     return above[:96], first, mid, last, below[8:]
 
 
-def first_edge_kernel(blocks, lat_ref, hid_ref, cell_ref, left_ref, right_ref, far_ref, near_ref,
-                      w_ref, b_ref, m_ref, _, mid_part_ref, mid_prev_ref, part_ref, prev_ref, *rest):
-    sends, tiles, (cols, h_scr, c_scr, out_scr) = rest[:2], rest[2:6], rest[6:]
+def first_edge_kernel(batch, blocks, lat_ref, hid_ref, cell_ref, left_ref, right_ref, far_ref, near_ref,
+                      w_ref, b_ref, m_ref, _, *rest):
+    send_ref, htile_ref, ctile_ref, cols, h_scr, c_scr, out_scr = rest[-7:]
     tile = lat_ref.shape[1]
     wide = tile + 8
     size = EDGE * wide
@@ -283,23 +283,23 @@
     @pl.when(lax.axis_index("section") == 0)
     def _():
         starts = (0, (tile + 6 - EDGE) * wide)
-        prev = []
-        for batch in range(2):
-            for k, ref in enumerate((lat_ref, hid_ref)):
-                whole = full(batch, k, ref)
-                for half, start in enumerate(starts):
-                    src = whole[start : min(start + size + 3 * wide, whole.shape[0])]
-                    taps(src, WIDE, cols, size, wide, 2 * CH, k * CH, (2 * batch + half) * size)
-            state = rolled(full(batch, 2, cell_ref), WIDE + 1)
-            prev += [state[start + wide : start + wide + size] for start in starts]
-        h, c = updated(cols.at[: 4 * size], blocks, w_ref, b_ref[...], jnp.concatenate(prev))
-        h_scr[: 4 * size, :] = h
-        c_scr[: 4 * size, :] = c
-        for batch in range(2):
-            sent(tile, 0, 1, h_scr, 2 * batch * size, out_scr, sends[batch], m_ref)
-            kept(tile, 0, 1, h_scr, 2 * batch * size, tiles[2 * batch])
-            kept(tile, 0, 1, c_scr, 2 * batch * size, tiles[2 * batch + 1])
-
+        for k, ref in enumerate((lat_ref, hid_ref)):
+            whole = full(batch, k, ref)
+            for half, start in enumerate(starts):
+                src = whole[start : min(start + size + 3 * wide, whole.shape[0])]
+                taps(src, WIDE, cols, size, wide, 2 * CH, k * CH, half * size)
+        state = rolled(full(batch, 2, cell_ref), WIDE + 1)
+        prev = [state[start + wide : start + wide + size] for start in starts]
+        h, c = updated(cols.at[: 2 * size], blocks, w_ref, b_ref[...], jnp.concatenate(prev))
+        h_scr[: 2 * size, :] = h
+        c_scr[: 2 * size, :] = c
+        sent(tile, 0, 1, h_scr, 0, out_scr, send_ref, m_ref)
+        kept(tile, 0, 1, h_scr, 0, htile_ref)
+        kept(tile, 0, 1, c_scr, 0, ctile_ref)
+
+    if batch == 0:
+        return
+    mid_part_ref, mid_prev_ref, part_ref, prev_ref = rest[:4]
     for s in range(1, LAYERS):
 
         @pl.when(lax.axis_index("section") == s)
@@ -498,20 +498,20 @@
     xs, tiles = [hop(send, 0)], [htile, ctile]
     slots, packed = sizes(0, 1)
     inner, outer = sizes(1, 0)[0], 2 * sizes(1, 1)[0]
-    *state, first, second, h0, c0, h1, c1 = call(
-        functools.partial(first_edge_kernel, BLOCKS),
-        (lat, hid, cell, left, right, far, near, w, b, mask, htile),
-        [VMEM] * 11,
-        [vm((rows, width), F32) for rows in (inner, outer) for width in (4 * CH, CH)]
-        + [vm((packed, CH), BF16)] * 2
-        + tiles_of(0, 1) * 2,
-        [VMEM] * 10,
-        scratch(max(2 * slots, outer + inner), 18 * CH, 640),
-        flops=4 * slots * 2304 * 512,
-    )
+    for batch in range(2):
+        extra = [vm((rows, width), F32) for rows in (inner, outer) for width in (4 * CH, CH)] if batch else []
+        *state, send, htile, ctile = call(
+            functools.partial(first_edge_kernel, batch, BLOCKS),
+            (lat, hid, cell, left, right, far, near, w, b, mask, htile),
+            [VMEM] * 11,
+            extra + [vm((packed, CH), BF16)] + tiles_of(0, 1),
+            [VMEM] * (3 + len(extra)),
+            scratch(max(slots, outer + inner), 18 * CH, 640),
+            flops=2 * slots * 2304 * 512,
+        )
+        xs.append(hop(send, 0))
+        tiles += [htile, ctile]
     state = (state[:2], state[2:])
-    xs += [hop(first, 0), hop(second, 0)]
-    tiles += [h0, c0, h1, c1]
 
     out_shapes = [
         jax.ShapeDtypeStruct((1, 2, tile, tile, CH), BF16),

time: 42.7 us -> 42.1 us (0.986)
  the two profiles are of different devices: /device:TPU:110 before, /device:TPU:230 now
where the time goes in v6:
time: 42.1 us; the launch traced here: 41.7 us
  starting transfers between devices  20.3 us (48%)
  waiting for transfers between devices  12.9 us (31%)
  Pallas kernels  7.54 us (18%)
  between operations  0.9 us (2%)
    ppermute x9, waiting for transfers between devices, hop(): return lax.ppermute(v, 'section', [(tick, tick + 1)])  9.83 us
    ppermute x9, starting transfers between devices, hop(): return lax.ppermute(v, 'section', [(tick, tick + 1)])  7.86 us
    pallas_call x16, Pallas kernels, call(): pl.pallas_call(body, out_shape=tuple(outs), in_specs=in_specs, out_specs=...  7.54 us
    ppermute x1, starting transfers between devices, on_device(): left = lax.ppermute(left, 'col', both(odd(n_col)))  5.04 us
    ppermute x1, starting transfers between devices, on_device(): near = lax.ppermute(near, 'row', both(even(n_row)))  4.84 us
    ppermute x1, waiting for transfers between devices, on_device(): right = lax.ppermute(right, 'col', both(even(n_col)))  2.8 us
    ppermute x1, starting transfers between devices, on_device(): right = lax.ppermute(right, 'col', both(even(n_col)))  1.92 us
  transfers between devices with their start and end apart: 13, of which 5 were waited for; matrix products, arithmetic and copies ran while one was open for 0% of the time, Pallas kernels for 12%

profile of v6, /device:TPU:230, one launch (start us, length us, event | category | flops | bytes accessed | tf_op | source)
XLA Modules:
  0.0 41.7 jit_solution(14716482532227516958)
XLA Ops:
  0.6 1.1 %shard_map.68 = (bf16[2,16,16,128]{3,2,1,0:T(8,128)(2,1)S(1)}, bf16[2,16,16,128]{3,2,1,0:T(8,128)(2,1)S(1)}, f32[2,16,16,128]{3,2,1,0:T(8,128)S(1)}, bf16[128,384]{1,0:T(8,128)(2,1)S(1)}, bf16[128,384]{1,0:T(8,128)(2,1)S(1)}) custom-call(bf16[2,16,16,128]{3,2,1,0:T(8,128)(2,1)} %lat_hbm.1, bf16[2,16,16,128]{3,2,1,0:T(8,128)(2,1)} %bitcast.4, ...), custom_call_target="tpu_custom_call" | custom-call | bytes 1048576 | tf_op jit(solution)/shard_map/pallas_call | solution.py:48
  1.8 5.0 %collective-permute-start = (bf16[128,384]{1,0:T(8,128)(2,1)S(1)}, bf16[128,384]{1,0:T(8,128)(2,1)S(1)}, u32[]{:S(2)}, u32[]{:S(2)}) collective-permute-start(bf16[128,384]{1,0:T(8,128)(2,1)S(1)} %get-tuple-element.53), channel_id=1, source_target_pairs={{1,2},{3,4},{5,6},{7,8},{9,10},{11,12},{13,14},{2,1},{4,3},{6,5},{... | collective-permute-start | bytes 294920 | tf_op jit(solution)/shard_map/ppermute | solution.py:464
  6.8 1.9 %collective-permute-start.1 = (bf16[128,384]{1,0:T(8,128)(2,1)S(1)}, bf16[128,384]{1,0:T(8,128)(2,1)S(1)}, u32[]{:S(2)}, u32[]{:S(2)}) collective-permute-start(bf16[128,384]{1,0:T(8,128)(2,1)S(1)} %get-tuple-element.54._), channel_id=1, source_target_pairs={{0,1},{2,3},{4,5},{6,7},{8,9},{10,11},{12,13},{14,15},{1,0},{3,2},... | collective-permute-start | bytes 294920 | tf_op jit(solution)/shard_map/ppermute | solution.py:465
  8.8 1.8 %shard_map.69 = (bf16[2304,512]{1,0:T(8,128)(2,1)S(1)}, f32[1,512]{1,0:T(1,128)S(1)}, bf16[1152,512]{1,0:T(8,128)(2,1)S(1)}, f32[504,128]{1,0:T(8,128)S(1)}) custom-call(bf16[128,384]{1,0:T(8,128)(2,1)S(1)} %get-tuple-element.54._, bf16[2304,512]{1,0:T(8,128)(2,1)} %bitcast.5, f32[1,512]{1,0:T(1,128)} %b_hbm.1), custom_call_target="tpu_custom_call" | custom-call | flops 2147483648 | bytes 1048576 | tf_op jit(solution)/shard_map/pallas_call | solution.py:48
  10.5 0.0 collective-permute-done.left_ref
  10.5 2.8 %collective-permute-done.1.right_ref = bf16[128,384]{1,0:T(8,128)(2,1)S(1)} collective-permute-done((bf16[128,384]{1,0:T(8,128)(2,1)S(1)}, bf16[128,384]{1,0:T(8,128)(2,1)S(1)}, u32[]{:S(2)}, u32[]{:S(2)}) %collective-permute-start.1) | collective-permute-done | bytes 98336 | tf_op jit(solution)/shard_map/ppermute | solution.py:465
  13.3 0.1 shard_map.70
  13.5 0.7 %collective-permute-start.2 = (bf16[208,384]{1,0:T(8,128)(2,1)S(1)}, bf16[208,384]{1,0:T(8,128)(2,1)S(1)}, u32[]{:S(2)}, u32[]{:S(2)}) collective-permute-start(bf16[208,384]{1,0:T(8,128)(2,1)S(1)} %get-tuple-element.56), channel_id=1, source_target_pairs={{16,32},{48,64},{80,96},{32,16},{64,48},{96,80},{17,33},{49,65},{8... | collective-permute-start | bytes 479240 | tf_op jit(solution)/shard_map/ppermute | solution.py:470
  14.2 4.8 %collective-permute-start.3 = (bf16[208,384]{1,0:T(8,128)(2,1)S(1)}, bf16[208,384]{1,0:T(8,128)(2,1)S(1)}, u32[]{:S(2)}, u32[]{:S(2)}) collective-permute-start(bf16[208,384]{1,0:T(8,128)(2,1)S(1)} %get-tuple-element.57), channel_id=1, source_target_pairs={{0,16},{32,48},{64,80},{96,112},{16,0},{48,32},{80,64},{112,96},{1... | collective-permute-start | bytes 479240 | tf_op jit(solution)/shard_map/ppermute | solution.py:471
  19.0 0.7 %collective-permute-start.5 = (bf16[448,128]{1,0:T(8,128)(2,1)S(1)}, bf16[448,128]{1,0:T(8,128)(2,1)S(1)}, u32[]{:S(2)}, u32[]{:S(2)}) collective-permute-start(bf16[448,128]{1,0:T(8,128)(2,1)S(1)} %get-tuple-element.63), channel_id=1, source_target_pairs={{0,128},{1,129},{2,130},{3,131},{4,132},{5,133},{6,134},{7,135},{8... | collective-permute-start | bytes 344072 | tf_op jit(solution)/shard_map/ppermute | solution.py:486
  19.7 0.0 collective-permute-done.2.far_ref
  19.7 0.3 collective-permute-done.3.near_ref
  20.0 0.7 %collective-permute-start.6 = (bf16[272,128]{1,0:T(8,128)(2,1)S(1)}, bf16[272,128]{1,0:T(8,128)(2,1)S(1)}, u32[]{:S(2)}, u32[]{:S(2)}) collective-permute-start(bf16[272,128]{1,0:T(8,128)(2,1)S(1)} %get-tuple-element.67), channel_id=1, source_target_pairs={{0,128},{1,129},{2,130},{3,131},{4,132},{5,133},{6,134},{7,135},{8... | collective-permute-start | bytes 208904 | tf_op jit(solution)/shard_map/ppermute | solution.py:486
  20.7 1.2 %shard_map.73 = (f32[352,512]{1,0:T(8,128)S(1)}, f32[352,128]{1,0:T(8,128)S(1)}, f32[576,512]{1,0:T(8,128)S(1)}, f32[576,128]{1,0:T(8,128)S(1)}, bf16[272,128]{1...) custom-call(bf16[2,16,16,128]{3,2,1,0:T(8,128)(2,1)S(1)} %get-tuple-element.50.lat_ref, ...), custom_call_target="tpu_custom_call" | custom-call | flops 679477248 | bytes 1048576 | tf_op jit(solution)/shard_map/pallas_call | solution.py:48
  21.9 0.7 %collective-permute-start.4 = (bf16[272,128]{1,0:T(8,128)(2,1)S(1)}, bf16[272,128]{1,0:T(8,128)(2,1)S(1)}, u32[]{:S(2)}, u32[]{:S(2)}) collective-permute-start(bf16[272,128]{1,0:T(8,128)(2,1)S(1)} %get-tuple-element.62), channel_id=1, source_target_pairs={{0,128},{1,129},{2,130},{3,131},{4,132},{5,133},{6,134},{7,135},{8... | collective-permute-start | bytes 208904 | tf_op jit(solution)/shard_map/ppermute | solution.py:486
  22.5 0.0 collective-permute-done.5.x_ref.refs_1_
  22.6 0.7 %collective-permute-start.8 = (bf16[320,128]{1,0:T(8,128)(2,1)S(1)}, bf16[320,128]{1,0:T(8,128)(2,1)S(1)}, u32[]{:S(2)}, u32[]{:S(2)}) collective-permute-start(bf16[320,128]{1,0:T(8,128)(2,1)S(1)} %get-tuple-element.73), channel_id=1, source_target_pairs={{128,256},{129,257},{130,258},{131,259},{132,260},{133,261},{134,2... | collective-permute-start | bytes 245768 | tf_op jit(solution)/shard_map/ppermute | solution.py:486
  23.2 0.0 collective-permute-done.6.refs_0_
  23.3 0.7 %collective-permute-start.9 = (bf16[240,128]{1,0:T(8,128)(2,1)S(1)}, bf16[240,128]{1,0:T(8,128)(2,1)S(1)}, u32[]{:S(2)}, u32[]{:S(2)}) collective-permute-start(bf16[240,128]{1,0:T(8,128)(2,1)S(1)} %get-tuple-element.74), channel_id=1, source_target_pairs={{128,256},{129,257},{130,258},{131,259},{132,260},{133,261},{134,2... | collective-permute-start | bytes 184328 | tf_op jit(solution)/shard_map/ppermute | solution.py:486
  24.0 0.0 collective-permute-done.4.refs_0_
  24.0 0.7 %collective-permute-start.7 = (bf16[240,128]{1,0:T(8,128)(2,1)S(1)}, bf16[240,128]{1,0:T(8,128)(2,1)S(1)}, u32[]{:S(2)}, u32[]{:S(2)}) collective-permute-start(bf16[240,128]{1,0:T(8,128)(2,1)S(1)} %get-tuple-element.72), channel_id=1, source_target_pairs={{128,256},{129,257},{130,258},{131,259},{132,260},{133,261},{134,2... | collective-permute-start | bytes 184328 | tf_op jit(solution)/shard_map/ppermute | solution.py:486
  24.7 0.0 collective-permute-done.8.x_ref.refs_1_
  24.7 1.3 %collective-permute-start.11 = (bf16[224,128]{1,0:T(8,128)(2,1)S(1)}, bf16[224,128]{1,0:T(8,128)(2,1)S(1)}, u32[]{:S(2)}, u32[]{:S(2)}) collective-permute-start(bf16[224,128]{1,0:T(8,128)(2,1)S(1)} %get-tuple-element.78), channel_id=1, source_target_pairs={{256,384},{257,385},{258,386},{259,387},{260,388},{261,389},{262,3... | collective-permute-start | bytes 172040 | tf_op jit(solution)/shard_map/ppermute | solution.py:486
  26.0 0.0 collective-permute-done.9.refs_0_
  26.0 1.3 %collective-permute-start.12 = (bf16[224,128]{1,0:T(8,128)(2,1)S(1)}, bf16[224,128]{1,0:T(8,128)(2,1)S(1)}, u32[]{:S(2)}, u32[]{:S(2)}) collective-permute-start(bf16[224,128]{1,0:T(8,128)(2,1)S(1)} %get-tuple-element.79), channel_id=1, source_target_pairs={{256,384},{257,385},{258,386},{259,387},{260,388},{261,389},{262,3... | collective-permute-start | bytes 172040 | tf_op jit(solution)/shard_map/ppermute | solution.py:486
  27.3 0.0 collective-permute-done.7.refs_0_
  27.4 1.3 %collective-permute-start.10 = (bf16[224,128]{1,0:T(8,128)(2,1)S(1)}, bf16[224,128]{1,0:T(8,128)(2,1)S(1)}, u32[]{:S(2)}, u32[]{:S(2)}) collective-permute-start(bf16[224,128]{1,0:T(8,128)(2,1)S(1)} %get-tuple-element.77), channel_id=1, source_target_pairs={{256,384},{257,385},{258,386},{259,387},{260,388},{261,389},{262,3... | collective-permute-start | bytes 172040 | tf_op jit(solution)/shard_map/ppermute | solution.py:486
  28.7 0.2 shard_map.81
  28.9 7.7 %collective-permute-done.11.x_ref.inner_ref = bf16[224,128]{1,0:T(8,128)(2,1)S(1)} collective-permute-done((bf16[224,128]{1,0:T(8,128)(2,1)S(1)}, bf16[224,128]{1,0:T(8,128)(2,1)S(1)}, u32[]{:S(2)}, u32[]{:S(2)}) %collective-permute-start.11) | collective-permute-done | bytes 57376 | tf_op jit(solution)/shard_map/ppermute | solution.py:486
  36.5 0.5 %shard_map.80 = (bf16[2,4,16,128]{3,2,1,0:T(8,128)(2,1)S(1)}, f32[2,4,16,128]{3,2,1,0:T(8,128)S(1)}) custom-call(bf16[224,128]{1,0:T(8,128)(2,1)S(1)} %collective-permute-done.11.x_ref.inner_ref, f32[352,512]{1,0:T(8,128)S(1)} %get-tuple-element.68.part_ref, f32[352,128]{1,0:T(8,128)S(1)} %get-tuple-element.69.prev_ref, ...), custom_call_target="tpu_custom_call" | custom-call | flops 188743680 | bytes 1048576 | tf_op jit(solution)/shard_map/pallas_call | solution.py:48
  37.0 1.5 %collective-permute-done.12.x_ref = bf16[224,128]{1,0:T(8,128)(2,1)S(1)} collective-permute-done((bf16[224,128]{1,0:T(8,128)(2,1)S(1)}, bf16[224,128]{1,0:T(8,128)(2,1)S(1)}, u32[]{:S(2)}, u32[]{:S(2)}) %collective-permute-start.12) | collective-permute-done | bytes 57376 | tf_op jit(solution)/shard_map/ppermute | solution.py:486
  38.5 1.3 %shard_map.82 = (bf16[1,2,16,16,128]{4,3,2,1,0:T(8,128)(2,1)}, f32[1,2,16,16,128]{4,3,2,1,0:T(8,128)}) custom-call(bf16[224,128]{1,0:T(8,128)(2,1)S(1)} %collective-permute-done.12.x_ref, bf16[224,128]{1,0:T(8,128)(2,1)S(1)} %collective-permute-done.11.x_ref.inner_ref, ...), custom_call_target="tpu_custom_call", output_to_operand_aliasing={{0}: (8, {}), {1}: (9, {})} | custom-call | flops 264241152 | bytes 1048576 | tf_op jit(solution)/shard_map/pallas_call | solution.py:48
  39.8 0.7 %collective-permute-done.10.x_ref = bf16[224,128]{1,0:T(8,128)(2,1)S(1)} collective-permute-done((bf16[224,128]{1,0:T(8,128)(2,1)S(1)}, bf16[224,128]{1,0:T(8,128)(2,1)S(1)}, u32[]{:S(2)}, u32[]{:S(2)}) %collective-permute-start.10) | collective-permute-done | bytes 57376 | tf_op jit(solution)/shard_map/ppermute | solution.py:486
  40.4 1.3 %shard_map.83 = (bf16[1,2,16,16,128]{4,3,2,1,0:T(8,128)(2,1)}, f32[1,2,16,16,128]{4,3,2,1,0:T(8,128)}) custom-call(bf16[224,128]{1,0:T(8,128)(2,1)S(1)} %collective-permute-done.10.x_ref, bf16[224,128]{1,0:T(8,128)(2,1)S(1)} %collective-permute-done.11.x_ref.inner_ref, ...), custom_call_target="tpu_custom_call", output_to_operand_aliasing={{0}: (6, {}), {1}: (7, {})} | custom-call | flops 264241152 | bytes 1048576 | tf_op jit(solution)/shard_map/pallas_call | solution.py:48
  (8 shorter events, 0.1 us)
Async XLA Ops:
  1.8 8.7 %collective-permute-start = (bf16[128,384]{1,0:T(8,128)(2,1)S(1)}, bf16[128,384]{1,0:T(8,128)(2,1)S(1)}, u32[]{:S(2)}, u32[]{:S(2)}) collective-permute-start(bf16[128,384]{1,0:T(8,128)(2,1)S(1)} %get-tuple-element.53), channel_id=1, source_target_pairs={{1,2},{3,4},{5,6},{7,8},{9,10},{11,12},{13,14},{2,1},{4,3},{6,5},{... | collective-permute-start | bytes 294920 | tf_op jit(solution)/shard_map/ppermute | solution.py:464
  6.8 6.5 %collective-permute-start.1 = (bf16[128,384]{1,0:T(8,128)(2,1)S(1)}, bf16[128,384]{1,0:T(8,128)(2,1)S(1)}, u32[]{:S(2)}, u32[]{:S(2)}) collective-permute-start(bf16[128,384]{1,0:T(8,128)(2,1)S(1)} %get-tuple-element.54._), channel_id=1, source_target_pairs={{0,1},{2,3},{4,5},{6,7},{8,9},{10,11},{12,13},{14,15},{1,0},{3,2},... | collective-permute-start | bytes 294920 | tf_op jit(solution)/shard_map/ppermute | solution.py:465
  13.5 6.2 %collective-permute-start.2 = (bf16[208,384]{1,0:T(8,128)(2,1)S(1)}, bf16[208,384]{1,0:T(8,128)(2,1)S(1)}, u32[]{:S(2)}, u32[]{:S(2)}) collective-permute-start(bf16[208,384]{1,0:T(8,128)(2,1)S(1)} %get-tuple-element.56), channel_id=1, source_target_pairs={{16,32},{48,64},{80,96},{32,16},{64,48},{96,80},{17,33},{49,65},{8... | collective-permute-start | bytes 479240 | tf_op jit(solution)/shard_map/ppermute | solution.py:470
  14.2 5.8 %collective-permute-start.3 = (bf16[208,384]{1,0:T(8,128)(2,1)S(1)}, bf16[208,384]{1,0:T(8,128)(2,1)S(1)}, u32[]{:S(2)}, u32[]{:S(2)}) collective-permute-start(bf16[208,384]{1,0:T(8,128)(2,1)S(1)} %get-tuple-element.57), channel_id=1, source_target_pairs={{0,16},{32,48},{64,80},{96,112},{16,0},{48,32},{80,64},{112,96},{1... | collective-permute-start | bytes 479240 | tf_op jit(solution)/shard_map/ppermute | solution.py:471
  19.0 3.5 %collective-permute-start.5 = (bf16[448,128]{1,0:T(8,128)(2,1)S(1)}, bf16[448,128]{1,0:T(8,128)(2,1)S(1)}, u32[]{:S(2)}, u32[]{:S(2)}) collective-permute-start(bf16[448,128]{1,0:T(8,128)(2,1)S(1)} %get-tuple-element.63), channel_id=1, source_target_pairs={{0,128},{1,129},{2,130},{3,131},{4,132},{5,133},{6,134},{7,135},{8... | collective-permute-start | bytes 344072 | tf_op jit(solution)/shard_map/ppermute | solution.py:486
  20.0 3.2 %collective-permute-start.6 = (bf16[272,128]{1,0:T(8,128)(2,1)S(1)}, bf16[272,128]{1,0:T(8,128)(2,1)S(1)}, u32[]{:S(2)}, u32[]{:S(2)}) collective-permute-start(bf16[272,128]{1,0:T(8,128)(2,1)S(1)} %get-tuple-element.67), channel_id=1, source_target_pairs={{0,128},{1,129},{2,130},{3,131},{4,132},{5,133},{6,134},{7,135},{8... | collective-permute-start | bytes 208904 | tf_op jit(solution)/shard_map/ppermute | solution.py:486
  21.9 2.1 %collective-permute-start.4 = (bf16[272,128]{1,0:T(8,128)(2,1)S(1)}, bf16[272,128]{1,0:T(8,128)(2,1)S(1)}, u32[]{:S(2)}, u32[]{:S(2)}) collective-permute-start(bf16[272,128]{1,0:T(8,128)(2,1)S(1)} %get-tuple-element.62), channel_id=1, source_target_pairs={{0,128},{1,129},{2,130},{3,131},{4,132},{5,133},{6,134},{7,135},{8... | collective-permute-start | bytes 208904 | tf_op jit(solution)/shard_map/ppermute | solution.py:486
  22.6 2.1 %collective-permute-start.8 = (bf16[320,128]{1,0:T(8,128)(2,1)S(1)}, bf16[320,128]{1,0:T(8,128)(2,1)S(1)}, u32[]{:S(2)}, u32[]{:S(2)}) collective-permute-start(bf16[320,128]{1,0:T(8,128)(2,1)S(1)} %get-tuple-element.73), channel_id=1, source_target_pairs={{128,256},{129,257},{130,258},{131,259},{132,260},{133,261},{134,2... | collective-permute-start | bytes 245768 | tf_op jit(solution)/shard_map/ppermute | solution.py:486
  23.3 2.7 %collective-permute-start.9 = (bf16[240,128]{1,0:T(8,128)(2,1)S(1)}, bf16[240,128]{1,0:T(8,128)(2,1)S(1)}, u32[]{:S(2)}, u32[]{:S(2)}) collective-permute-start(bf16[240,128]{1,0:T(8,128)(2,1)S(1)} %get-tuple-element.74), channel_id=1, source_target_pairs={{128,256},{129,257},{130,258},{131,259},{132,260},{133,261},{134,2... | collective-permute-start | bytes 184328 | tf_op jit(solution)/shard_map/ppermute | solution.py:486
  24.0 3.3 %collective-permute-start.7 = (bf16[240,128]{1,0:T(8,128)(2,1)S(1)}, bf16[240,128]{1,0:T(8,128)(2,1)S(1)}, u32[]{:S(2)}, u32[]{:S(2)}) collective-permute-start(bf16[240,128]{1,0:T(8,128)(2,1)S(1)} %get-tuple-element.72), channel_id=1, source_target_pairs={{128,256},{129,257},{130,258},{131,259},{132,260},{133,261},{134,2... | collective-permute-start | bytes 184328 | tf_op jit(solution)/shard_map/ppermute | solution.py:486
  24.7 11.8 %collective-permute-start.11 = (bf16[224,128]{1,0:T(8,128)(2,1)S(1)}, bf16[224,128]{1,0:T(8,128)(2,1)S(1)}, u32[]{:S(2)}, u32[]{:S(2)}) collective-permute-start(bf16[224,128]{1,0:T(8,128)(2,1)S(1)} %get-tuple-element.78), channel_id=1, source_target_pairs={{256,384},{257,385},{258,386},{259,387},{260,388},{261,389},{262,3... | collective-permute-start | bytes 172040 | tf_op jit(solution)/shard_map/ppermute | solution.py:486
  26.0 12.5 %collective-permute-start.12 = (bf16[224,128]{1,0:T(8,128)(2,1)S(1)}, bf16[224,128]{1,0:T(8,128)(2,1)S(1)}, u32[]{:S(2)}, u32[]{:S(2)}) collective-permute-start(bf16[224,128]{1,0:T(8,128)(2,1)S(1)} %get-tuple-element.79), channel_id=1, source_target_pairs={{256,384},{257,385},{258,386},{259,387},{260,388},{261,389},{262,3... | collective-permute-start | bytes 172040 | tf_op jit(solution)/shard_map/ppermute | solution.py:486
  27.4 13.1 %collective-permute-start.10 = (bf16[224,128]{1,0:T(8,128)(2,1)S(1)}, bf16[224,128]{1,0:T(8,128)(2,1)S(1)}, u32[]{:S(2)}, u32[]{:S(2)}) collective-permute-start(bf16[224,128]{1,0:T(8,128)(2,1)S(1)} %get-tuple-element.77), channel_id=1, source_target_pairs={{256,384},{257,385},{258,386},{259,387},{260,388},{261,389},{262,3... | collective-permute-start | bytes 172040 | tf_op jit(solution)/shard_map/ppermute | solution.py:486
